TPU v7x, 128 devices: a whole 4x4x4 slice. The times are simulated.
128 devices in a mesh: chan: 32 (over z, x_lo, y), win: 4 (over x_hi, core).
Axes of the slice: x: 4 (x_hi: 2, x_lo: 2; x = x_hi * 2 + x_lo), y: 4, z: 4, core: 2. Of those that a mesh axis runs over, the one named last changes fastest.
Arguments:
- samples: int32 [6144, 8, 6144], P('chan', 'win'), may hold values from -2048 to 2046
- exponents: int32 [6144, 8, 24], P('chan', 'win'), may hold values from 0 to 4
- alive: int32 [6144], P('chan'), may hold values 0 or 1
- offsets: int32 [128], P('chan'), may hold values from 0 to 191
Outputs:
- stacks: float32 [128, 384, 2048], P('chan', 'win')
All inputs are finite; a program needn't handle non-finite values. No bound on the sum of `alive` on one device may be relied on, other than what follows from the above.
Results may differ from a plain program's by a relative error of at most 0.0032.
Values may be sent and summed in bfloat16 or wider, within the bound.
No kernel may reach another device: no remote copies, remote signals or barrier semaphores. Data moves between devices by JAX's collectives and lax.ppermute only.
A program may use at most 256 MiB of HBM per device.

v0:
```python
import functools
import math

import jax
import jax.numpy as jnp
import numpy as np
from jax import lax
from jax.experimental import pallas as pl
from jax.experimental.pallas import tpu as pltpu
from jax.sharding import PartitionSpec as P


SEG = 1024
HALF = 96
LANES = 128
GROUPS = SEG // LANES
PAIR = 2 * LANES
CHUNKS = ((0, 4), (4, 4))
FOLD = 32
UNROLL = 4
TILE = 32
SUB = 16
PITCH = 104
SOURCES = 4
SLOT = 16
SEGMENTS = 12
COLS = 256


def small_tables():
    k = GROUPS * np.arange(LANES)[None, :] + np.arange(GROUPS)[:, None]
    step = np.arange(FOLD)

    def waves(stride):
        phase = (stride * step[None, :, None] * k[:, None, :]) % (2 * SEG)
        angle = phase * (2.0 * math.pi / (2 * SEG))
        return np.stack([np.cos(angle), np.sin(angle)], axis=1).astype(np.float32)

    return waves(FOLD), waves(1)


def table_kernel(coarse_ref, fine_ref, out_ref, *, rest):
    fine_cos = fine_ref[0, 0]
    fine_sin = fine_ref[0, 1]

    def row_block(step, carry):
        for inner in range(UNROLL):
            a = step * UNROLL + inner
            base_cos = coarse_ref[0, 0, pl.ds(a, 8, stride=0), :]
            base_sin = coarse_ref[0, 1, pl.ds(a, 8, stride=0), :]
            base_cos = jnp.concatenate([base_cos] * (FOLD // 8), axis=0)
            base_sin = jnp.concatenate([base_sin] * (FOLD // 8), axis=0)
            real = base_cos * fine_cos - base_sin * fine_sin
            imag = -(base_sin * fine_cos + base_cos * fine_sin)
            rows = pl.ds(pl.multiple_of(a * FOLD, FOLD), FOLD)
            for part, lane in ((real, 0), (imag, LANES)):
                top = part.astype(jnp.bfloat16)
                if rest:
                    top = (part - top.astype(jnp.float32)).astype(jnp.bfloat16)
                out_ref[0, rows, lane:lane + LANES] = top
        return carry

    lax.fori_loop(0, FOLD // UNROLL, row_block, 0)


def make_tables(first, count, coarse, fine, rest=False):
    shape = jax.ShapeDtypeStruct((count, SEG, PAIR), jnp.bfloat16)
    small = pl.BlockSpec((1, 2, FOLD, LANES), lambda p: (first + p, 0, 0, 0))
    large = pl.BlockSpec((1, SEG, PAIR), lambda p: (p, 0, 0))
    return pl.pallas_call(
        functools.partial(table_kernel, rest=rest),
        grid=(count,),
        in_specs=[small, small],
        out_specs=large,
        out_shape=shape,
        name="tables",
    )(coarse, fine)


def normalize_kernel(half_ref, samples_ref, scale_ref, out_ref, buffer_ref, spread_ref, wide_ref, sems, *,
                     seg_count, windows):
    step = pl.program_id(0)
    steps = pl.num_programs(0)
    per_channel = samples_ref.shape[1]
    pieces = SEG // LANES
    pairs = pieces // 2
    blocks = seg_count * pairs
    slot = step % 2

    def copy(at, into):
        first = half_ref[0] * HALF + at * TILE
        return pltpu.make_async_copy(
            samples_ref.at[pl.ds(first, TILE)],
            buffer_ref.at[into, :, pl.ds(0, per_channel), :],
            sems.at[into],
        )

    @pl.when(step == 0)
    def _():
        copy(0, 0).start()

    @pl.when(step + 1 < steps)
    def _():
        copy(step + 1, 1 - slot).start()

    columns = wide_ref.shape[0]

    @pl.when(step == 0)
    def _():
        for column in range(columns):
            row = lax.broadcasted_iota(jnp.int32, (columns, LANES), 0)
            spread_ref[:, column * LANES:(column + 1) * LANES] = jnp.where(row == column, 1.0, 0.0).astype(jnp.bfloat16)

    scale = scale_ref[...]
    narrow = scale[:, :columns].astype(jnp.bfloat16)
    for column in range(0, columns, 2):
        both = jnp.dot(
            narrow, spread_ref[:, column * LANES:(column + 2) * LANES], preferred_element_type=jnp.float32
        )
        wide_ref[column] = both[:, :LANES]
        wide_ref[column + 1] = both[:, LANES:]

    copy(step, slot).wait()
    flat = buffer_ref.reshape(2 * TILE * PITCH, LANES)
    base = slot * (TILE * PITCH)

    def rows(w, n, piece):
        start = base + (n * pieces + piece) * windows + w
        return flat[pl.ds(start, TILE, stride=PITCH), :].astype(jnp.float32)

    live = scale[:, windows * blocks:windows * blocks + 1]
    for w in range(windows):
        total = jnp.zeros((TILE, LANES), jnp.float32)
        for n in range(seg_count):
            for pair in range(pairs):
                column = w * blocks + n * pairs + pair
                one = rows(w, n, 2 * pair)
                two = rows(w, n, 2 * pair + 1)
                weight = wide_ref[column]
                total = total + (one * one + two * two) * (weight * weight)
        energy = jnp.sum(total, axis=1, keepdims=True) * (1.0 / (seg_count * SEG))
        factor = jnp.broadcast_to(live * lax.rsqrt(energy + 1e-06), (TILE, LANES))
        for n in range(seg_count):
            for pair in range(pairs):
                column = w * blocks + n * pairs + pair
                weight = wide_ref[column] * factor
                for piece in (2 * pair, 2 * pair + 1):
                    value = rows(w, n, piece) * weight
                    out_ref[w * seg_count + n, :, piece * LANES:(piece + 1) * LANES] = value.astype(jnp.bfloat16)


def normalize_half(half, samples_rows, scales, seg_count, windows):
    steps = HALF // TILE
    return pl.pallas_call(
        functools.partial(normalize_kernel, seg_count=seg_count, windows=windows),
        grid_spec=pltpu.PrefetchScalarGridSpec(
            num_scalar_prefetch=1,
            grid=(steps,),
            in_specs=[
                pl.BlockSpec(memory_space=pl.ANY),
                pl.BlockSpec((TILE, scales.shape[1]), lambda i, h: (h[0] * steps + i, 0)),
            ],
            out_specs=pl.BlockSpec((windows * seg_count, TILE, SEG), lambda i, h: (0, i, 0)),
            scratch_shapes=[
                pltpu.VMEM((2, TILE, PITCH, LANES), jnp.int32),
                pltpu.VMEM((scales.shape[1] - 1, (scales.shape[1] - 1) * LANES), jnp.bfloat16),
                pltpu.VMEM((scales.shape[1] - 1, TILE, LANES), jnp.float32),
                pltpu.SemaphoreType.DMA((2,)),
            ],
        ),
        out_shape=jax.ShapeDtypeStruct((windows * seg_count, HALF, SEG), jnp.bfloat16),
        name="normalize",
    )(half, samples_rows, scales)


def source_kernel(offsets_ref, samples_ref, scale_ref, out_ref, sorted_ref, buffer_ref, rows_ref, sems, *,
                  seg_count, windows):
    pieces = SEG // LANES
    pairs = pieces // 2
    blocks = seg_count * pairs
    per_channel = samples_ref.shape[1]
    given = [offsets_ref[j] for j in range(SOURCES)]
    ranks = []
    for j in range(SOURCES):
        rank = jnp.int32(0)
        for i in range(SOURCES):
            if i != j:
                ahead = given[i] <= given[j] if i < j else given[i] < given[j]
                rank = rank + jnp.where(ahead, 1, 0)
        ranks.append(rank)
    order = []
    for r in range(SOURCES):
        offset = jnp.int32(0)
        origin = jnp.int32(0)
        for j in range(SOURCES):
            hit = ranks[j] == r
            offset = jnp.where(hit, given[j], offset)
            origin = jnp.where(hit, j, origin)
        sorted_ref[r] = offset
        sorted_ref[SOURCES + r] = origin
        order.append(offset)
    copies = []
    for r in range(SOURCES):
        copy = pltpu.make_async_copy(
            samples_ref.at[order[r]], buffer_ref.at[r, pl.ds(0, per_channel), :], sems.at[r]
        )
        copy.start()
        copies.append(copy)
    channel = lax.broadcasted_iota(jnp.int32, scale_ref.shape, 0)
    lane = lax.broadcasted_iota(jnp.int32, (8, scale_ref.shape[1]), 1)
    segment = lax.broadcasted_iota(jnp.int32, (8, scale_ref.shape[1]), 0)
    valid = lax.broadcasted_iota(jnp.int32, (8, LANES), 0) < seg_count
    rows_ref[...] = jnp.zeros(rows_ref.shape, jnp.float32)
    for r in range(SOURCES):
        picked = jnp.sum(jnp.where(channel == order[r], scale_ref[...], 0.0), axis=0, keepdims=True)
        picked = jnp.broadcast_to(picked, (8, scale_ref.shape[1]))
        live = jnp.sum(jnp.where(lane == windows * blocks, picked, 0.0), axis=1, keepdims=True)
        copies[r].wait()
        for w in range(windows):
            parts = []
            total = jnp.zeros((8, LANES), jnp.float32)
            for pair in range(pairs):
                column = w * blocks + segment * pairs + pair
                weight = jnp.sum(jnp.where(lane == column, picked, 0.0), axis=1, keepdims=True)
                for piece in (2 * pair, 2 * pair + 1):
                    raw = buffer_ref[r, pl.ds(piece * windows + w, 8, stride=pieces * windows), :]
                    part = jnp.where(valid, raw.astype(jnp.float32), 0.0) * weight
                    total = total + part * part
                    parts.append(part)
            energy = jnp.sum(jnp.sum(total, axis=1, keepdims=True), axis=0, keepdims=True)
            factor = live * lax.rsqrt(energy * (1.0 / (seg_count * SEG)) + 1e-06)
            for piece in range(pieces):
                rows_ref[r, pl.ds(w * seg_count, seg_count), piece * LANES:(piece + 1) * LANES] = (
                    parts[piece] * factor
                )[:seg_count]
        rows_ref[r, pl.ds(windows * seg_count, 1), :] = jnp.full((1, SEG), 1, jnp.float32) * (
            order[r] + 1
        ).astype(jnp.float32)
        out_ref[r] = rows_ref[r].astype(jnp.bfloat16)


def source_rows(offsets, samples_rows, scales, seg_count, windows):
    return pl.pallas_call(
        functools.partial(source_kernel, seg_count=seg_count, windows=windows),
        grid_spec=pltpu.PrefetchScalarGridSpec(
            num_scalar_prefetch=1,
            grid=(1,),
            in_specs=[
                pl.BlockSpec(memory_space=pl.ANY),
                pl.BlockSpec(scales.shape, lambda i, h: (0, 0)),
            ],
            out_specs=[
                pl.BlockSpec((SOURCES, SLOT, SEG), lambda i, h: (0, 0, 0)),
                pl.BlockSpec(memory_space=pltpu.SMEM),
            ],
            scratch_shapes=[
                pltpu.VMEM((SOURCES, 128, LANES), jnp.int32),
                pltpu.VMEM((SOURCES, SLOT, SEG), jnp.float32),
                pltpu.SemaphoreType.DMA((SOURCES,)),
            ],
        ),
        out_shape=[
            jax.ShapeDtypeStruct((SOURCES, SLOT, SEG), jnp.bfloat16),
            jax.ShapeDtypeStruct((2 * SOURCES,), jnp.int32),
        ],
        name="sources",
    )(offsets, samples_rows, scales)


def products(band_ref, sources, base, members, out_ref, g, row):
    src_ref, plus_ref, minus_ref = sources
    count = SEGMENTS
    lane = pl.multiple_of(g * PAIR, PAIR)
    real_lanes = pl.ds(lane, LANES)
    imag_lanes = pl.ds(pl.multiple_of(lane + LANES, LANES), LANES)
    zero = jnp.zeros((8, LANES), jnp.float32)
    acc = {(t, j): [zero, zero, zero] for t in range(SUB // 8) for j in members}
    for q in range(2 * count):
        band = []
        for t in range(SUB // 8):
            at = pl.ds(q * TILE + row + 8 * t, 8)
            g_re = band_ref[2 * g, at, :]
            g_im = band_ref[2 * g + 1, at, :]
            band.append((g_re, g_im, g_re + g_im))
        spot = q if q < count else SLOT + q - count
        for j in members:
            at = pl.ds(base + j * 2 * SLOT + spot, 8, stride=0)
            s_re = src_ref[g, at, :]
            s_plus = plus_ref[g, at, :]
            s_minus = minus_ref[g, at, :]
            for t in range(SUB // 8):
                g_re, g_im, g_sum = band[t]
                a = acc[t, j]
                a[0] = a[0] + s_re * g_sum
                a[1] = a[1] + s_minus * g_im
                a[2] = a[2] + s_plus * g_re
    for j in members:
        real = jnp.concatenate([acc[t, j][0] + acc[t, j][1] for t in range(SUB // 8)], axis=0)
        imag = jnp.concatenate([acc[t, j][0] - acc[t, j][2] for t in range(SUB // 8)], axis=0)
        out_ref[j, pl.ds(row, SUB), real_lanes] = real.astype(out_ref.dtype)
        out_ref[j, pl.ds(row, SUB), imag_lanes] = imag.astype(out_ref.dtype)


def outer_kernel(limits_ref, near_ref, far_ref, own_src_ref, above_src_ref, below_src_ref, table_ref,
                 up_ref, down_ref, band_ref, own_re_ref, own_plus_ref, own_minus_ref, src_ref, plus_ref, minus_ref):
    step = pl.program_id(0)
    count = near_ref.shape[0]
    groups = table_ref.shape[0]
    src_rows = 2 * SLOT
    per_side = SOURCES * src_rows

    @pl.when(step == 0)
    def _():
        scratch = (src_ref, plus_ref, minus_ref)
        for ref, base, into in (
            (own_src_ref, 0, (own_re_ref, own_plus_ref, own_minus_ref)),
            (above_src_ref, 0, scratch),
            (below_src_ref, per_side, scratch),
        ):
            rows = ref[...].reshape(per_side, SEG)
            at = pl.ds(base, per_side)
            for g in range(groups):
                spec = jnp.dot(rows, table_ref[g], preferred_element_type=jnp.float32)
                spec = spec.astype(jnp.bfloat16).astype(jnp.float32)
                real = spec[:, :LANES]
                imag = spec[:, LANES:]
                into[0][g, at, :] = real
                into[1][g, at, :] = real + imag
                into[2][g, at, :] = imag - real

    for part, ref in ((0, near_ref), (1, far_ref)):
        rows = ref[...].reshape(count * TILE, SEG)
        at = pl.ds(part * count * TILE, count * TILE)
        for g in range(groups):
            spec = jnp.dot(rows, table_ref[g], preferred_element_type=jnp.float32)
            spec = spec.astype(jnp.bfloat16).astype(jnp.float32)
            band_ref[2 * g, at, :] = spec[:, :LANES]
            band_ref[2 * g + 1, at, :] = spec[:, LANES:]

    def tile(index, carry):
        g = index // (TILE // SUB)
        row = pl.multiple_of((index % (TILE // SUB)) * SUB, SUB)
        channel = limits_ref[0] + step * TILE + row
        sources = (src_ref, plus_ref, minus_ref)
        for first in (0, 2):
            pair = (first, first + 1)

            @pl.when(channel + SUB > limits_ref[1 + first])
            def _():
                products(band_ref, sources, 0, pair, up_ref, g, row)

            @pl.when(channel < limits_ref[1 + SOURCES + first + 1])
            def _():
                products(band_ref, sources, per_side, pair, down_ref, g, row)

        return carry

    lax.fori_loop(0, groups * (TILE // SUB), tile, 0)


def own_kernel(band_ref, src_ref, plus_ref, minus_ref, out_ref):
    groups = src_ref.shape[0]

    def tile(index, carry):
        g = index // (TILE // SUB)
        row = pl.multiple_of((index % (TILE // SUB)) * SUB, SUB)
        for first in (0, 2):
            products(band_ref, (src_ref, plus_ref, minus_ref), 0, (first, first + 1), out_ref, g, row)
        return carry

    lax.fori_loop(0, groups * (TILE // SUB), tile, 0)


def outer_chunk(limits, near, far, own_src, above_src, below_src, table):
    count = near.shape[0]
    groups = table.shape[0]
    width = groups * PAIR
    per_side = SOURCES * 2 * SLOT
    steps = HALF // TILE
    band_rows = 2 * count * TILE
    block = pl.BlockSpec((count, TILE, SEG), lambda i, h: (0, i, 0))
    src = pl.BlockSpec((SOURCES, 2 * SLOT, SEG), lambda i, h: (0, 0, 0))
    result = pl.BlockSpec((SOURCES, TILE, width), lambda i, h: (0, i, 0))
    spectra = pl.BlockSpec((groups, per_side, LANES), lambda i, h: (0, 0, 0))
    returned = jax.ShapeDtypeStruct((SOURCES, HALF, width), jnp.bfloat16)
    own = jax.ShapeDtypeStruct((groups, per_side, LANES), jnp.float32)
    return pl.pallas_call(
        outer_kernel,
        grid_spec=pltpu.PrefetchScalarGridSpec(
            num_scalar_prefetch=1,
            grid=(steps,),
            in_specs=[block, block, src, src, src, pl.BlockSpec((groups, SEG, PAIR), lambda i, h: (0, 0, 0))],
            out_specs=[
                result,
                result,
                pl.BlockSpec((2 * groups, band_rows, LANES), lambda i, h: (0, i, 0)),
                spectra,
                spectra,
                spectra,
            ],
            scratch_shapes=[pltpu.VMEM((groups, 2 * per_side, LANES), jnp.float32)] * 3,
        ),
        out_shape=[
            returned,
            returned,
            jax.ShapeDtypeStruct((2 * groups, steps * band_rows, LANES), jnp.float32),
            own,
            own,
            own,
        ],
        name="outer",
    )(limits, near, far, own_src, above_src, below_src, table)


def own_chunk(band, src, plus, minus):
    groups, per_side, _ = src.shape
    steps = HALF // TILE
    width = groups * PAIR
    spectra = pl.BlockSpec((groups, per_side, LANES), lambda i: (0, 0, 0))
    return pl.pallas_call(
        own_kernel,
        grid=(steps,),
        in_specs=[pl.BlockSpec((2 * groups, band.shape[1] // steps, LANES), lambda i: (0, i, 0)), spectra, spectra, spectra],
        out_specs=pl.BlockSpec((SOURCES, TILE, width), lambda i: (0, i, 0)),
        out_shape=jax.ShapeDtypeStruct((SOURCES, HALF, width), jnp.float32),
        name="own",
    )(band, src, plus, minus)


def select_rows(below_source, keep, own, from_below, from_above):
    other = jnp.where(below_source, from_above, from_below)
    kept = jnp.where(keep, own, other.astype(jnp.float32))
    return kept, jnp.where(keep, other, own.astype(jnp.bfloat16))


def turned(ordered_ref, mine_ref, mate_ref, top_ref, halve):
    source_row = lax.broadcasted_iota(jnp.int32, (HALF, 2 * HALF), 1)
    target_row = lax.broadcasted_iota(jnp.int32, (HALF, 2 * HALF), 0)
    for j in range(SOURCES):
        wanted = target_row + ordered_ref[j]
        wanted = jnp.where(wanted >= 2 * HALF, wanted - 2 * HALF, wanted)
        turn = jnp.where(source_row == wanted, 1.0, 0.0).astype(jnp.bfloat16)
        rows = jnp.concatenate([mine_ref[j], mate_ref[j]], axis=0)
        top_ref[pl.ds(j * HALF, HALF), :] = jnp.dot(turn, rows, preferred_element_type=jnp.float32).astype(
            jnp.bfloat16
        )
    if halve:
        lane = lax.broadcasted_iota(jnp.int32, (SOURCES * HALF, LANES), 1)
        first = top_ref[:, :LANES].astype(jnp.float32)
        top_ref[:, :LANES] = jnp.where(lane == 0, 0.5 * first, first).astype(jnp.bfloat16)


def folded(top_ref, hi_ref, lo_ref, first, sums):
    for g in range(hi_ref.shape[0]):
        rows = top_ref[:, g * PAIR:(g + 1) * PAIR]
        for table in (hi_ref[g], lo_ref[g]):
            part = lax.dot_general(rows, table, (((1,), (1,)), ((), ())), preferred_element_type=jnp.float32)
            parity = (first + g) % 2
            sums[parity] = part if sums[parity] is None else sums[parity] + part


def early_kernel(ordered_ref, *refs, firsts):
    count = len(firsts)
    even_ref, odd_ref = refs[4 * count:4 * count + 2]
    tops = refs[4 * count + 2:]

    @pl.when(pl.program_id(0) == 0)
    def _():
        for c, first in enumerate(firsts):
            turned(ordered_ref, refs[4 * c], refs[4 * c + 1], tops[c], first == 0)

    sums = [None, None]
    for c, first in enumerate(firsts):
        folded(tops[c], refs[4 * c + 2], refs[4 * c + 3], first, sums)
    even_ref[...] = sums[0]
    odd_ref[...] = sums[1]


def chunk_specs(groups, first):
    assert first % groups == 0
    rows = pl.BlockSpec((SOURCES, HALF, groups * PAIR), lambda m, h: (0, 0, 0))
    table = pl.BlockSpec((groups, COLS, PAIR), lambda m, h: (0, m, 0))
    rest = pl.BlockSpec((groups, COLS, PAIR), lambda m, h: (first // groups, m, 0))
    return [rows, rows, table, rest]


def early_inverse(ordered, parts, firsts):
    specs, operands, tops = [], [], []
    for part, first in zip(parts, firsts):
        groups = part[2].shape[0]
        specs += chunk_specs(groups, first)
        operands += list(part)
        tops.append(pltpu.VMEM((SOURCES * HALF, groups * PAIR), jnp.bfloat16))
    block = pl.BlockSpec((SOURCES * HALF, COLS), lambda m, h: (0, m))
    shape = jax.ShapeDtypeStruct((SOURCES * HALF, SEG), jnp.float32)
    return pl.pallas_call(
        functools.partial(early_kernel, firsts=firsts),
        grid_spec=pltpu.PrefetchScalarGridSpec(
            num_scalar_prefetch=1,
            grid=(SEG // COLS,),
            in_specs=specs,
            out_specs=[block, block],
            scratch_shapes=tops,
        ),
        out_shape=[shape, shape],
        name="early",
    )(ordered, *operands)


def last_kernel(ordered_ref, mine_ref, mate_ref, hi_ref, lo_ref, even_ref, odd_ref, out_ref, top_ref, stage_ref, sem,
                *, first, scale):
    m = pl.program_id(0)

    @pl.when(m == 0)
    def _():
        turned(ordered_ref, mine_ref, mate_ref, top_ref, first == 0)

    sums = [even_ref[...], odd_ref[...]]
    folded(top_ref, hi_ref, lo_ref, first, sums)
    stage_ref[m, 0] = (sums[0] - sums[1]) * scale
    stage_ref[m, 1] = (sums[0] + sums[1]) * scale

    def copy(step, side, j):
        lane = pl.multiple_of(side * SEG + step * COLS, COLS)
        return pltpu.make_async_copy(
            stage_ref.at[step, side, pl.ds(j * HALF, HALF), :],
            out_ref.at[ordered_ref[SOURCES + j], :, pl.ds(lane, COLS)],
            sem.at[step, side, j],
        )

    for side in range(2):
        for j in range(SOURCES):
            copy(m, side, j).start()

    @pl.when(m == pl.num_programs(0) - 1)
    def _():
        for step in range(SEG // COLS):
            for side in range(2):
                for j in range(SOURCES):
                    copy(step, side, j).wait()


def last_inverse(ordered, part, even, odd, first, scale):
    groups = part[2].shape[0]
    block = pl.BlockSpec((SOURCES * HALF, COLS), lambda m, h: (0, m))
    return pl.pallas_call(
        functools.partial(last_kernel, first=first, scale=scale),
        grid_spec=pltpu.PrefetchScalarGridSpec(
            num_scalar_prefetch=1,
            grid=(SEG // COLS,),
            in_specs=chunk_specs(groups, first) + [block, block],
            out_specs=pl.BlockSpec(memory_space=pl.ANY),
            scratch_shapes=[
                pltpu.VMEM((SOURCES * HALF, groups * PAIR), jnp.bfloat16),
                pltpu.VMEM((SEG // COLS, 2, SOURCES * HALF, COLS), jnp.float32),
                pltpu.SemaphoreType.DMA((SEG // COLS, 2, SOURCES)),
            ],
        ),
        out_shape=jax.ShapeDtypeStruct((SOURCES, HALF, 2 * SEG), jnp.float32),
        name="last",
    )(ordered, *part, even, odd)


def block_scale(exponents):
    levels = jnp.arange(5, dtype=jnp.int32)
    powers = jnp.exp2(levels.astype(jnp.float32))
    return jnp.sum(jnp.where(exponents[..., None] == levels, powers, 0.0), axis=-1)


def passed_along(block, axis, distance):
    devices = range(lax.axis_size(axis))
    route = [(i - distance, i) for i in devices if i - distance in devices]
    return lax.ppermute(block, axis, route)


def partner(block, bit):
    return lax.ppermute(block, "win", [(i, i ^ bit) for i in range(lax.axis_size("win"))])


def pipeline(samples, exponents, alive, offsets):
    channels, windows, length = samples.shape
    seg_count = length // SEG
    place = lax.axis_index("win")
    core = place & 1
    upper_half = place >> 1

    samples_rows = samples.reshape(channels, windows, length // LANES, LANES)
    samples_rows = samples_rows.transpose(0, 2, 1, 3).reshape(channels, windows * (length // LANES), LANES)
    scales = block_scale(exponents).reshape(channels, -1)
    scales = jnp.concatenate([scales, alive.astype(jnp.float32).reshape(channels, 1)], axis=1)

    own_src, ordered = source_rows(offsets, samples_rows, scales, seg_count, windows)
    mate_src = partner(own_src, 1)
    own_src = jnp.concatenate([own_src, mate_src], axis=1)
    above_src = passed_along(own_src, "chan", -1)
    below_src = passed_along(own_src, "chan", 1)

    sent = normalize_half((1 - core).reshape(1), samples_rows, scales, seg_count, windows)
    far = partner(sent, 1)
    near = normalize_half(core.reshape(1), samples_rows, scales, seg_count, windows)
    coarse, fine = (jnp.asarray(t) for t in small_tables())

    flag = windows * seg_count
    above_off = above_src[:, flag, 0].astype(jnp.int32)
    below_off = below_src[:, flag, 0].astype(jnp.int32)
    limits = jnp.concatenate(
        [(core * HALF).reshape(1), jnp.where(above_off == 0, channels, above_off - 1), below_off - 1]
    ).astype(jnp.int32)
    index = core * HALF + jnp.arange(HALF, dtype=jnp.int32)
    below_source = (index[None, :] < ordered[:SOURCES, None])[:, :, None]
    keep = below_source == (upper_half == 0)
    scale = 2.0 / float(2 * SEG * windows * lax.axis_size("win") * seg_count * SEG)

    tables = []
    for first, count in CHUNKS:
        tables.append(make_tables(first, count, coarse, fine))
    crossed, returned, selected = [], [], []

    def select(c):
        pieces = (crossed[c],) + returned[c]
        if c:
            pieces = lax.optimization_barrier(pieces + (selected[c - 1][2],))[:3]
        kept, moved = select_rows(below_source, keep, *pieces)
        selected.append((kept, partner(moved, 2), moved))

    kept_spectra = []
    for c in range(len(CHUNKS)):
        to_above, to_below, *spectra = outer_chunk(limits, near, far, own_src, above_src, below_src, tables[c])
        kept_spectra.append(spectra)
        from_below = passed_along(to_above, "chan", 1)
        from_above = passed_along(to_below, "chan", -1)
        returned.append((from_below, from_above))
    for c in range(len(CHUNKS)):
        crossed.append(own_chunk(*kept_spectra[c]))
        select(c)
    rest = make_tables(0, GROUPS, coarse, lax.optimization_barrier((fine, selected[0][2]))[0], True)
    parts = []
    for c in range(len(CHUNKS)):
        kept, moved, _ = selected[c]
        if c:
            kept = lax.optimization_barrier((kept, parts[c - 1][0]))[0]
        total = (kept + moved.astype(jnp.float32)).astype(jnp.bfloat16)
        mate = partner(total, 1)
        parts.append((total, mate, tables[c], rest))
    firsts = tuple(first for first, _ in CHUNKS)
    even, odd = early_inverse(ordered, parts[:-1], firsts[:-1])
    return last_inverse(ordered, parts[-1], even, odd, firsts[-1], scale)


def solution(mesh):
    placed = (P("chan", "win", None), P("chan", "win", None), P("chan"), P("chan"))
    return jax.shard_map(pipeline, mesh=mesh, in_specs=placed, out_specs=P("chan", "win", None), check_vma=False)
```

profile of v0, /device:TPU:65, one launch (start us, length us, event | category | flops | bytes accessed | tf_op | source)
XLA Modules:
  0.0 171.5 jit_solution(6109941174431502505)
XLA Ops:
  0.0 0.9 select_reduce_fusion
  2.6 6.1 %normalize.3 = bf16[12,96,1024]{2,1,0:T(8,128)(2,1)} custom-call(s32[1]{0:T(128)} %bitcast.9.half_ref, s32[192,96,128]{2,1,0:T(8,128)} %bitcast.11, f32[192,49]{1,0:T(8,128)} %pad_maximum_fusion.scale_ref), custom_call_target="tpu_custom_call" | custom-call | tf_op jit(solution)/shard_map/normalize/pallas_call | solution.py:154
  8.7 0.8 collective-permute-start.3
  9.4 3.8 %sources.1 = (bf16[4,16,1024]{2,1,0:T(8,128)(2,1)}, s32[8]{0:T(128)}) custom-call(s32[4]{0:T(128)} %offsets_ref.1, s32[192,96,128]{2,1,0:T(8,128)} %bitcast.12, f32[192,49]{1,0:T(8,128)} %pad_maximum_fusion.scale_ref), custom_call_target="tpu_custom_call" | custom-call | tf_op jit(solution)/shard_map/sources/pallas_call | solution.py:243
  13.3 0.9 constant_dynamic-update-slice_fusion.1
  14.9 3.2 %collective-permute-start.2 = (bf16[4,32,1024]{2,1,0:T(8,128)(2,1)S(1)}, bf16[4,32,1024]{2,1,0:T(8,128)(2,1)S(1)}, u32[]{:S(2)}, u32[]{:S(2)}) collective-permute-start(bf16[4,32,1024]{2,1,0:T(8,128)(2,1)S(1)} %constant_dynamic-update-slice_fusion.own_src_ref), channel_id=1, source_target_pairs={{0,4},{4,8},{8,12},{12,16},{16,20},{20,24},{24,28},{28,32},{32,36}... | collective-permute-start | bytes 786440 | tf_op jit(solution)/shard_map/ppermute | solution.py:573
  18.1 5.1 %collective-permute-start.1 = (bf16[4,32,1024]{2,1,0:T(8,128)(2,1)S(1)}, bf16[4,32,1024]{2,1,0:T(8,128)(2,1)S(1)}, u32[]{:S(2)}, u32[]{:S(2)}) collective-permute-start(bf16[4,32,1024]{2,1,0:T(8,128)(2,1)S(1)} %constant_dynamic-update-slice_fusion.own_src_ref), channel_id=1, source_target_pairs={{4,0},{8,4},{12,8},{16,12},{20,16},{24,20},{28,24},{32,28},{36,32}... | collective-permute-start | bytes 786440 | tf_op jit(solution)/shard_map/ppermute | solution.py:573
  23.2 6.1 %normalize.2.near_ref = bf16[12,96,1024]{2,1,0:T(8,128)(2,1)} custom-call(s32[1]{0:T(128)} %bitcast.6.half_ref, s32[192,96,128]{2,1,0:T(8,128)} %bitcast.13, f32[192,49]{1,0:T(8,128)} %pad_maximum_fusion.scale_ref), custom_call_target="tpu_custom_call" | custom-call | tf_op jit(solution)/shard_map/normalize/pallas_call | solution.py:154
  29.3 3.6 %tables.4.table_ref.refs_2_ = bf16[4,1024,256]{2,1,0:T(8,128)(2,1)} custom-call(f32[8,2,32,128]{3,2,1,0:T(8,128)} %constant.25.clone.coarse_ref, f32[8,2,32,128]{3,2,1,0:T(8,128)} %constant.26.clone.fine_ref), custom_call_target="tpu_custom_call" | custom-call | tf_op jit(solution)/shard_map/tables/pallas_call | solution.py:70
  33.9 1.4 copy-done.2
  35.3 17.4 %outer.3 = (bf16[4,96,1024]{2,1,0:T(8,128)(2,1)}, bf16[4,96,1024]{2,1,0:T(8,128)(2,1)}, f32[8,2304,128]{2,1,0:T(8,128)}, f32[4,128,128]{2,1,0:T(8,128)}, f32[4,128,128]{2,1,0:T(8,128)}, /*index=5*/f32[4,128,128]{2,1,0:T(8,128)}) custom-call(s32[9]{0:T(128)} %pad_add_fusion.limits_ref, bf16[12,96,1024]{2,1,0:T(8,128)(2,1)} %normalize.2.near_ref, ...), custom_call_target="tpu_custom_call" | custom-call | tf_op jit(solution)/shard_map/outer/pallas_call | solution.py:387
  52.7 5.5 %collective-permute-start.6 = (bf16[4,96,1024]{2,1,0:T(8,128)(2,1)}, bf16[4,96,1024]{2,1,0:T(8,128)(2,1)S(1)}, u32[]{:S(2)}, u32[]{:S(2)}) collective-permute-start(bf16[4,96,1024]{2,1,0:T(8,128)(2,1)} %get-tuple-element.34), channel_id=1, source_target_pairs={{4,0},{8,4},{12,8},{16,12},{20,16},{24,20},{28,24},{32,28},{36,32}... | collective-permute-start | bytes 2359304 | tf_op jit(solution)/shard_map/ppermute | solution.py:573
  58.3 1.9 %collective-permute-start.7 = (bf16[4,96,1024]{2,1,0:T(8,128)(2,1)}, bf16[4,96,1024]{2,1,0:T(8,128)(2,1)S(1)}, u32[]{:S(2)}, u32[]{:S(2)}) collective-permute-start(bf16[4,96,1024]{2,1,0:T(8,128)(2,1)} %get-tuple-element.35), channel_id=1, source_target_pairs={{0,4},{4,8},{8,12},{12,16},{16,20},{20,24},{24,28},{28,32},{32,36}... | collective-permute-start | bytes 2359304 | tf_op jit(solution)/shard_map/ppermute | solution.py:573
  60.2 3.6 %tables.3.table_ref.hi_ref = bf16[4,1024,256]{2,1,0:T(8,128)(2,1)} custom-call(f32[8,2,32,128]{3,2,1,0:T(8,128)} %constant.25.clone.coarse_ref, f32[8,2,32,128]{3,2,1,0:T(8,128)} %constant.26.clone.fine_ref), custom_call_target="tpu_custom_call" | custom-call | tf_op jit(solution)/shard_map/tables/pallas_call | solution.py:70
  63.8 17.5 %outer.2 = (bf16[4,96,1024]{2,1,0:T(8,128)(2,1)}, bf16[4,96,1024]{2,1,0:T(8,128)(2,1)}, f32[8,2304,128]{2,1,0:T(8,128)}, f32[4,128,128]{2,1,0:T(8,128)}, f32[4,128,128]{2,1,0:T(8,128)}, /*index=5*/f32[4,128,128]{2,1,0:T(8,128)}) custom-call(s32[9]{0:T(128)} %pad_add_fusion.limits_ref, bf16[12,96,1024]{2,1,0:T(8,128)(2,1)} %normalize.2.near_ref, ...), custom_call_target="tpu_custom_call" | custom-call | tf_op jit(solution)/shard_map/outer/pallas_call | solution.py:387
  81.3 1.9 %collective-permute-start.4 = (bf16[4,96,1024]{2,1,0:T(8,128)(2,1)}, bf16[4,96,1024]{2,1,0:T(8,128)(2,1)S(1)}, u32[]{:S(2)}, u32[]{:S(2)}) collective-permute-start(bf16[4,96,1024]{2,1,0:T(8,128)(2,1)} %get-tuple-element.32), channel_id=1, source_target_pairs={{0,4},{4,8},{8,12},{12,16},{16,20},{20,24},{24,28},{28,32},{32,36}... | collective-permute-start | bytes 2359304 | tf_op jit(solution)/shard_map/ppermute | solution.py:573
  83.2 9.4 %collective-permute-start.5 = (bf16[4,96,1024]{2,1,0:T(8,128)(2,1)}, bf16[4,96,1024]{2,1,0:T(8,128)(2,1)S(1)}, u32[]{:S(2)}, u32[]{:S(2)}) collective-permute-start(bf16[4,96,1024]{2,1,0:T(8,128)(2,1)} %get-tuple-element.33), channel_id=1, source_target_pairs={{4,0},{8,4},{12,8},{16,12},{20,16},{24,20},{28,24},{32,28},{36,32}... | collective-permute-start | bytes 2359304 | tf_op jit(solution)/shard_map/ppermute | solution.py:573
  92.7 8.5 %own.3 = f32[4,96,1024]{2,1,0:T(8,128)} custom-call(f32[8,2304,128]{2,1,0:T(8,128)} %get-tuple-element.36.band_ref, f32[4,128,128]{2,1,0:T(8,128)} %get-tuple-element.37.src_ref, f32[4,128,128]{2,1,0:T(8,128)} %get-tuple-element.38.plus_ref, f32[4,128,128]{2,1,0:T(8,128)} %get-tuple-element.39.minus_ref), custom_call_target="tpu_custom_call" | custom-call | tf_op jit(solution)/shard_map/own/pallas_call | solution.py:420
  101.3 2.5 %convert_select_fusion.2 = bf16[4,96,1024]{2,1,0:T(8,128)(2,1)} fusion(f32[4,96,1024]{2,1,0:T(8,128)} %own.3, pred[4,96]{1,0:T(4,128)(4,1)S(1)} %get-tuple-element.47, bf16[4,96,1024]{2,1,0:T(8,128)(2,1)S(1)} %collective-permute-done.6, bf16[4,96,1024]{2,1,0:T(8,128)(2,1)S(1)} %collective-permute-done.7, pred[4,96]{1,0:T(4,128)(4,1)S(1)} %get-tuple-element.48), kind=kLoop, calls=%fused_computation.4 | loop fusion | flops 1179648 | bytes 3932928 | tf_op jit(solution)/shard_map/jit(_where)/select_n | solution.py:433
  103.8 2.7 %collective-permute-start.8 = (bf16[4,96,1024]{2,1,0:T(8,128)(2,1)}, bf16[4,96,1024]{2,1,0:T(8,128)(2,1)}, u32[]{:S(2)}, u32[]{:S(2)}) collective-permute-start(bf16[4,96,1024]{2,1,0:T(8,128)(2,1)} %convert_select_fusion.2), channel_id=1, source_target_pairs={{0,2},{1,3},{2,0},{3,1},{4,6},{5,7},{6,4},{7,5},{8,10},{9,11},{10,... | collective-permute-start | bytes 2359304 | tf_op jit(solution)/shard_map/ppermute | solution.py:577
  106.5 8.6 %own.2 = f32[4,96,1024]{2,1,0:T(8,128)} custom-call(f32[8,2304,128]{2,1,0:T(8,128)} %get-tuple-element.28.band_ref, f32[4,128,128]{2,1,0:T(8,128)} %get-tuple-element.29.src_ref, f32[4,128,128]{2,1,0:T(8,128)} %get-tuple-element.30.plus_ref, f32[4,128,128]{2,1,0:T(8,128)} %get-tuple-element.31.minus_ref), custom_call_target="tpu_custom_call" | custom-call | tf_op jit(solution)/shard_map/own/pallas_call | solution.py:420
  115.1 1.8 %convert_select_fusion.1 = bf16[4,96,1024]{2,1,0:T(8,128)(2,1)S(1)} fusion(f32[4,96,1024]{2,1,0:T(8,128)} %own.2, pred[4,96]{1,0:T(4,128)(4,1)S(1)} %get-tuple-element.47, bf16[4,96,1024]{2,1,0:T(8,128)(2,1)S(1)} %collective-permute-done.5, bf16[4,96,1024]{2,1,0:T(8,128)(2,1)S(1)} %collective-permute-done.4, pred[4,96]{1,0:T(4,128)(4,1)S(1)} %get-tuple-element.48), kind=kLoop, calls=%fused_computation.3 | loop fusion | flops 1179648 | bytes 3932928 | tf_op jit(solution)/shard_map/jit(_where)/select_n | solution.py:433
  117.2 10.2 %collective-permute-done.8 = bf16[4,96,1024]{2,1,0:T(8,128)(2,1)} collective-permute-done((bf16[4,96,1024]{2,1,0:T(8,128)(2,1)}, bf16[4,96,1024]{2,1,0:T(8,128)(2,1)}, u32[]{:S(2)}, u32[]{:S(2)}) %collective-permute-start.8) | collective-permute-done | bytes 786464 | tf_op jit(solution)/shard_map/ppermute | solution.py:577
  127.4 2.7 %add_convert_fusion.1 = (bf16[4,96,1024]{2,1,0:T(8,128)(2,1)}, f32[4,96,1024]{2,1,0:T(8,128)S(1)}) fusion(bf16[4,96,1024]{2,1,0:T(8,128)(2,1)} %collective-permute-done.8, f32[4,96,1024]{2,1,0:T(8,128)S(1)} %copy-done, pred[4,96]{1,0:T(4,128)(4,1)S(1)} %get-tuple-element.47, bf16[4,96,1024]{2,1,0:T(8,128)(2,1)S(1)} %collective-permute-done.6, ...), kind=kLoop, calls=%fused_computation.1 | loop fusion | flops 3538944 | bytes 9437952 | tf_op jit(solution)/shard_map/convert_element_type | solution.py:642
  130.1 6.8 %collective-permute-start.11 = (bf16[4,96,1024]{2,1,0:T(8,128)(2,1)}, bf16[4,96,1024]{2,1,0:T(8,128)(2,1)S(1)}, u32[]{:S(2)}, u32[]{:S(2)}) collective-permute-start(bf16[4,96,1024]{2,1,0:T(8,128)(2,1)} %get-tuple-element.49.refs_0_), channel_id=1, source_target_pairs={{0,1},{1,0},{2,3},{3,2},{4,5},{5,4},{6,7},{7,6},{8,9},{9,8},{10,11... | collective-permute-start | bytes 2359304 | tf_op jit(solution)/shard_map/ppermute | solution.py:577
  137.0 7.2 %collective-permute-done.9 = bf16[4,96,1024]{2,1,0:T(8,128)(2,1)S(1)} collective-permute-done((bf16[4,96,1024]{2,1,0:T(8,128)(2,1)S(1)}, bf16[4,96,1024]{2,1,0:T(8,128)(2,1)S(1)}, u32[]{:S(2)}, u32[]{:S(2)}) %collective-permute-start.9) | collective-permute-done | bytes 786464 | tf_op jit(solution)/shard_map/ppermute | solution.py:577
  144.4 3.7 %collective-permute-start.10 = (bf16[4,96,1024]{2,1,0:T(8,128)(2,1)S(1)}, bf16[4,96,1024]{2,1,0:T(8,128)(2,1)S(1)}, u32[]{:S(2)}, u32[]{:S(2)}) collective-permute-start(bf16[4,96,1024]{2,1,0:T(8,128)(2,1)S(1)} %add_convert_fusion.mine_ref), channel_id=1, source_target_pairs={{0,1},{1,0},{2,3},{3,2},{4,5},{5,4},{6,7},{7,6},{8,9},{9,8},{10,11... | collective-permute-start | bytes 2359304 | tf_op jit(solution)/shard_map/ppermute | solution.py:577
  148.1 6.1 %tables.5.refs_3_.lo_ref = bf16[8,1024,256]{2,1,0:T(8,128)(2,1)} custom-call(f32[8,2,32,128]{3,2,1,0:T(8,128)} %constant.25.clone.coarse_ref, f32[8,2,32,128]{3,2,1,0:T(8,128)} %constant.26.clone.fine_ref), custom_call_target="tpu_custom_call" | custom-call | tf_op jit(solution)/shard_map/tables/pallas_call | solution.py:70
  154.3 0.9 copy-done.8
  155.2 7.2 %early.1 = (f32[384,1024]{1,0:T(8,128)}, f32[384,1024]{1,0:T(8,128)}) custom-call(s32[8]{0:T(128)} %get-tuple-element.26.ordered_ref, bf16[4,96,1024]{2,1,0:T(8,128)(2,1)} %get-tuple-element.49.refs_0_, bf16[4,96,1024]{2,1,0:T(8,128)(2,1)} %copy-done.8, bf16[4,1024,256]{2,1,0:T(8,128)(2,1)} %tables.4.table_ref.refs_2_, ...), custom_call_target="tpu_custom_call" | custom-call | tf_op jit(solution)/shard_map/early/pallas_call | solution.py:496
  162.4 0.9 copy-done.7
  163.3 8.1 %last.1 = f32[4,96,2048]{2,1,0:T(8,128)} custom-call(s32[8]{0:T(128)} %get-tuple-element.26.ordered_ref, bf16[4,96,1024]{2,1,0:T(8,128)(2,1)} %copy-done.3, bf16[4,96,1024]{2,1,0:T(8,128)(2,1)} %copy-done.7, bf16[4,1024,256]{2,1,0:T(8,128)(2,1)} %tables.3.table_ref.hi_ref, bf16[8,1024,256]{2,1,0:T(8,128)(2,1)} %tables.5.refs_3_.lo_ref, ...), custom_call_target="tpu_custom_call" | custom-call | tf_op jit(solution)/shard_map/last/pallas_call | solution.py:546
  (41 shorter events, 4.1 us)
Async XLA Ops:
  8.7 25.3 %collective-permute-start.3 = (bf16[12,96,1024]{2,1,0:T(8,128)(2,1)}, bf16[12,96,1024]{2,1,0:T(8,128)(2,1)S(1)}, u32[]{:S(2)}, u32[]{:S(2)}) collective-permute-start(bf16[12,96,1024]{2,1,0:T(8,128)(2,1)} %normalize.3), channel_id=1, source_target_pairs={{0,1},{1,0},{2,3},{3,2},{4,5},{5,4},{6,7},{7,6},{8,9},{9,8},{10,11... | collective-permute-start | bytes 7077896 | tf_op jit(solution)/shard_map/ppermute | solution.py:577
  13.2 1.6 collective-permute-start
  14.9 14.4 %copy-start.4 = (bf16[4,32,1024]{2,1,0:T(8,128)(2,1)}, bf16[4,32,1024]{2,1,0:T(8,128)(2,1)S(1)}, u32[]{:S(2)}) copy-start(bf16[4,32,1024]{2,1,0:T(8,128)(2,1)S(1)} %constant_dynamic-update-slice_fusion.own_src_ref) | copy-start | bytes 786436
  14.9 18.0 %collective-permute-start.2 = (bf16[4,32,1024]{2,1,0:T(8,128)(2,1)S(1)}, bf16[4,32,1024]{2,1,0:T(8,128)(2,1)S(1)}, u32[]{:S(2)}, u32[]{:S(2)}) collective-permute-start(bf16[4,32,1024]{2,1,0:T(8,128)(2,1)S(1)} %constant_dynamic-update-slice_fusion.own_src_ref), channel_id=1, source_target_pairs={{0,4},{4,8},{8,12},{12,16},{16,20},{20,24},{24,28},{28,32},{32,36}... | collective-permute-start | bytes 786440 | tf_op jit(solution)/shard_map/ppermute | solution.py:573
  18.1 14.9 %collective-permute-start.1 = (bf16[4,32,1024]{2,1,0:T(8,128)(2,1)S(1)}, bf16[4,32,1024]{2,1,0:T(8,128)(2,1)S(1)}, u32[]{:S(2)}, u32[]{:S(2)}) collective-permute-start(bf16[4,32,1024]{2,1,0:T(8,128)(2,1)S(1)} %constant_dynamic-update-slice_fusion.own_src_ref), channel_id=1, source_target_pairs={{4,0},{8,4},{12,8},{16,12},{20,16},{24,20},{28,24},{32,28},{36,32}... | collective-permute-start | bytes 786440 | tf_op jit(solution)/shard_map/ppermute | solution.py:573
  32.9 1.0 copy-start.5
  33.1 0.9 copy-start.6
  33.9 1.4 copy-start.2
  52.7 48.6 %collective-permute-start.6 = (bf16[4,96,1024]{2,1,0:T(8,128)(2,1)}, bf16[4,96,1024]{2,1,0:T(8,128)(2,1)S(1)}, u32[]{:S(2)}, u32[]{:S(2)}) collective-permute-start(bf16[4,96,1024]{2,1,0:T(8,128)(2,1)} %get-tuple-element.34), channel_id=1, source_target_pairs={{4,0},{8,4},{12,8},{16,12},{20,16},{24,20},{28,24},{32,28},{36,32}... | collective-permute-start | bytes 2359304 | tf_op jit(solution)/shard_map/ppermute | solution.py:573
  58.3 43.0 %collective-permute-start.7 = (bf16[4,96,1024]{2,1,0:T(8,128)(2,1)}, bf16[4,96,1024]{2,1,0:T(8,128)(2,1)S(1)}, u32[]{:S(2)}, u32[]{:S(2)}) collective-permute-start(bf16[4,96,1024]{2,1,0:T(8,128)(2,1)} %get-tuple-element.35), channel_id=1, source_target_pairs={{0,4},{4,8},{8,12},{12,16},{16,20},{20,24},{24,28},{28,32},{32,36}... | collective-permute-start | bytes 2359304 | tf_op jit(solution)/shard_map/ppermute | solution.py:573
  63.8 28.8 %copy-start.9 = (s32[8]{0:T(128)S(1)}, s32[8]{0:T(128)}, u32[]{:S(2)}) copy-start(s32[8]{0:T(128)} %get-tuple-element.26.ordered_ref) | copy-start | bytes 100
  81.3 33.8 %collective-permute-start.4 = (bf16[4,96,1024]{2,1,0:T(8,128)(2,1)}, bf16[4,96,1024]{2,1,0:T(8,128)(2,1)S(1)}, u32[]{:S(2)}, u32[]{:S(2)}) collective-permute-start(bf16[4,96,1024]{2,1,0:T(8,128)(2,1)} %get-tuple-element.32), channel_id=1, source_target_pairs={{0,4},{4,8},{8,12},{12,16},{16,20},{20,24},{24,28},{28,32},{32,36}... | collective-permute-start | bytes 2359304 | tf_op jit(solution)/shard_map/ppermute | solution.py:573
  83.2 31.9 %collective-permute-start.5 = (bf16[4,96,1024]{2,1,0:T(8,128)(2,1)}, bf16[4,96,1024]{2,1,0:T(8,128)(2,1)S(1)}, u32[]{:S(2)}, u32[]{:S(2)}) collective-permute-start(bf16[4,96,1024]{2,1,0:T(8,128)(2,1)} %get-tuple-element.33), channel_id=1, source_target_pairs={{4,0},{8,4},{12,8},{16,12},{20,16},{24,20},{28,24},{32,28},{36,32}... | collective-permute-start | bytes 2359304 | tf_op jit(solution)/shard_map/ppermute | solution.py:573
  103.8 23.6 %collective-permute-start.8 = (bf16[4,96,1024]{2,1,0:T(8,128)(2,1)}, bf16[4,96,1024]{2,1,0:T(8,128)(2,1)}, u32[]{:S(2)}, u32[]{:S(2)}) collective-permute-start(bf16[4,96,1024]{2,1,0:T(8,128)(2,1)} %convert_select_fusion.2), channel_id=1, source_target_pairs={{0,2},{1,3},{2,0},{3,1},{4,6},{5,7},{6,4},{7,5},{8,10},{9,11},{10,... | collective-permute-start | bytes 2359304 | tf_op jit(solution)/shard_map/ppermute | solution.py:577
  115.1 12.3 %copy-start = (f32[4,96,1024]{2,1,0:T(8,128)S(1)}, f32[4,96,1024]{2,1,0:T(8,128)}, u32[]{:S(2)}) copy-start(f32[4,96,1024]{2,1,0:T(8,128)} %own.3) | copy-start | bytes 4718596
  115.1 12.3 %copy-start.1 = (f32[4,96,1024]{2,1,0:T(8,128)S(1)}, f32[4,96,1024]{2,1,0:T(8,128)}, u32[]{:S(2)}) copy-start(f32[4,96,1024]{2,1,0:T(8,128)} %own.2) | copy-start | bytes 4718596
  116.9 27.3 %collective-permute-start.9 = (bf16[4,96,1024]{2,1,0:T(8,128)(2,1)S(1)}, bf16[4,96,1024]{2,1,0:T(8,128)(2,1)S(1)}, u32[]{:S(2)}, u32[]{:S(2)}) collective-permute-start(bf16[4,96,1024]{2,1,0:T(8,128)(2,1)S(1)} %convert_select_fusion.1), channel_id=1, source_target_pairs={{0,2},{1,3},{2,0},{3,1},{4,6},{5,7},{6,4},{7,5},{8,10},{9,11},{10,... | collective-permute-start | bytes 2359304 | tf_op jit(solution)/shard_map/ppermute | solution.py:577
  130.1 24.1 %collective-permute-start.11 = (bf16[4,96,1024]{2,1,0:T(8,128)(2,1)}, bf16[4,96,1024]{2,1,0:T(8,128)(2,1)S(1)}, u32[]{:S(2)}, u32[]{:S(2)}) collective-permute-start(bf16[4,96,1024]{2,1,0:T(8,128)(2,1)} %get-tuple-element.49.refs_0_), channel_id=1, source_target_pairs={{0,1},{1,0},{2,3},{3,2},{4,5},{5,4},{6,7},{7,6},{8,9},{9,8},{10,11... | collective-permute-start | bytes 2359304 | tf_op jit(solution)/shard_map/ppermute | solution.py:577
  144.4 9.8 %copy-start.3 = (bf16[4,96,1024]{2,1,0:T(8,128)(2,1)}, bf16[4,96,1024]{2,1,0:T(8,128)(2,1)S(1)}, u32[]{:S(2)}) copy-start(bf16[4,96,1024]{2,1,0:T(8,128)(2,1)S(1)} %add_convert_fusion.mine_ref) | copy-start | bytes 2359300
  144.4 17.9 %collective-permute-start.10 = (bf16[4,96,1024]{2,1,0:T(8,128)(2,1)S(1)}, bf16[4,96,1024]{2,1,0:T(8,128)(2,1)S(1)}, u32[]{:S(2)}, u32[]{:S(2)}) collective-permute-start(bf16[4,96,1024]{2,1,0:T(8,128)(2,1)S(1)} %add_convert_fusion.mine_ref), channel_id=1, source_target_pairs={{0,1},{1,0},{2,3},{3,2},{4,5},{5,4},{6,7},{7,6},{8,9},{9,8},{10,11... | collective-permute-start | bytes 2359304 | tf_op jit(solution)/shard_map/ppermute | solution.py:577
  154.3 0.9 copy-start.8
  162.4 0.9 copy-start.7
where the time goes:
time: 174 us; the launch traced here: 172 us
  Pallas kernels  96.5 us (55%)
  starting transfers between devices  41.5 us (24%)
  waiting for transfers between devices  18 us (10%)
  other arithmetic  10.7 us (6%)
  local copies, waits for them, and re-layouts  4.4 us (3%)
    pallas_call x2, Pallas kernels, outer_chunk(): pl.pallas_call(outer_kernel, grid_spec=pltpu.PrefetchScalarGridSpec(num_s...  34.8 us
    ppermute x6, starting transfers between devices, passed_along(): return lax.ppermute(block, axis, route)  27.1 us
    ppermute x6, waiting for transfers between devices, partner(): lax.ppermute(block, 'win', [(i, i ^ bit) for i in range(lax.axis_size('wi...  18 us
    pallas_call x2, Pallas kernels, own_chunk(): pl.pallas_call(own_kernel, grid=(steps,), in_specs=[pl.BlockSpec((2 * gro...  17.1 us
    ppermute x6, starting transfers between devices, partner(): lax.ppermute(block, 'win', [(i, i ^ bit) for i in range(lax.axis_size('wi...  14.4 us
    pallas_call x3, Pallas kernels, make_tables(): pl.pallas_call(functools.partial(table_kernel, rest=rest), grid=(count,),...  13.4 us
    pallas_call x2, Pallas kernels, normalize_half(): pl.pallas_call(functools.partial(normalize_kernel, seg_count=seg_count, w...  12.1 us
    pallas_call x1, Pallas kernels, last_inverse(): pl.pallas_call(functools.partial(last_kernel, first=first, scale=scale),...  8.06 us
  transfers between devices with their start and end apart: 12, of which 3 were waited for; matrix products, arithmetic and copies ran while one was open for 5% of the time, Pallas kernels for 38%

commit v1 on v0

--- a/solution.py
+++ b/solution.py
@@ -39,7 +39,7 @@
     return waves(FOLD), waves(1)
 
 
-def table_kernel(coarse_ref, fine_ref, out_ref, *, rest):
+def table_kernel(coarse_ref, fine_ref, hi_ref, lo_ref):
     fine_cos = fine_ref[0, 0]
     fine_sin = fine_ref[0, 1]
 
@@ -55,24 +55,23 @@
             rows = pl.ds(pl.multiple_of(a * FOLD, FOLD), FOLD)
             for part, lane in ((real, 0), (imag, LANES)):
                 top = part.astype(jnp.bfloat16)
-                if rest:
-                    top = (part - top.astype(jnp.float32)).astype(jnp.bfloat16)
-                out_ref[0, rows, lane:lane + LANES] = top
+                hi_ref[0, rows, lane:lane + LANES] = top
+                lo_ref[0, rows, lane:lane + LANES] = (part - top.astype(jnp.float32)).astype(jnp.bfloat16)
         return carry
 
     lax.fori_loop(0, FOLD // UNROLL, row_block, 0)
 
 
-def make_tables(first, count, coarse, fine, rest=False):
+def make_tables(first, count, coarse, fine):
     shape = jax.ShapeDtypeStruct((count, SEG, PAIR), jnp.bfloat16)
     small = pl.BlockSpec((1, 2, FOLD, LANES), lambda p: (first + p, 0, 0, 0))
     large = pl.BlockSpec((1, SEG, PAIR), lambda p: (p, 0, 0))
     return pl.pallas_call(
-        functools.partial(table_kernel, rest=rest),
+        table_kernel,
         grid=(count,),
         in_specs=[small, small],
-        out_specs=large,
-        out_shape=shape,
+        out_specs=[large, large],
+        out_shape=[shape, shape],
         name="tables",
     )(coarse, fine)
 
@@ -267,7 +266,7 @@
     )(offsets, samples_rows, scales)
 
 
-def products(band_ref, sources, base, members, out_ref, g, row):
+def products(band_ref, sources, base, members, emit, g, row):
     src_ref, plus_ref, minus_ref = sources
     count = SEGMENTS
     lane = pl.multiple_of(g * PAIR, PAIR)
@@ -297,8 +296,8 @@
     for j in members:
         real = jnp.concatenate([acc[t, j][0] + acc[t, j][1] for t in range(SUB // 8)], axis=0)
         imag = jnp.concatenate([acc[t, j][0] - acc[t, j][2] for t in range(SUB // 8)], axis=0)
-        out_ref[j, pl.ds(row, SUB), real_lanes] = real.astype(out_ref.dtype)
-        out_ref[j, pl.ds(row, SUB), imag_lanes] = imag.astype(out_ref.dtype)
+        emit(j, pl.ds(row, SUB), real_lanes, real)
+        emit(j, pl.ds(row, SUB), imag_lanes, imag)
 
 
 def outer_kernel(limits_ref, near_ref, far_ref, own_src_ref, above_src_ref, below_src_ref, table_ref,
@@ -337,6 +336,12 @@
             band_ref[2 * g, at, :] = spec[:, :LANES]
             band_ref[2 * g + 1, at, :] = spec[:, LANES:]
 
+    def to_up(j, rows, lanes, value):
+        up_ref[j, rows, lanes] = value.astype(up_ref.dtype)
+
+    def to_down(j, rows, lanes, value):
+        down_ref[j, rows, lanes] = value.astype(down_ref.dtype)
+
     def tile(index, carry):
         g = index // (TILE // SUB)
         row = pl.multiple_of((index % (TILE // SUB)) * SUB, SUB)
@@ -347,25 +352,38 @@
 
             @pl.when(channel + SUB > limits_ref[1 + first])
             def _():
-                products(band_ref, sources, 0, pair, up_ref, g, row)
+                products(band_ref, sources, 0, pair, to_up, g, row)
 
             @pl.when(channel < limits_ref[1 + SOURCES + first + 1])
             def _():
-                products(band_ref, sources, per_side, pair, down_ref, g, row)
+                products(band_ref, sources, per_side, pair, to_down, g, row)
 
         return carry
 
     lax.fori_loop(0, groups * (TILE // SUB), tile, 0)
 
 
-def own_kernel(band_ref, src_ref, plus_ref, minus_ref, out_ref):
+def own_kernel(ordered_ref, place_ref, band_ref, src_ref, plus_ref, minus_ref, below_ref, above_ref,
+               kept_ref, passed_ref):
     groups = src_ref.shape[0]
+    lower = place_ref[1] == 0
+    base = place_ref[0] + pl.program_id(0) * TILE
 
     def tile(index, carry):
         g = index // (TILE // SUB)
         row = pl.multiple_of((index % (TILE // SUB)) * SUB, SUB)
+        channel = base + row + lax.broadcasted_iota(jnp.int32, (SUB, LANES), 0)
+
+        def emit(j, rows, lanes, value):
+            below_source = channel < ordered_ref[j]
+            above = above_ref[j, rows, lanes].astype(jnp.float32)
+            other = jnp.where(below_source, above, below_ref[j, rows, lanes].astype(jnp.float32))
+            keep = jnp.where(below_source, 1, 0) == jnp.where(lower, 1, 0)
+            kept_ref[j, rows, lanes] = jnp.where(keep, value, other)
+            passed_ref[j, rows, lanes] = jnp.where(keep, other, value).astype(jnp.bfloat16)
+
         for first in (0, 2):
-            products(band_ref, (src_ref, plus_ref, minus_ref), 0, (first, first + 1), out_ref, g, row)
+            products(band_ref, (src_ref, plus_ref, minus_ref), 0, (first, first + 1), emit, g, row)
         return carry
 
     lax.fori_loop(0, groups * (TILE // SUB), tile, 0)
@@ -412,25 +430,33 @@
     )(limits, near, far, own_src, above_src, below_src, table)
 
 
-def own_chunk(band, src, plus, minus):
+def own_chunk(ordered, place, band, src, plus, minus, from_below, from_above):
     groups, per_side, _ = src.shape
     steps = HALF // TILE
     width = groups * PAIR
-    spectra = pl.BlockSpec((groups, per_side, LANES), lambda i: (0, 0, 0))
+    spectra = pl.BlockSpec((groups, per_side, LANES), lambda i, o, p: (0, 0, 0))
+    rows = pl.BlockSpec((SOURCES, TILE, width), lambda i, o, p: (0, i, 0))
     return pl.pallas_call(
         own_kernel,
-        grid=(steps,),
-        in_specs=[pl.BlockSpec((2 * groups, band.shape[1] // steps, LANES), lambda i: (0, i, 0)), spectra, spectra, spectra],
-        out_specs=pl.BlockSpec((SOURCES, TILE, width), lambda i: (0, i, 0)),
-        out_shape=jax.ShapeDtypeStruct((SOURCES, HALF, width), jnp.float32),
+        grid_spec=pltpu.PrefetchScalarGridSpec(
+            num_scalar_prefetch=2,
+            grid=(steps,),
+            in_specs=[
+                pl.BlockSpec((2 * groups, band.shape[1] // steps, LANES), lambda i, o, p: (0, i, 0)),
+                spectra,
+                spectra,
+                spectra,
+                rows,
+                rows,
+            ],
+            out_specs=[rows, rows],
+        ),
+        out_shape=[
+            jax.ShapeDtypeStruct((SOURCES, HALF, width), jnp.float32),
+            jax.ShapeDtypeStruct((SOURCES, HALF, width), jnp.bfloat16),
+        ],
         name="own",
-    )(band, src, plus, minus)
-
-
-def select_rows(below_source, keep, own, from_below, from_above):
-    other = jnp.where(below_source, from_above, from_below)
-    kept = jnp.where(keep, own, other.astype(jnp.float32))
-    return kept, jnp.where(keep, other, own.astype(jnp.bfloat16))
+    )(ordered, place, band, src, plus, minus, from_below, from_above)
 
 
 def turned(ordered_ref, mine_ref, mate_ref, top_ref, halve):
@@ -476,19 +502,17 @@
     odd_ref[...] = sums[1]
 
 
-def chunk_specs(groups, first):
-    assert first % groups == 0
+def chunk_specs(groups):
     rows = pl.BlockSpec((SOURCES, HALF, groups * PAIR), lambda m, h: (0, 0, 0))
     table = pl.BlockSpec((groups, COLS, PAIR), lambda m, h: (0, m, 0))
-    rest = pl.BlockSpec((groups, COLS, PAIR), lambda m, h: (first // groups, m, 0))
-    return [rows, rows, table, rest]
+    return [rows, rows, table, table]
 
 
 def early_inverse(ordered, parts, firsts):
     specs, operands, tops = [], [], []
-    for part, first in zip(parts, firsts):
+    for part in parts:
         groups = part[2].shape[0]
-        specs += chunk_specs(groups, first)
+        specs += chunk_specs(groups)
         operands += list(part)
         tops.append(pltpu.VMEM((SOURCES * HALF, groups * PAIR), jnp.bfloat16))
     block = pl.BlockSpec((SOURCES * HALF, COLS), lambda m, h: (0, m))
@@ -548,7 +572,7 @@
         grid_spec=pltpu.PrefetchScalarGridSpec(
             num_scalar_prefetch=1,
             grid=(SEG // COLS,),
-            in_specs=chunk_specs(groups, first) + [block, block],
+            in_specs=chunk_specs(groups) + [block, block],
             out_specs=pl.BlockSpec(memory_space=pl.ANY),
             scratch_shapes=[
                 pltpu.VMEM((SOURCES * HALF, groups * PAIR), jnp.bfloat16),
@@ -606,42 +630,32 @@
     limits = jnp.concatenate(
         [(core * HALF).reshape(1), jnp.where(above_off == 0, channels, above_off - 1), below_off - 1]
     ).astype(jnp.int32)
-    index = core * HALF + jnp.arange(HALF, dtype=jnp.int32)
-    below_source = (index[None, :] < ordered[:SOURCES, None])[:, :, None]
-    keep = below_source == (upper_half == 0)
+    where_am_i = jnp.stack([core * HALF, upper_half]).astype(jnp.int32)
     scale = 2.0 / float(2 * SEG * windows * lax.axis_size("win") * seg_count * SEG)
 
     tables = []
     for first, count in CHUNKS:
         tables.append(make_tables(first, count, coarse, fine))
-    crossed, returned, selected = [], [], []
-
-    def select(c):
-        pieces = (crossed[c],) + returned[c]
-        if c:
-            pieces = lax.optimization_barrier(pieces + (selected[c - 1][2],))[:3]
-        kept, moved = select_rows(below_source, keep, *pieces)
-        selected.append((kept, partner(moved, 2), moved))
+    returned, selected = [], []
 
     kept_spectra = []
     for c in range(len(CHUNKS)):
-        to_above, to_below, *spectra = outer_chunk(limits, near, far, own_src, above_src, below_src, tables[c])
+        to_above, to_below, *spectra = outer_chunk(limits, near, far, own_src, above_src, below_src, tables[c][0])
         kept_spectra.append(spectra)
         from_below = passed_along(to_above, "chan", 1)
         from_above = passed_along(to_below, "chan", -1)
         returned.append((from_below, from_above))
     for c in range(len(CHUNKS)):
-        crossed.append(own_chunk(*kept_spectra[c]))
-        select(c)
-    rest = make_tables(0, GROUPS, coarse, lax.optimization_barrier((fine, selected[0][2]))[0], True)
+        kept, moved = own_chunk(ordered, where_am_i, *kept_spectra[c], *returned[c])
+        selected.append((kept, partner(moved, 2)))
     parts = []
     for c in range(len(CHUNKS)):
-        kept, moved, _ = selected[c]
+        kept, moved = selected[c]
         if c:
             kept = lax.optimization_barrier((kept, parts[c - 1][0]))[0]
         total = (kept + moved.astype(jnp.float32)).astype(jnp.bfloat16)
         mate = partner(total, 1)
-        parts.append((total, mate, tables[c], rest))
+        parts.append((total, mate) + tuple(tables[c]))
     firsts = tuple(first for first, _ in CHUNKS)
     even, odd = early_inverse(ordered, parts[:-1], firsts[:-1])
     return last_inverse(ordered, parts[-1], even, odd, firsts[-1], scale)

time: 174 us -> 169 us (0.971)
  the two profiles are of different devices: /device:TPU:65 before, /device:TPU:97 now
where the time goes in v1:
time: 169 us; the launch traced here: 167 us
  Pallas kernels  98.7 us (58%)
  starting transfers between devices  43.2 us (26%)
  waiting for transfers between devices  14.3 us (8%)
  local copies, waits for them, and re-layouts  6.56 us (4%)
  other arithmetic  4.47 us (3%)
    pallas_call x2, Pallas kernels, outer_chunk(): pl.pallas_call(outer_kernel, grid_spec=pltpu.PrefetchScalarGridSpec(num_s...  38.2 us
    ppermute x6, starting transfers between devices, passed_along(): return lax.ppermute(block, axis, route)  24.9 us
    pallas_call x2, Pallas kernels, own_chunk(): pl.pallas_call(own_kernel, grid_spec=pltpu.PrefetchScalarGridSpec(num_sca...  21 us
    ppermute x6, starting transfers between devices, partner(): lax.ppermute(block, 'win', [(i, i ^ bit) for i in range(lax.axis_size('wi...  18.3 us
    ppermute x6, waiting for transfers between devices, partner(): lax.ppermute(block, 'win', [(i, i ^ bit) for i in range(lax.axis_size('wi...  14.3 us
    pallas_call x2, Pallas kernels, normalize_half(): pl.pallas_call(functools.partial(normalize_kernel, seg_count=seg_count, w...  12.1 us
    pallas_call x2, Pallas kernels, make_tables(): pl.pallas_call(table_kernel, grid=(count,), in_specs=[small, small], out_...  8.44 us
    pallas_call x1, Pallas kernels, last_inverse(): pl.pallas_call(functools.partial(last_kernel, first=first, scale=scale),...  8.06 us
  transfers between devices with their start and end apart: 12, of which 3 were waited for; matrix products, arithmetic and copies ran while one was open for 2% of the time, Pallas kernels for 39%

profile of v1, /device:TPU:97, one launch (start us, length us, event | category | flops | bytes accessed | tf_op | source)
XLA Modules:
  0.0 167.4 jit_solution(10217852628138699369)
XLA Ops:
  0.0 0.9 select_reduce_fusion
  1.0 0.7 convert_element_type.27
  1.8 0.7 pad_maximum_fusion.scale_ref
  2.6 6.1 %normalize.3 = bf16[12,96,1024]{2,1,0:T(8,128)(2,1)} custom-call(s32[1]{0:T(128)} %bitcast.10.half_ref, s32[192,96,128]{2,1,0:T(8,128)} %bitcast.11, f32[192,49]{1,0:T(8,128)} %pad_maximum_fusion.scale_ref), custom_call_target="tpu_custom_call" | custom-call | tf_op jit(solution)/shard_map/normalize/pallas_call | solution.py:153
  8.6 0.8 collective-permute-start.3
  9.4 3.8 %sources.1 = (bf16[4,16,1024]{2,1,0:T(8,128)(2,1)}, s32[8]{0:T(128)}) custom-call(s32[4]{0:T(128)} %offsets_ref.1, s32[192,96,128]{2,1,0:T(8,128)} %bitcast.12, f32[192,49]{1,0:T(8,128)} %pad_maximum_fusion.scale_ref), custom_call_target="tpu_custom_call" | custom-call | tf_op jit(solution)/shard_map/sources/pallas_call | solution.py:242
  13.3 0.9 constant_dynamic-update-slice_fusion.1
  14.9 3.2 %collective-permute-start.2 = (bf16[4,32,1024]{2,1,0:T(8,128)(2,1)S(1)}, bf16[4,32,1024]{2,1,0:T(8,128)(2,1)S(1)}, u32[]{:S(2)}, u32[]{:S(2)}) collective-permute-start(bf16[4,32,1024]{2,1,0:T(8,128)(2,1)S(1)} %constant_dynamic-update-slice_fusion.own_src_ref), channel_id=1, source_target_pairs={{0,4},{4,8},{8,12},{12,16},{16,20},{20,24},{24,28},{28,32},{32,36}... | collective-permute-start | bytes 786440 | tf_op jit(solution)/shard_map/ppermute | solution.py:597
  18.1 5.1 %collective-permute-start.1 = (bf16[4,32,1024]{2,1,0:T(8,128)(2,1)S(1)}, bf16[4,32,1024]{2,1,0:T(8,128)(2,1)S(1)}, u32[]{:S(2)}, u32[]{:S(2)}) collective-permute-start(bf16[4,32,1024]{2,1,0:T(8,128)(2,1)S(1)} %constant_dynamic-update-slice_fusion.own_src_ref), channel_id=1, source_target_pairs={{4,0},{8,4},{12,8},{16,12},{20,16},{24,20},{28,24},{32,28},{36,32}... | collective-permute-start | bytes 786440 | tf_op jit(solution)/shard_map/ppermute | solution.py:597
  23.2 6.1 %normalize.2.near_ref = bf16[12,96,1024]{2,1,0:T(8,128)(2,1)} custom-call(s32[1]{0:T(128)} %bitcast.7.half_ref, s32[192,96,128]{2,1,0:T(8,128)} %bitcast.13, f32[192,49]{1,0:T(8,128)} %pad_maximum_fusion.scale_ref), custom_call_target="tpu_custom_call" | custom-call | tf_op jit(solution)/shard_map/normalize/pallas_call | solution.py:153
  29.3 4.2 %tables.3 = (bf16[4,1024,256]{2,1,0:T(8,128)(2,1)}, bf16[4,1024,256]{2,1,0:T(8,128)(2,1)}) custom-call(f32[8,2,32,128]{3,2,1,0:T(8,128)} %constant.24.clone.coarse_ref, f32[8,2,32,128]{3,2,1,0:T(8,128)} %constant.25.clone.fine_ref), custom_call_target="tpu_custom_call" | custom-call | tf_op jit(solution)/shard_map/tables/pallas_call | solution.py:69
  34.5 1.4 copy-done
  35.9 19.1 %outer.3 = (bf16[4,96,1024]{2,1,0:T(8,128)(2,1)}, bf16[4,96,1024]{2,1,0:T(8,128)(2,1)}, f32[8,2304,128]{2,1,0:T(8,128)}, f32[4,128,128]{2,1,0:T(8,128)}, f32[4,128,128]{2,1,0:T(8,128)}, /*index=5*/f32[4,128,128]{2,1,0:T(8,128)}) custom-call(s32[9]{0:T(128)} %pad_add_fusion.1.limits_ref, bf16[12,96,1024]{2,1,0:T(8,128)(2,1)} %normalize.2.near_ref, ...), custom_call_target="tpu_custom_call" | custom-call | tf_op jit(solution)/shard_map/outer/pallas_call | solution.py:405
  55.0 1.9 %collective-permute-start.6 = (bf16[4,96,1024]{2,1,0:T(8,128)(2,1)}, bf16[4,96,1024]{2,1,0:T(8,128)(2,1)S(1)}, u32[]{:S(2)}, u32[]{:S(2)}) collective-permute-start(bf16[4,96,1024]{2,1,0:T(8,128)(2,1)} %get-tuple-element.45), channel_id=1, source_target_pairs={{0,4},{4,8},{8,12},{12,16},{16,20},{20,24},{24,28},{28,32},{32,36}... | collective-permute-start | bytes 2359304 | tf_op jit(solution)/shard_map/ppermute | solution.py:597
  57.0 6.4 %collective-permute-start.7 = (bf16[4,96,1024]{2,1,0:T(8,128)(2,1)}, bf16[4,96,1024]{2,1,0:T(8,128)(2,1)S(1)}, u32[]{:S(2)}, u32[]{:S(2)}) collective-permute-start(bf16[4,96,1024]{2,1,0:T(8,128)(2,1)} %get-tuple-element.46), channel_id=1, source_target_pairs={{4,0},{8,4},{12,8},{16,12},{20,16},{24,20},{28,24},{32,28},{36,32}... | collective-permute-start | bytes 2359304 | tf_op jit(solution)/shard_map/ppermute | solution.py:597
  63.3 4.2 %tables.2 = (bf16[4,1024,256]{2,1,0:T(8,128)(2,1)}, bf16[4,1024,256]{2,1,0:T(8,128)(2,1)}) custom-call(f32[8,2,32,128]{3,2,1,0:T(8,128)} %constant.24.clone.coarse_ref, f32[8,2,32,128]{3,2,1,0:T(8,128)} %constant.25.clone.fine_ref), custom_call_target="tpu_custom_call" | custom-call | tf_op jit(solution)/shard_map/tables/pallas_call | solution.py:69
  67.6 19.1 %outer.2 = (bf16[4,96,1024]{2,1,0:T(8,128)(2,1)}, bf16[4,96,1024]{2,1,0:T(8,128)(2,1)}, f32[8,2304,128]{2,1,0:T(8,128)}, f32[4,128,128]{2,1,0:T(8,128)}, f32[4,128,128]{2,1,0:T(8,128)}, /*index=5*/f32[4,128,128]{2,1,0:T(8,128)}) custom-call(s32[9]{0:T(128)} %pad_add_fusion.1.limits_ref, bf16[12,96,1024]{2,1,0:T(8,128)(2,1)} %normalize.2.near_ref, ...), custom_call_target="tpu_custom_call" | custom-call | tf_op jit(solution)/shard_map/outer/pallas_call | solution.py:405
  86.7 1.9 %collective-permute-start.4 = (bf16[4,96,1024]{2,1,0:T(8,128)(2,1)}, bf16[4,96,1024]{2,1,0:T(8,128)(2,1)S(1)}, u32[]{:S(2)}, u32[]{:S(2)}) collective-permute-start(bf16[4,96,1024]{2,1,0:T(8,128)(2,1)} %get-tuple-element.37), channel_id=1, source_target_pairs={{0,4},{4,8},{8,12},{12,16},{16,20},{20,24},{24,28},{28,32},{32,36}... | collective-permute-start | bytes 2359304 | tf_op jit(solution)/shard_map/ppermute | solution.py:597
  88.6 6.4 %collective-permute-start.5 = (bf16[4,96,1024]{2,1,0:T(8,128)(2,1)}, bf16[4,96,1024]{2,1,0:T(8,128)(2,1)S(1)}, u32[]{:S(2)}, u32[]{:S(2)}) collective-permute-start(bf16[4,96,1024]{2,1,0:T(8,128)(2,1)} %get-tuple-element.38), channel_id=1, source_target_pairs={{4,0},{8,4},{12,8},{16,12},{20,16},{24,20},{28,24},{32,28},{36,32}... | collective-permute-start | bytes 2359304 | tf_op jit(solution)/shard_map/ppermute | solution.py:597
  95.6 0.9 copy-done.8
  96.7 10.5 %own.3 = (f32[4,96,1024]{2,1,0:T(8,128)}, bf16[4,96,1024]{2,1,0:T(8,128)(2,1)}) custom-call(s32[8]{0:T(128)} %get-tuple-element.30.ordered_ref, s32[2]{0:T(128)} %pad_add_fusion.place_ref, f32[8,2304,128]{2,1,0:T(8,128)} %get-tuple-element.41.band_ref, f32[4,128,128]{2,1,0:T(8,128)} %get-tuple-element.42.src_ref, f32[4,128,128]{2,1,0:T(8,128)} %get-tuple-element.43.plus_ref, ...), custom_call_target="tpu_custom_call" | custom-call | tf_op jit(solution)/shard_map/own/pallas_call | solution.py:439
  107.2 2.7 %collective-permute-start.8 = (bf16[4,96,1024]{2,1,0:T(8,128)(2,1)}, bf16[4,96,1024]{2,1,0:T(8,128)(2,1)S(1)}, u32[]{:S(2)}, u32[]{:S(2)}) collective-permute-start(bf16[4,96,1024]{2,1,0:T(8,128)(2,1)} %get-tuple-element.48), channel_id=1, source_target_pairs={{0,2},{1,3},{2,0},{3,1},{4,6},{5,7},{6,4},{7,5},{8,10},{9,11},{10,... | collective-permute-start | bytes 2359304 | tf_op jit(solution)/shard_map/ppermute | solution.py:601
  109.9 0.9 copy-done.11
  111.1 10.5 %own.2 = (f32[4,96,1024]{2,1,0:T(8,128)}, bf16[4,96,1024]{2,1,0:T(8,128)(2,1)}) custom-call(s32[8]{0:T(128)} %get-tuple-element.30.ordered_ref, s32[2]{0:T(128)} %pad_add_fusion.place_ref, f32[8,2304,128]{2,1,0:T(8,128)} %get-tuple-element.33.band_ref, f32[4,128,128]{2,1,0:T(8,128)} %get-tuple-element.34.src_ref, f32[4,128,128]{2,1,0:T(8,128)} %get-tuple-element.35.plus_ref, ...), custom_call_target="tpu_custom_call" | custom-call | tf_op jit(solution)/shard_map/own/pallas_call | solution.py:439
  122.1 6.3 %collective-permute-done.8 = bf16[4,96,1024]{2,1,0:T(8,128)(2,1)S(1)} collective-permute-done((bf16[4,96,1024]{2,1,0:T(8,128)(2,1)}, bf16[4,96,1024]{2,1,0:T(8,128)(2,1)S(1)}, u32[]{:S(2)}, u32[]{:S(2)}) %collective-permute-start.8) | collective-permute-done | bytes 786464 | tf_op jit(solution)/shard_map/ppermute | solution.py:601
  128.7 9.3 %collective-permute-start.11 = (bf16[4,96,1024]{2,1,0:T(8,128)(2,1)S(1)}, bf16[4,96,1024]{2,1,0:T(8,128)(2,1)S(1)}, u32[]{:S(2)}, u32[]{:S(2)}) collective-permute-start(bf16[4,96,1024]{2,1,0:T(8,128)(2,1)S(1)} %add_convert_fusion.1.refs_0_), channel_id=1, source_target_pairs={{0,1},{1,0},{2,3},{3,2},{4,5},{5,4},{6,7},{7,6},{8,9},{9,8},{10,11... | collective-permute-start | bytes 2359304 | tf_op jit(solution)/shard_map/ppermute | solution.py:601
  138.0 7.3 %collective-permute-done.9 = bf16[4,96,1024]{2,1,0:T(8,128)(2,1)S(1)} collective-permute-done((bf16[4,96,1024]{2,1,0:T(8,128)(2,1)}, bf16[4,96,1024]{2,1,0:T(8,128)(2,1)S(1)}, u32[]{:S(2)}, u32[]{:S(2)}) %collective-permute-start.9) | collective-permute-done | bytes 786464 | tf_op jit(solution)/shard_map/ppermute | solution.py:601
  145.6 4.9 %collective-permute-start.10 = (bf16[4,96,1024]{2,1,0:T(8,128)(2,1)S(1)}, bf16[4,96,1024]{2,1,0:T(8,128)(2,1)S(1)}, u32[]{:S(2)}, u32[]{:S(2)}) collective-permute-start(bf16[4,96,1024]{2,1,0:T(8,128)(2,1)S(1)} %add_convert_fusion.mine_ref), channel_id=1, source_target_pairs={{0,1},{1,0},{2,3},{3,2},{4,5},{5,4},{6,7},{7,6},{8,9},{9,8},{10,11... | collective-permute-start | bytes 2359304 | tf_op jit(solution)/shard_map/ppermute | solution.py:601
  150.5 0.9 copy-done.13
  151.3 7.1 %early.1 = (f32[384,1024]{1,0:T(8,128)}, f32[384,1024]{1,0:T(8,128)}) custom-call(s32[8]{0:T(128)} %get-tuple-element.30.ordered_ref, bf16[4,96,1024]{2,1,0:T(8,128)(2,1)} %copy-done.2, bf16[4,96,1024]{2,1,0:T(8,128)(2,1)} %copy-done.13, bf16[4,1024,256]{2,1,0:T(8,128)(2,1)} %get-tuple-element.40.table_ref.refs_2_, ...), custom_call_target="tpu_custom_call" | custom-call | tf_op jit(solution)/shard_map/early/pallas_call | solution.py:520
  158.5 0.9 copy-done.12
  159.4 8.1 %last.1 = f32[4,96,2048]{2,1,0:T(8,128)} custom-call(s32[8]{0:T(128)} %get-tuple-element.30.ordered_ref, bf16[4,96,1024]{2,1,0:T(8,128)(2,1)} %copy-done.1, bf16[4,96,1024]{2,1,0:T(8,128)(2,1)} %copy-done.12, bf16[4,1024,256]{2,1,0:T(8,128)(2,1)} %get-tuple-element.32.table_ref.hi_ref, bf16[4,1024,256]{2,1,0:T(8,128)(2,1)} %get-tuple-element.51.lo_ref, ...), custom_call_target="tpu_custom_call" | custom-call | tf_op jit(solution)/shard_map/last/pallas_call | solution.py:570
  (45 shorter events, 4.2 us)
Async XLA Ops:
  8.6 25.9 %collective-permute-start.3 = (bf16[12,96,1024]{2,1,0:T(8,128)(2,1)}, bf16[12,96,1024]{2,1,0:T(8,128)(2,1)S(1)}, u32[]{:S(2)}, u32[]{:S(2)}) collective-permute-start(bf16[12,96,1024]{2,1,0:T(8,128)(2,1)} %normalize.3), channel_id=1, source_target_pairs={{0,1},{1,0},{2,3},{3,2},{4,5},{5,4},{6,7},{7,6},{8,9},{9,8},{10,11... | collective-permute-start | bytes 7077896 | tf_op jit(solution)/shard_map/ppermute | solution.py:601
  13.2 1.6 collective-permute-start
  14.9 14.4 %copy-start.3 = (bf16[4,32,1024]{2,1,0:T(8,128)(2,1)}, bf16[4,32,1024]{2,1,0:T(8,128)(2,1)S(1)}, u32[]{:S(2)}) copy-start(bf16[4,32,1024]{2,1,0:T(8,128)(2,1)S(1)} %constant_dynamic-update-slice_fusion.own_src_ref) | copy-start | bytes 786436
  14.9 18.6 %collective-permute-start.2 = (bf16[4,32,1024]{2,1,0:T(8,128)(2,1)S(1)}, bf16[4,32,1024]{2,1,0:T(8,128)(2,1)S(1)}, u32[]{:S(2)}, u32[]{:S(2)}) collective-permute-start(bf16[4,32,1024]{2,1,0:T(8,128)(2,1)S(1)} %constant_dynamic-update-slice_fusion.own_src_ref), channel_id=1, source_target_pairs={{0,4},{4,8},{8,12},{12,16},{16,20},{20,24},{24,28},{28,32},{32,36}... | collective-permute-start | bytes 786440 | tf_op jit(solution)/shard_map/ppermute | solution.py:597
  18.1 15.5 %collective-permute-start.1 = (bf16[4,32,1024]{2,1,0:T(8,128)(2,1)S(1)}, bf16[4,32,1024]{2,1,0:T(8,128)(2,1)S(1)}, u32[]{:S(2)}, u32[]{:S(2)}) collective-permute-start(bf16[4,32,1024]{2,1,0:T(8,128)(2,1)S(1)} %constant_dynamic-update-slice_fusion.own_src_ref), channel_id=1, source_target_pairs={{4,0},{8,4},{12,8},{16,12},{20,16},{24,20},{28,24},{32,28},{36,32}... | collective-permute-start | bytes 786440 | tf_op jit(solution)/shard_map/ppermute | solution.py:597
  33.5 1.0 copy-start.6
  33.7 0.9 copy-start.7
  34.5 1.4 copy-start
  55.0 40.6 %collective-permute-start.6 = (bf16[4,96,1024]{2,1,0:T(8,128)(2,1)}, bf16[4,96,1024]{2,1,0:T(8,128)(2,1)S(1)}, u32[]{:S(2)}, u32[]{:S(2)}) collective-permute-start(bf16[4,96,1024]{2,1,0:T(8,128)(2,1)} %get-tuple-element.45), channel_id=1, source_target_pairs={{0,4},{4,8},{8,12},{12,16},{16,20},{20,24},{24,28},{28,32},{32,36}... | collective-permute-start | bytes 2359304 | tf_op jit(solution)/shard_map/ppermute | solution.py:597
  57.0 38.6 %collective-permute-start.7 = (bf16[4,96,1024]{2,1,0:T(8,128)(2,1)}, bf16[4,96,1024]{2,1,0:T(8,128)(2,1)S(1)}, u32[]{:S(2)}, u32[]{:S(2)}) collective-permute-start(bf16[4,96,1024]{2,1,0:T(8,128)(2,1)} %get-tuple-element.46), channel_id=1, source_target_pairs={{4,0},{8,4},{12,8},{16,12},{20,16},{24,20},{28,24},{32,28},{36,32}... | collective-permute-start | bytes 2359304 | tf_op jit(solution)/shard_map/ppermute | solution.py:597
  86.7 23.3 %collective-permute-start.4 = (bf16[4,96,1024]{2,1,0:T(8,128)(2,1)}, bf16[4,96,1024]{2,1,0:T(8,128)(2,1)S(1)}, u32[]{:S(2)}, u32[]{:S(2)}) collective-permute-start(bf16[4,96,1024]{2,1,0:T(8,128)(2,1)} %get-tuple-element.37), channel_id=1, source_target_pairs={{0,4},{4,8},{8,12},{12,16},{16,20},{20,24},{24,28},{28,32},{32,36}... | collective-permute-start | bytes 2359304 | tf_op jit(solution)/shard_map/ppermute | solution.py:597
  88.6 21.3 %collective-permute-start.5 = (bf16[4,96,1024]{2,1,0:T(8,128)(2,1)}, bf16[4,96,1024]{2,1,0:T(8,128)(2,1)S(1)}, u32[]{:S(2)}, u32[]{:S(2)}) collective-permute-start(bf16[4,96,1024]{2,1,0:T(8,128)(2,1)} %get-tuple-element.38), channel_id=1, source_target_pairs={{4,0},{8,4},{12,8},{16,12},{20,16},{24,20},{28,24},{32,28},{36,32}... | collective-permute-start | bytes 2359304 | tf_op jit(solution)/shard_map/ppermute | solution.py:597
  95.6 0.9 copy-start.8
  95.6 1.1 copy-start.9
  107.2 21.3 %collective-permute-start.8 = (bf16[4,96,1024]{2,1,0:T(8,128)(2,1)}, bf16[4,96,1024]{2,1,0:T(8,128)(2,1)S(1)}, u32[]{:S(2)}, u32[]{:S(2)}) collective-permute-start(bf16[4,96,1024]{2,1,0:T(8,128)(2,1)} %get-tuple-element.48), channel_id=1, source_target_pairs={{0,2},{1,3},{2,0},{3,1},{4,6},{5,7},{6,4},{7,5},{8,10},{9,11},{10,... | collective-permute-start | bytes 2359304 | tf_op jit(solution)/shard_map/ppermute | solution.py:601
  109.9 1.1 copy-start.10
  109.9 0.9 copy-start.11
  111.1 17.4 %copy-start.4 = (f32[4,96,1024]{2,1,0:T(8,128)S(1)}, f32[4,96,1024]{2,1,0:T(8,128)}, u32[]{:S(2)}) copy-start(f32[4,96,1024]{2,1,0:T(8,128)} %get-tuple-element.47) | copy-start | bytes 4718596
  121.6 23.7 %copy-start.5 = (f32[4,96,1024]{2,1,0:T(8,128)S(1)}, f32[4,96,1024]{2,1,0:T(8,128)}, u32[]{:S(2)}) copy-start(f32[4,96,1024]{2,1,0:T(8,128)} %get-tuple-element.49) | copy-start | bytes 4718596
  121.6 23.7 %collective-permute-start.9 = (bf16[4,96,1024]{2,1,0:T(8,128)(2,1)}, bf16[4,96,1024]{2,1,0:T(8,128)(2,1)S(1)}, u32[]{:S(2)}, u32[]{:S(2)}) collective-permute-start(bf16[4,96,1024]{2,1,0:T(8,128)(2,1)} %get-tuple-element.50), channel_id=1, source_target_pairs={{0,2},{1,3},{2,0},{3,1},{4,6},{5,7},{6,4},{7,5},{8,10},{9,11},{10,... | collective-permute-start | bytes 2359304 | tf_op jit(solution)/shard_map/ppermute | solution.py:601
  128.7 21.7 %copy-start.2 = (bf16[4,96,1024]{2,1,0:T(8,128)(2,1)}, bf16[4,96,1024]{2,1,0:T(8,128)(2,1)S(1)}, u32[]{:S(2)}) copy-start(bf16[4,96,1024]{2,1,0:T(8,128)(2,1)S(1)} %add_convert_fusion.1.refs_0_) | copy-start | bytes 2359300
  128.7 21.7 %collective-permute-start.11 = (bf16[4,96,1024]{2,1,0:T(8,128)(2,1)S(1)}, bf16[4,96,1024]{2,1,0:T(8,128)(2,1)S(1)}, u32[]{:S(2)}, u32[]{:S(2)}) collective-permute-start(bf16[4,96,1024]{2,1,0:T(8,128)(2,1)S(1)} %add_convert_fusion.1.refs_0_), channel_id=1, source_target_pairs={{0,1},{1,0},{2,3},{3,2},{4,5},{5,4},{6,7},{7,6},{8,9},{9,8},{10,11... | collective-permute-start | bytes 2359304 | tf_op jit(solution)/shard_map/ppermute | solution.py:601
  145.6 12.9 %copy-start.1 = (bf16[4,96,1024]{2,1,0:T(8,128)(2,1)}, bf16[4,96,1024]{2,1,0:T(8,128)(2,1)S(1)}, u32[]{:S(2)}) copy-start(bf16[4,96,1024]{2,1,0:T(8,128)(2,1)S(1)} %add_convert_fusion.mine_ref) | copy-start | bytes 2359300
  145.6 12.9 %collective-permute-start.10 = (bf16[4,96,1024]{2,1,0:T(8,128)(2,1)S(1)}, bf16[4,96,1024]{2,1,0:T(8,128)(2,1)S(1)}, u32[]{:S(2)}, u32[]{:S(2)}) collective-permute-start(bf16[4,96,1024]{2,1,0:T(8,128)(2,1)S(1)} %add_convert_fusion.mine_ref), channel_id=1, source_target_pairs={{0,1},{1,0},{2,3},{3,2},{4,5},{5,4},{6,7},{7,6},{8,9},{9,8},{10,11... | collective-permute-start | bytes 2359304 | tf_op jit(solution)/shard_map/ppermute | solution.py:601
  150.5 0.9 copy-start.13
  158.5 0.9 copy-start.12

commit v2 on v1

--- a/solution.py
+++ b/solution.py
@@ -15,7 +15,7 @@
 LANES = 128
 GROUPS = SEG // LANES
 PAIR = 2 * LANES
-CHUNKS = ((0, 4), (4, 4))
+CHUNKS = ((0, 5), (5, 3))
 FOLD = 32
 UNROLL = 4
 TILE = 32
@@ -39,7 +39,7 @@
     return waves(FOLD), waves(1)
 
 
-def table_kernel(coarse_ref, fine_ref, hi_ref, lo_ref):
+def table_kernel(coarse_ref, fine_ref, out_ref, *, rest):
     fine_cos = fine_ref[0, 0]
     fine_sin = fine_ref[0, 1]
 
@@ -55,23 +55,24 @@
             rows = pl.ds(pl.multiple_of(a * FOLD, FOLD), FOLD)
             for part, lane in ((real, 0), (imag, LANES)):
                 top = part.astype(jnp.bfloat16)
-                hi_ref[0, rows, lane:lane + LANES] = top
-                lo_ref[0, rows, lane:lane + LANES] = (part - top.astype(jnp.float32)).astype(jnp.bfloat16)
+                if rest:
+                    top = (part - top.astype(jnp.float32)).astype(jnp.bfloat16)
+                out_ref[0, rows, lane:lane + LANES] = top
         return carry
 
     lax.fori_loop(0, FOLD // UNROLL, row_block, 0)
 
 
-def make_tables(first, count, coarse, fine):
+def make_tables(first, count, coarse, fine, rest=False):
     shape = jax.ShapeDtypeStruct((count, SEG, PAIR), jnp.bfloat16)
     small = pl.BlockSpec((1, 2, FOLD, LANES), lambda p: (first + p, 0, 0, 0))
     large = pl.BlockSpec((1, SEG, PAIR), lambda p: (p, 0, 0))
     return pl.pallas_call(
-        table_kernel,
+        functools.partial(table_kernel, rest=rest),
         grid=(count,),
         in_specs=[small, small],
-        out_specs=[large, large],
-        out_shape=[shape, shape],
+        out_specs=large,
+        out_shape=shape,
         name="tables",
     )(coarse, fine)
 
@@ -640,22 +641,26 @@
 
     kept_spectra = []
     for c in range(len(CHUNKS)):
-        to_above, to_below, *spectra = outer_chunk(limits, near, far, own_src, above_src, below_src, tables[c][0])
+        to_above, to_below, *spectra = outer_chunk(limits, near, far, own_src, above_src, below_src, tables[c])
         kept_spectra.append(spectra)
         from_below = passed_along(to_above, "chan", 1)
         from_above = passed_along(to_below, "chan", -1)
         returned.append((from_below, from_above))
     for c in range(len(CHUNKS)):
         kept, moved = own_chunk(ordered, where_am_i, *kept_spectra[c], *returned[c])
-        selected.append((kept, partner(moved, 2)))
+        selected.append((kept, partner(moved, 2), moved))
+    rests = []
+    for first, count in CHUNKS:
+        later = lax.optimization_barrier((fine, selected[-1][2]))[0]
+        rests.append(make_tables(first, count, coarse, later, True))
     parts = []
     for c in range(len(CHUNKS)):
-        kept, moved = selected[c]
+        kept, moved, _ = selected[c]
         if c:
             kept = lax.optimization_barrier((kept, parts[c - 1][0]))[0]
         total = (kept + moved.astype(jnp.float32)).astype(jnp.bfloat16)
         mate = partner(total, 1)
-        parts.append((total, mate) + tuple(tables[c]))
+        parts.append((total, mate, tables[c], rests[c]))
     firsts = tuple(first for first, _ in CHUNKS)
     even, odd = early_inverse(ordered, parts[:-1], firsts[:-1])
     return last_inverse(ordered, parts[-1], even, odd, firsts[-1], scale)

time: 169 us -> 199 us (1.18)
  the two profiles are of different devices: /device:TPU:97 before, /device:TPU:89 now
where the time goes in v2:
time: 199 us; the launch traced here: 197 us
  Pallas kernels  110 us (55%)
  waiting for transfers between devices  52.7 us (26%)
  starting transfers between devices  21.8 us (11%)
  local copies, waits for them, and re-layouts  7.03 us (4%)
  other arithmetic  5.54 us (3%)
    pallas_call x2, Pallas kernels, outer_chunk(): pl.pallas_call(outer_kernel, grid_spec=pltpu.PrefetchScalarGridSpec(num_s...  43.4 us
    ppermute x6, waiting for transfers between devices, passed_along(): return lax.ppermute(block, axis, route)  39.4 us
    pallas_call x2, Pallas kernels, own_chunk(): pl.pallas_call(own_kernel, grid_spec=pltpu.PrefetchScalarGridSpec(num_sca...  21.2 us
    ppermute x6, starting transfers between devices, passed_along(): return lax.ppermute(block, axis, route)  15.8 us
    pallas_call x4, Pallas kernels, make_tables(): pl.pallas_call(functools.partial(table_kernel, rest=rest), grid=(count,),...  14.1 us
    ppermute x6, waiting for transfers between devices, partner(): lax.ppermute(block, 'win', [(i, i ^ bit) for i in range(lax.axis_size('wi...  13.4 us
    pallas_call x2, Pallas kernels, normalize_half(): pl.pallas_call(functools.partial(normalize_kernel, seg_count=seg_count, w...  12.1 us
    pallas_call x1, Pallas kernels, early_inverse(): pl.pallas_call(functools.partial(early_kernel, firsts=firsts), grid_spec=...  7.85 us
  transfers between devices with their start and end apart: 12, of which 6 were waited for; matrix products, arithmetic and copies ran while one was open for 2% of the time, Pallas kernels for 29%

profile of v2, /device:TPU:89, one launch (start us, length us, event | category | flops | bytes accessed | tf_op | source)
XLA Modules:
  0.0 197.1 jit_solution(17868710829201528301)
XLA Ops:
  2.6 6.1 %normalize.3 = bf16[12,96,1024]{2,1,0:T(8,128)(2,1)} custom-call(s32[1]{0:T(128)} %bitcast.10.half_ref, s32[192,96,128]{2,1,0:T(8,128)} %bitcast.11, f32[192,49]{1,0:T(8,128)} %pad_maximum_fusion.scale_ref), custom_call_target="tpu_custom_call" | custom-call | tf_op jit(solution)/shard_map/normalize/pallas_call | solution.py:154
  9.4 3.8 %sources.1 = (bf16[4,16,1024]{2,1,0:T(8,128)(2,1)}, s32[8]{0:T(128)}) custom-call(s32[4]{0:T(128)} %offsets_ref.1, s32[192,96,128]{2,1,0:T(8,128)} %bitcast.12, f32[192,49]{1,0:T(8,128)} %pad_maximum_fusion.scale_ref), custom_call_target="tpu_custom_call" | custom-call | tf_op jit(solution)/shard_map/sources/pallas_call | solution.py:243
  13.3 0.9 constant_dynamic-update-slice_fusion.1
  14.9 2.8 %collective-permute-start.2 = (bf16[4,32,1024]{2,1,0:T(8,128)(2,1)S(1)}, bf16[4,32,1024]{2,1,0:T(8,128)(2,1)S(1)}, u32[]{:S(2)}, u32[]{:S(2)}) collective-permute-start(bf16[4,32,1024]{2,1,0:T(8,128)(2,1)S(1)} %constant_dynamic-update-slice_fusion.own_src_ref), channel_id=1, source_target_pairs={{0,4},{4,8},{8,12},{12,16},{16,20},{20,24},{24,28},{28,32},{32,36}... | collective-permute-start | bytes 786440 | tf_op jit(solution)/shard_map/ppermute | solution.py:598
  17.7 2.5 %collective-permute-start.1 = (bf16[4,32,1024]{2,1,0:T(8,128)(2,1)S(1)}, bf16[4,32,1024]{2,1,0:T(8,128)(2,1)S(1)}, u32[]{:S(2)}, u32[]{:S(2)}) collective-permute-start(bf16[4,32,1024]{2,1,0:T(8,128)(2,1)S(1)} %constant_dynamic-update-slice_fusion.own_src_ref), channel_id=1, source_target_pairs={{4,0},{8,4},{12,8},{16,12},{20,16},{24,20},{28,24},{32,28},{36,32}... | collective-permute-start | bytes 786440 | tf_op jit(solution)/shard_map/ppermute | solution.py:598
  20.2 6.1 %normalize.2.near_ref = bf16[12,96,1024]{2,1,0:T(8,128)(2,1)} custom-call(s32[1]{0:T(128)} %bitcast.7.half_ref, s32[192,96,128]{2,1,0:T(8,128)} %bitcast.13, f32[192,49]{1,0:T(8,128)} %pad_maximum_fusion.scale_ref), custom_call_target="tpu_custom_call" | custom-call | tf_op jit(solution)/shard_map/normalize/pallas_call | solution.py:154
  26.3 3.9 %tables.5.table_ref.refs_2_ = bf16[5,1024,256]{2,1,0:T(8,128)(2,1)} custom-call(f32[8,2,32,128]{3,2,1,0:T(8,128)} %constant.24.clone.coarse_ref, f32[8,2,32,128]{3,2,1,0:T(8,128)} %constant.25.clone.fine_ref), custom_call_target="tpu_custom_call" | custom-call | tf_op jit(solution)/shard_map/tables/pallas_call | solution.py:70
  31.2 1.4 copy-done
  32.6 26.1 %outer.3 = (bf16[4,96,1280]{2,1,0:T(8,128)(2,1)}, bf16[4,96,1280]{2,1,0:T(8,128)(2,1)}, f32[10,2304,128]{2,1,0:T(8,128)}, f32[5,128,128]{2,1,0:T(8,128)}, f32[5,...) custom-call(s32[9]{0:T(128)} %pad_add_fusion.1.limits_ref, bf16[12,96,1024]{2,1,0:T(8,128)(2,1)} %normalize.2.near_ref, ...), custom_call_target="tpu_custom_call" | custom-call | tf_op jit(solution)/shard_map/outer/pallas_call | solution.py:406
  58.7 2.2 %collective-permute-start.6 = (bf16[4,96,1280]{2,1,0:T(8,128)(2,1)}, bf16[4,96,1280]{2,1,0:T(8,128)(2,1)S(1)}, u32[]{:S(2)}, u32[]{:S(2)}) collective-permute-start(bf16[4,96,1280]{2,1,0:T(8,128)(2,1)} %get-tuple-element.40), channel_id=1, source_target_pairs={{0,4},{4,8},{8,12},{12,16},{16,20},{20,24},{24,28},{28,32},{32,36}... | collective-permute-start | bytes 2949128 | tf_op jit(solution)/shard_map/ppermute | solution.py:598
  60.9 3.1 %collective-permute-start.7 = (bf16[4,96,1280]{2,1,0:T(8,128)(2,1)}, bf16[4,96,1280]{2,1,0:T(8,128)(2,1)S(1)}, u32[]{:S(2)}, u32[]{:S(2)}) collective-permute-start(bf16[4,96,1280]{2,1,0:T(8,128)(2,1)} %get-tuple-element.41), channel_id=1, source_target_pairs={{4,0},{8,4},{12,8},{16,12},{20,16},{24,20},{28,24},{32,28},{36,32}... | collective-permute-start | bytes 2949128 | tf_op jit(solution)/shard_map/ppermute | solution.py:598
  64.6 19.6 %collective-permute-done.6.below_ref = bf16[4,96,1280]{2,1,0:T(8,128)(2,1)S(1)} collective-permute-done((bf16[4,96,1280]{2,1,0:T(8,128)(2,1)}, bf16[4,96,1280]{2,1,0:T(8,128)(2,1)S(1)}, u32[]{:S(2)}, u32[]{:S(2)}) %collective-permute-start.6) | collective-permute-done | bytes 983072 | tf_op jit(solution)/shard_map/ppermute | solution.py:598
  84.2 3.7 %collective-permute-done.7.above_ref = bf16[4,96,1280]{2,1,0:T(8,128)(2,1)S(1)} collective-permute-done((bf16[4,96,1280]{2,1,0:T(8,128)(2,1)}, bf16[4,96,1280]{2,1,0:T(8,128)(2,1)S(1)}, u32[]{:S(2)}, u32[]{:S(2)}) %collective-permute-start.7) | collective-permute-done | bytes 983072 | tf_op jit(solution)/shard_map/ppermute | solution.py:598
  88.0 0.9 copy-done.10
  88.9 12.5 %own.3 = (f32[4,96,1280]{2,1,0:T(8,128)}, bf16[4,96,1280]{2,1,0:T(8,128)(2,1)}) custom-call(s32[8]{0:T(128)} %get-tuple-element.27.ordered_ref, s32[2]{0:T(128)} %pad_add_fusion.place_ref, f32[10,2304,128]{2,1,0:T(8,128)} %get-tuple-element.36.band_ref, f32[5,128,128]{2,1,0:T(8,128)} %get-tuple-element.37.src_ref, ...), custom_call_target="tpu_custom_call" | custom-call | tf_op jit(solution)/shard_map/own/pallas_call | solution.py:440
  101.4 2.7 %collective-permute-start.8 = (bf16[4,96,1280]{2,1,0:T(8,128)(2,1)}, bf16[4,96,1280]{2,1,0:T(8,128)(2,1)S(1)}, u32[]{:S(2)}, u32[]{:S(2)}) collective-permute-start(bf16[4,96,1280]{2,1,0:T(8,128)(2,1)} %get-tuple-element.43), channel_id=1, source_target_pairs={{0,2},{1,3},{2,0},{3,1},{4,6},{5,7},{6,4},{7,5},{8,10},{9,11},{10,... | collective-permute-start | bytes 2949128 | tf_op jit(solution)/shard_map/ppermute | solution.py:602
  104.1 2.9 %tables.4.table_ref.hi_ref = bf16[3,1024,256]{2,1,0:T(8,128)(2,1)} custom-call(f32[8,2,32,128]{3,2,1,0:T(8,128)} %constant.24.clone.coarse_ref, f32[8,2,32,128]{3,2,1,0:T(8,128)} %constant.25.clone.fine_ref), custom_call_target="tpu_custom_call" | custom-call | tf_op jit(solution)/shard_map/tables/pallas_call | solution.py:70
  107.0 17.3 %outer.2 = (bf16[4,96,768]{2,1,0:T(8,128)(2,1)}, bf16[4,96,768]{2,1,0:T(8,128)(2,1)}, f32[6,2304,128]{2,1,0:T(8,128)}, f32[3,128,128]{2,1,0:T(8,128)}, f32[3,128,128]{2,1,0:T(8,128)}, /*index=5*/f32[3,128,128]{2,1,0:T(8,128)}) custom-call(s32[9]{0:T(128)} %pad_add_fusion.1.limits_ref, bf16[12,96,1024]{2,1,0:T(8,128)(2,1)} %normalize.2.near_ref, ...), custom_call_target="tpu_custom_call" | custom-call | tf_op jit(solution)/shard_map/outer/pallas_call | solution.py:406
  124.3 1.9 collective-permute-start.4
  126.2 3.4 %collective-permute-start.5 = (bf16[4,96,768]{2,1,0:T(8,128)(2,1)}, bf16[4,96,768]{2,1,0:T(8,128)(2,1)S(1)}, u32[]{:S(2)}, u32[]{:S(2)}) collective-permute-start(bf16[4,96,768]{2,1,0:T(8,128)(2,1)} %get-tuple-element.34), channel_id=1, source_target_pairs={{4,0},{8,4},{12,8},{16,12},{20,16},{24,20},{28,24},{32,28},{36,32}... | collective-permute-start | bytes 1769480 | tf_op jit(solution)/shard_map/ppermute | solution.py:598
  129.6 12.0 %collective-permute-done.4.below_ref = bf16[4,96,768]{2,1,0:T(8,128)(2,1)S(1)} collective-permute-done((bf16[4,96,768]{2,1,0:T(8,128)(2,1)}, bf16[4,96,768]{2,1,0:T(8,128)(2,1)S(1)}, u32[]{:S(2)}, u32[]{:S(2)}) %collective-permute-start.4) | collective-permute-done | bytes 589856 | tf_op jit(solution)/shard_map/ppermute | solution.py:598
  141.6 4.0 %collective-permute-done.5.above_ref = bf16[4,96,768]{2,1,0:T(8,128)(2,1)S(1)} collective-permute-done((bf16[4,96,768]{2,1,0:T(8,128)(2,1)}, bf16[4,96,768]{2,1,0:T(8,128)(2,1)S(1)}, u32[]{:S(2)}, u32[]{:S(2)}) %collective-permute-start.5) | collective-permute-done | bytes 589856 | tf_op jit(solution)/shard_map/ppermute | solution.py:598
  146.4 8.7 %own.2 = (f32[4,96,768]{2,1,0:T(8,128)}, bf16[4,96,768]{2,1,0:T(8,128)(2,1)}) custom-call(s32[8]{0:T(128)} %get-tuple-element.27.ordered_ref, s32[2]{0:T(128)} %pad_add_fusion.place_ref, f32[6,2304,128]{2,1,0:T(8,128)} %get-tuple-element.29.band_ref, f32[3,128,128]{2,1,0:T(8,128)} %get-tuple-element.30.src_ref, f32[3,128,128]{2,1,0:T(8,128)} %get-tuple-element.31.plus_ref, ...), custom_call_target="tpu_custom_call" | custom-call | tf_op jit(solution)/shard_map/own/pallas_call | solution.py:440
  155.3 1.0 copy-done.11
  156.2 1.5 add_convert_fusion.refs_0_
  158.5 12.7 %collective-permute-done.9 = bf16[4,96,768]{2,1,0:T(8,128)(2,1)S(1)} collective-permute-done((bf16[4,96,768]{2,1,0:T(8,128)(2,1)}, bf16[4,96,768]{2,1,0:T(8,128)(2,1)S(1)}, u32[]{:S(2)}, u32[]{:S(2)}) %collective-permute-start.9) | collective-permute-done | bytes 589856 | tf_op jit(solution)/shard_map/ppermute | solution.py:602
  171.3 1.5 collective-permute-start.10
  172.8 4.2 %tables.7.refs_3_ = bf16[5,1024,256]{2,1,0:T(8,128)(2,1)} custom-call(f32[8,2,32,128]{3,2,1,0:T(8,128)} %constant.24.clone.coarse_ref, f32[8,2,32,128]{3,2,1,0:T(8,128)} %constant.25.clone.fine_ref), custom_call_target="tpu_custom_call" | custom-call | tf_op jit(solution)/shard_map/tables/pallas_call | solution.py:70
  177.0 3.1 %tables.6.lo_ref = bf16[3,1024,256]{2,1,0:T(8,128)(2,1)} custom-call(f32[8,2,32,128]{3,2,1,0:T(8,128)} %constant.24.clone.coarse_ref, f32[8,2,32,128]{3,2,1,0:T(8,128)} %constant.25.clone.fine_ref), custom_call_target="tpu_custom_call" | custom-call | tf_op jit(solution)/shard_map/tables/pallas_call | solution.py:70
  180.1 0.9 copy-done.8
  181.0 7.8 %early.1 = (f32[384,1024]{1,0:T(8,128)}, f32[384,1024]{1,0:T(8,128)}) custom-call(s32[8]{0:T(128)} %get-tuple-element.27.ordered_ref, bf16[4,96,1280]{2,1,0:T(8,128)(2,1)} %copy-done.1, bf16[4,96,1280]{2,1,0:T(8,128)(2,1)} %copy-done.8, bf16[5,1024,256]{2,1,0:T(8,128)(2,1)} %tables.5.table_ref.refs_2_, bf16[5,1024,256]{2,1,0:T(8,128)(2,1)} %tables.7.refs_3_), custom_call_target="tpu_custom_call" | custom-call | tf_op jit(solution)/shard_map/early/pallas_call | solution.py:521
  189.7 7.4 %last.1 = f32[4,96,2048]{2,1,0:T(8,128)} custom-call(s32[8]{0:T(128)} %get-tuple-element.27.ordered_ref, bf16[4,96,768]{2,1,0:T(8,128)(2,1)} %copy-done.2, bf16[4,96,768]{2,1,0:T(8,128)(2,1)} %copy-done.14, bf16[3,1024,256]{2,1,0:T(8,128)(2,1)} %tables.4.table_ref.hi_ref, bf16[3,1024,256]{2,1,0:T(8,128)(2,1)} %tables.6.lo_ref, ...), custom_call_target="tpu_custom_call" | custom-call | tf_op jit(solution)/shard_map/last/pallas_call | solution.py:571
  (49 shorter events, 8.3 us)
Async XLA Ops:
  8.6 22.5 %collective-permute-start.3 = (bf16[12,96,1024]{2,1,0:T(8,128)(2,1)}, bf16[12,96,1024]{2,1,0:T(8,128)(2,1)S(1)}, u32[]{:S(2)}, u32[]{:S(2)}) collective-permute-start(bf16[12,96,1024]{2,1,0:T(8,128)(2,1)} %normalize.3), channel_id=1, source_target_pairs={{0,1},{1,0},{2,3},{3,2},{4,5},{5,4},{6,7},{7,6},{8,9},{9,8},{10,11... | collective-permute-start | bytes 7077896 | tf_op jit(solution)/shard_map/ppermute | solution.py:602
  13.2 1.6 collective-permute-start
  14.9 11.4 %copy-start.4 = (bf16[4,32,1024]{2,1,0:T(8,128)(2,1)}, bf16[4,32,1024]{2,1,0:T(8,128)(2,1)S(1)}, u32[]{:S(2)}) copy-start(bf16[4,32,1024]{2,1,0:T(8,128)(2,1)S(1)} %constant_dynamic-update-slice_fusion.own_src_ref) | copy-start | bytes 786436
  14.9 15.3 %collective-permute-start.2 = (bf16[4,32,1024]{2,1,0:T(8,128)(2,1)S(1)}, bf16[4,32,1024]{2,1,0:T(8,128)(2,1)S(1)}, u32[]{:S(2)}, u32[]{:S(2)}) collective-permute-start(bf16[4,32,1024]{2,1,0:T(8,128)(2,1)S(1)} %constant_dynamic-update-slice_fusion.own_src_ref), channel_id=1, source_target_pairs={{0,4},{4,8},{8,12},{12,16},{16,20},{20,24},{24,28},{28,32},{32,36}... | collective-permute-start | bytes 786440 | tf_op jit(solution)/shard_map/ppermute | solution.py:598
  17.7 12.7 %collective-permute-start.1 = (bf16[4,32,1024]{2,1,0:T(8,128)(2,1)S(1)}, bf16[4,32,1024]{2,1,0:T(8,128)(2,1)S(1)}, u32[]{:S(2)}, u32[]{:S(2)}) collective-permute-start(bf16[4,32,1024]{2,1,0:T(8,128)(2,1)S(1)} %constant_dynamic-update-slice_fusion.own_src_ref), channel_id=1, source_target_pairs={{4,0},{8,4},{12,8},{16,12},{20,16},{24,20},{28,24},{32,28},{36,32}... | collective-permute-start | bytes 786440 | tf_op jit(solution)/shard_map/ppermute | solution.py:598
  30.2 1.0 copy-start.6
  30.4 0.8 copy-start.7
  31.2 1.4 copy-start
  58.7 25.5 %collective-permute-start.6 = (bf16[4,96,1280]{2,1,0:T(8,128)(2,1)}, bf16[4,96,1280]{2,1,0:T(8,128)(2,1)S(1)}, u32[]{:S(2)}, u32[]{:S(2)}) collective-permute-start(bf16[4,96,1280]{2,1,0:T(8,128)(2,1)} %get-tuple-element.40), channel_id=1, source_target_pairs={{0,4},{4,8},{8,12},{12,16},{16,20},{20,24},{24,28},{28,32},{32,36}... | collective-permute-start | bytes 2949128 | tf_op jit(solution)/shard_map/ppermute | solution.py:598
  60.9 27.0 %collective-permute-start.7 = (bf16[4,96,1280]{2,1,0:T(8,128)(2,1)}, bf16[4,96,1280]{2,1,0:T(8,128)(2,1)S(1)}, u32[]{:S(2)}, u32[]{:S(2)}) collective-permute-start(bf16[4,96,1280]{2,1,0:T(8,128)(2,1)} %get-tuple-element.41), channel_id=1, source_target_pairs={{4,0},{8,4},{12,8},{16,12},{20,16},{24,20},{28,24},{32,28},{36,32}... | collective-permute-start | bytes 2949128 | tf_op jit(solution)/shard_map/ppermute | solution.py:598
  84.2 3.7 %copy-start.9 = (bf16[4,96,1280]{2,1,0:T(8,128)(2,1)}, bf16[4,96,1280]{2,1,0:T(8,128)(2,1)S(1)}, u32[]{:S(2)}) copy-start(bf16[4,96,1280]{2,1,0:T(8,128)(2,1)S(1)} %collective-permute-done.6.below_ref) | copy-start | bytes 2949124
  88.0 0.9 copy-start.10
  101.4 53.9 %collective-permute-start.8 = (bf16[4,96,1280]{2,1,0:T(8,128)(2,1)}, bf16[4,96,1280]{2,1,0:T(8,128)(2,1)S(1)}, u32[]{:S(2)}, u32[]{:S(2)}) collective-permute-start(bf16[4,96,1280]{2,1,0:T(8,128)(2,1)} %get-tuple-element.43), channel_id=1, source_target_pairs={{0,2},{1,3},{2,0},{3,1},{4,6},{5,7},{6,4},{7,5},{8,10},{9,11},{10,... | collective-permute-start | bytes 2949128 | tf_op jit(solution)/shard_map/ppermute | solution.py:602
  124.3 17.3 %collective-permute-start.4 = (bf16[4,96,768]{2,1,0:T(8,128)(2,1)}, bf16[4,96,768]{2,1,0:T(8,128)(2,1)S(1)}, u32[]{:S(2)}, u32[]{:S(2)}) collective-permute-start(bf16[4,96,768]{2,1,0:T(8,128)(2,1)} %get-tuple-element.33), channel_id=1, source_target_pairs={{0,4},{4,8},{8,12},{12,16},{16,20},{20,24},{24,28},{28,32},{32,36}... | collective-permute-start | bytes 1769480 | tf_op jit(solution)/shard_map/ppermute | solution.py:598
  126.2 19.4 %collective-permute-start.5 = (bf16[4,96,768]{2,1,0:T(8,128)(2,1)}, bf16[4,96,768]{2,1,0:T(8,128)(2,1)S(1)}, u32[]{:S(2)}, u32[]{:S(2)}) collective-permute-start(bf16[4,96,768]{2,1,0:T(8,128)(2,1)} %get-tuple-element.34), channel_id=1, source_target_pairs={{4,0},{8,4},{12,8},{16,12},{20,16},{24,20},{28,24},{32,28},{36,32}... | collective-permute-start | bytes 1769480 | tf_op jit(solution)/shard_map/ppermute | solution.py:598
  141.6 4.8 %copy-start.12 = (bf16[4,96,768]{2,1,0:T(8,128)(2,1)}, bf16[4,96,768]{2,1,0:T(8,128)(2,1)S(1)}, u32[]{:S(2)}) copy-start(bf16[4,96,768]{2,1,0:T(8,128)(2,1)S(1)} %collective-permute-done.4.below_ref) | copy-start | bytes 1769476
  145.6 0.8 copy-start.13
  146.4 9.8 %copy-start.3 = (f32[4,96,1280]{2,1,0:T(8,128)S(1)}, f32[4,96,1280]{2,1,0:T(8,128)}, u32[]{:S(2)}) copy-start(f32[4,96,1280]{2,1,0:T(8,128)} %get-tuple-element.42) | copy-start | bytes 5898244
  155.1 16.0 %collective-permute-start.9 = (bf16[4,96,768]{2,1,0:T(8,128)(2,1)}, bf16[4,96,768]{2,1,0:T(8,128)(2,1)S(1)}, u32[]{:S(2)}, u32[]{:S(2)}) collective-permute-start(bf16[4,96,768]{2,1,0:T(8,128)(2,1)} %get-tuple-element.45), channel_id=1, source_target_pairs={{0,2},{1,3},{2,0},{3,1},{4,6},{5,7},{6,4},{7,5},{8,10},{9,11},{10,... | collective-permute-start | bytes 1769480 | tf_op jit(solution)/shard_map/ppermute | solution.py:602
  155.3 1.0 copy-start.11
  156.2 15.0 %copy-start.5 = (f32[4,96,768]{2,1,0:T(8,128)S(1)}, f32[4,96,768]{2,1,0:T(8,128)}, u32[]{:S(2)}) copy-start(f32[4,96,768]{2,1,0:T(8,128)} %get-tuple-element.44) | copy-start | bytes 3538948
  157.7 19.3 %copy-start.1 = (bf16[4,96,1280]{2,1,0:T(8,128)(2,1)}, bf16[4,96,1280]{2,1,0:T(8,128)(2,1)S(1)}, u32[]{:S(2)}) copy-start(bf16[4,96,1280]{2,1,0:T(8,128)(2,1)S(1)} %add_convert_fusion.refs_0_) | copy-start | bytes 2949124
  157.7 22.4 %collective-permute-start.11 = (bf16[4,96,1280]{2,1,0:T(8,128)(2,1)S(1)}, bf16[4,96,1280]{2,1,0:T(8,128)(2,1)S(1)}, u32[]{:S(2)}, u32[]{:S(2)}) collective-permute-start(bf16[4,96,1280]{2,1,0:T(8,128)(2,1)S(1)} %add_convert_fusion.refs_0_), channel_id=1, source_target_pairs={{0,1},{1,0},{2,3},{3,2},{4,5},{5,4},{6,7},{7,6},{8,9},{9,8},{10,11... | collective-permute-start | bytes 2949128 | tf_op jit(solution)/shard_map/ppermute | solution.py:602
  171.3 8.7 %copy-start.2 = (bf16[4,96,768]{2,1,0:T(8,128)(2,1)}, bf16[4,96,768]{2,1,0:T(8,128)(2,1)S(1)}, u32[]{:S(2)}) copy-start(bf16[4,96,768]{2,1,0:T(8,128)(2,1)S(1)} %add_convert_fusion.1.mine_ref) | copy-start | bytes 1769476
  171.3 17.5 %collective-permute-start.10 = (bf16[4,96,768]{2,1,0:T(8,128)(2,1)S(1)}, bf16[4,96,768]{2,1,0:T(8,128)(2,1)S(1)}, u32[]{:S(2)}, u32[]{:S(2)}) collective-permute-start(bf16[4,96,768]{2,1,0:T(8,128)(2,1)S(1)} %add_convert_fusion.1.mine_ref), channel_id=1, source_target_pairs={{0,1},{1,0},{2,3},{3,2},{4,5},{5,4},{6,7},{7,6},{8,9},{9,8},{10,11... | collective-permute-start | bytes 1769480 | tf_op jit(solution)/shard_map/ppermute | solution.py:602
  180.1 1.0 copy-start.8
  188.9 0.8 copy-start.14

commit v3 on v2

--- a/solution.py
+++ b/solution.py
@@ -15,7 +15,7 @@
 LANES = 128
 GROUPS = SEG // LANES
 PAIR = 2 * LANES
-CHUNKS = ((0, 5), (5, 3))
+CHUNKS = ((0, 4), (4, 4))
 FOLD = 32
 UNROLL = 4
 TILE = 32
@@ -112,7 +112,7 @@
             spread_ref[:, column * LANES:(column + 1) * LANES] = jnp.where(row == column, 1.0, 0.0).astype(jnp.bfloat16)
 
     scale = scale_ref[...]
-    narrow = scale[:, :columns].astype(jnp.bfloat16)
+    narrow = scale.astype(jnp.bfloat16)
     for column in range(0, columns, 2):
         both = jnp.dot(
             narrow, spread_ref[:, column * LANES:(column + 2) * LANES], preferred_element_type=jnp.float32
@@ -128,7 +128,6 @@
         start = base + (n * pieces + piece) * windows + w
         return flat[pl.ds(start, TILE, stride=PITCH), :].astype(jnp.float32)
 
-    live = scale[:, windows * blocks:windows * blocks + 1]
     for w in range(windows):
         total = jnp.zeros((TILE, LANES), jnp.float32)
         for n in range(seg_count):
@@ -139,7 +138,7 @@
                 weight = wide_ref[column]
                 total = total + (one * one + two * two) * (weight * weight)
         energy = jnp.sum(total, axis=1, keepdims=True) * (1.0 / (seg_count * SEG))
-        factor = jnp.broadcast_to(live * lax.rsqrt(energy + 1e-06), (TILE, LANES))
+        factor = jnp.broadcast_to(lax.rsqrt(energy + 1e-06), (TILE, LANES))
         for n in range(seg_count):
             for pair in range(pairs):
                 column = w * blocks + n * pairs + pair
@@ -163,8 +162,8 @@
             out_specs=pl.BlockSpec((windows * seg_count, TILE, SEG), lambda i, h: (0, i, 0)),
             scratch_shapes=[
                 pltpu.VMEM((2, TILE, PITCH, LANES), jnp.int32),
-                pltpu.VMEM((scales.shape[1] - 1, (scales.shape[1] - 1) * LANES), jnp.bfloat16),
-                pltpu.VMEM((scales.shape[1] - 1, TILE, LANES), jnp.float32),
+                pltpu.VMEM((scales.shape[1], scales.shape[1] * LANES), jnp.bfloat16),
+                pltpu.VMEM((scales.shape[1], TILE, LANES), jnp.float32),
                 pltpu.SemaphoreType.DMA((2,)),
             ],
         ),
@@ -214,7 +213,6 @@
     for r in range(SOURCES):
         picked = jnp.sum(jnp.where(channel == order[r], scale_ref[...], 0.0), axis=0, keepdims=True)
         picked = jnp.broadcast_to(picked, (8, scale_ref.shape[1]))
-        live = jnp.sum(jnp.where(lane == windows * blocks, picked, 0.0), axis=1, keepdims=True)
         copies[r].wait()
         for w in range(windows):
             parts = []
@@ -228,7 +226,7 @@
                     total = total + part * part
                     parts.append(part)
             energy = jnp.sum(jnp.sum(total, axis=1, keepdims=True), axis=0, keepdims=True)
-            factor = live * lax.rsqrt(energy * (1.0 / (seg_count * SEG)) + 1e-06)
+            factor = lax.rsqrt(energy * (1.0 / (seg_count * SEG)) + 1e-06)
             for piece in range(pieces):
                 rows_ref[r, pl.ds(w * seg_count, seg_count), piece * LANES:(piece + 1) * LANES] = (
                     parts[piece] * factor
@@ -586,10 +584,12 @@
     )(ordered, *part, even, odd)
 
 
-def block_scale(exponents):
-    levels = jnp.arange(5, dtype=jnp.int32)
-    powers = jnp.exp2(levels.astype(jnp.float32))
-    return jnp.sum(jnp.where(exponents[..., None] == levels, powers, 0.0), axis=-1)
+def block_scale(exponents, alive):
+    scale = jnp.zeros(exponents.shape, jnp.float32)
+    for level in range(5):
+        hit = (exponents == level) & (alive != 0)[:, None, None]
+        scale = jnp.where(hit, float(2 ** level), scale)
+    return scale
 
 
 def passed_along(block, axis, distance):
@@ -611,8 +611,7 @@
 
     samples_rows = samples.reshape(channels, windows, length // LANES, LANES)
     samples_rows = samples_rows.transpose(0, 2, 1, 3).reshape(channels, windows * (length // LANES), LANES)
-    scales = block_scale(exponents).reshape(channels, -1)
-    scales = jnp.concatenate([scales, alive.astype(jnp.float32).reshape(channels, 1)], axis=1)
+    scales = block_scale(exponents, alive).reshape(channels, -1)
 
     own_src, ordered = source_rows(offsets, samples_rows, scales, seg_count, windows)
     mate_src = partner(own_src, 1)
@@ -651,7 +650,7 @@
         selected.append((kept, partner(moved, 2), moved))
     rests = []
     for first, count in CHUNKS:
-        later = lax.optimization_barrier((fine, selected[-1][2]))[0]
+        later = lax.optimization_barrier((fine, selected[0][2]))[0]
         rests.append(make_tables(first, count, coarse, later, True))
     parts = []
     for c in range(len(CHUNKS)):

time: 199 us -> 175 us (0.88)
  the two profiles are of different devices: /device:TPU:89 before, /device:TPU:97 now
where the time goes in v3:
time: 175 us; the launch traced here: 173 us
  Pallas kernels  105 us (60%)
  starting transfers between devices  43.4 us (25%)
  waiting for transfers between devices  14.1 us (8%)
  local copies, waits for them, and re-layouts  7.15 us (4%)
  other arithmetic  3.61 us (2%)
    pallas_call x2, Pallas kernels, outer_chunk(): pl.pallas_call(outer_kernel, grid_spec=pltpu.PrefetchScalarGridSpec(num_s...  38.2 us
    ppermute x6, starting transfers between devices, passed_along(): return lax.ppermute(block, axis, route)  24.9 us
    pallas_call x2, Pallas kernels, own_chunk(): pl.pallas_call(own_kernel, grid_spec=pltpu.PrefetchScalarGridSpec(num_sca...  20.9 us
    ppermute x6, starting transfers between devices, partner(): lax.ppermute(block, 'win', [(i, i ^ bit) for i in range(lax.axis_size('wi...  18.5 us
    pallas_call x4, Pallas kernels, make_tables(): pl.pallas_call(functools.partial(table_kernel, rest=rest), grid=(count,),...  14.7 us
    ppermute x6, waiting for transfers between devices, partner(): lax.ppermute(block, 'win', [(i, i ^ bit) for i in range(lax.axis_size('wi...  14.1 us
    pallas_call x2, Pallas kernels, normalize_half(): pl.pallas_call(functools.partial(normalize_kernel, seg_count=seg_count, w...  11.9 us
    pallas_call x1, Pallas kernels, last_inverse(): pl.pallas_call(functools.partial(last_kernel, first=first, scale=scale),...  8.06 us
  transfers between devices with their start and end apart: 12, of which 3 were waited for; matrix products, arithmetic and copies ran while one was open for 2% of the time, Pallas kernels for 41%

profile of v3, /device:TPU:97, one launch (start us, length us, event | category | flops | bytes accessed | tf_op | source)
XLA Modules:
  0.0 173.2 jit_solution(11046781499879401264)
XLA Ops:
  0.7 0.8 select_select_fusion
  2.3 6.0 %normalize.3 = bf16[12,96,1024]{2,1,0:T(8,128)(2,1)} custom-call(s32[1]{0:T(128)} %bitcast.9.half_ref, s32[192,96,128]{2,1,0:T(8,128)} %bitcast.10, f32[192,48]{1,0:T(8,128)} %copy.10.scale_ref), custom_call_target="tpu_custom_call" | custom-call | tf_op jit(solution)/shard_map/normalize/pallas_call | solution.py:153
  8.2 0.8 collective-permute-start.3
  9.0 3.8 %sources.1 = (bf16[4,16,1024]{2,1,0:T(8,128)(2,1)}, s32[8]{0:T(128)}) custom-call(s32[4]{0:T(128)} %offsets_ref.1, s32[192,96,128]{2,1,0:T(8,128)} %bitcast.11, f32[192,48]{1,0:T(8,128)} %copy.10.scale_ref), custom_call_target="tpu_custom_call" | custom-call | tf_op jit(solution)/shard_map/sources/pallas_call | solution.py:241
  12.9 0.9 constant_dynamic-update-slice_fusion.1
  14.5 3.2 %collective-permute-start.2 = (bf16[4,32,1024]{2,1,0:T(8,128)(2,1)S(1)}, bf16[4,32,1024]{2,1,0:T(8,128)(2,1)S(1)}, u32[]{:S(2)}, u32[]{:S(2)}) collective-permute-start(bf16[4,32,1024]{2,1,0:T(8,128)(2,1)S(1)} %constant_dynamic-update-slice_fusion.own_src_ref), channel_id=1, source_target_pairs={{0,4},{4,8},{8,12},{12,16},{16,20},{20,24},{24,28},{28,32},{32,36}... | collective-permute-start | bytes 786440 | tf_op jit(solution)/shard_map/ppermute | solution.py:598
  17.7 5.1 %collective-permute-start.1 = (bf16[4,32,1024]{2,1,0:T(8,128)(2,1)S(1)}, bf16[4,32,1024]{2,1,0:T(8,128)(2,1)S(1)}, u32[]{:S(2)}, u32[]{:S(2)}) collective-permute-start(bf16[4,32,1024]{2,1,0:T(8,128)(2,1)S(1)} %constant_dynamic-update-slice_fusion.own_src_ref), channel_id=1, source_target_pairs={{4,0},{8,4},{12,8},{16,12},{20,16},{24,20},{28,24},{32,28},{36,32}... | collective-permute-start | bytes 786440 | tf_op jit(solution)/shard_map/ppermute | solution.py:598
  22.8 5.9 %normalize.2.near_ref = bf16[12,96,1024]{2,1,0:T(8,128)(2,1)} custom-call(s32[1]{0:T(128)} %bitcast.6.half_ref, s32[192,96,128]{2,1,0:T(8,128)} %bitcast.12, f32[192,48]{1,0:T(8,128)} %copy.10.scale_ref), custom_call_target="tpu_custom_call" | custom-call | tf_op jit(solution)/shard_map/normalize/pallas_call | solution.py:153
  28.7 3.6 %tables.5.table_ref.refs_2_ = bf16[4,1024,256]{2,1,0:T(8,128)(2,1)} custom-call(f32[8,2,32,128]{3,2,1,0:T(8,128)} %constant.16.clone.coarse_ref, f32[8,2,32,128]{3,2,1,0:T(8,128)} %constant.42.clone.fine_ref), custom_call_target="tpu_custom_call" | custom-call | tf_op jit(solution)/shard_map/tables/pallas_call | solution.py:70
  33.3 1.4 copy-done
  34.7 19.1 %outer.3 = (bf16[4,96,1024]{2,1,0:T(8,128)(2,1)}, bf16[4,96,1024]{2,1,0:T(8,128)(2,1)}, f32[8,2304,128]{2,1,0:T(8,128)}, f32[4,128,128]{2,1,0:T(8,128)}, f32[4,128,128]{2,1,0:T(8,128)}, /*index=5*/f32[4,128,128]{2,1,0:T(8,128)}) custom-call(s32[9]{0:T(128)} %pad_add_fusion.1.limits_ref, bf16[12,96,1024]{2,1,0:T(8,128)(2,1)} %normalize.2.near_ref, ...), custom_call_target="tpu_custom_call" | custom-call | tf_op jit(solution)/shard_map/outer/pallas_call | solution.py:404
  53.9 1.9 %collective-permute-start.6 = (bf16[4,96,1024]{2,1,0:T(8,128)(2,1)}, bf16[4,96,1024]{2,1,0:T(8,128)(2,1)S(1)}, u32[]{:S(2)}, u32[]{:S(2)}) collective-permute-start(bf16[4,96,1024]{2,1,0:T(8,128)(2,1)} %get-tuple-element.40), channel_id=1, source_target_pairs={{0,4},{4,8},{8,12},{12,16},{16,20},{20,24},{24,28},{28,32},{32,36}... | collective-permute-start | bytes 2359304 | tf_op jit(solution)/shard_map/ppermute | solution.py:598
  55.8 6.4 %collective-permute-start.7 = (bf16[4,96,1024]{2,1,0:T(8,128)(2,1)}, bf16[4,96,1024]{2,1,0:T(8,128)(2,1)S(1)}, u32[]{:S(2)}, u32[]{:S(2)}) collective-permute-start(bf16[4,96,1024]{2,1,0:T(8,128)(2,1)} %get-tuple-element.41), channel_id=1, source_target_pairs={{4,0},{8,4},{12,8},{16,12},{20,16},{24,20},{28,24},{32,28},{36,32}... | collective-permute-start | bytes 2359304 | tf_op jit(solution)/shard_map/ppermute | solution.py:598
  62.2 3.6 %tables.4.table_ref.hi_ref = bf16[4,1024,256]{2,1,0:T(8,128)(2,1)} custom-call(f32[8,2,32,128]{3,2,1,0:T(8,128)} %constant.16.clone.coarse_ref, f32[8,2,32,128]{3,2,1,0:T(8,128)} %constant.42.clone.fine_ref), custom_call_target="tpu_custom_call" | custom-call | tf_op jit(solution)/shard_map/tables/pallas_call | solution.py:70
  65.8 19.1 %outer.2 = (bf16[4,96,1024]{2,1,0:T(8,128)(2,1)}, bf16[4,96,1024]{2,1,0:T(8,128)(2,1)}, f32[8,2304,128]{2,1,0:T(8,128)}, f32[4,128,128]{2,1,0:T(8,128)}, f32[4,128,128]{2,1,0:T(8,128)}, /*index=5*/f32[4,128,128]{2,1,0:T(8,128)}) custom-call(s32[9]{0:T(128)} %pad_add_fusion.1.limits_ref, bf16[12,96,1024]{2,1,0:T(8,128)(2,1)} %normalize.2.near_ref, ...), custom_call_target="tpu_custom_call" | custom-call | tf_op jit(solution)/shard_map/outer/pallas_call | solution.py:404
  84.9 1.9 %collective-permute-start.4 = (bf16[4,96,1024]{2,1,0:T(8,128)(2,1)}, bf16[4,96,1024]{2,1,0:T(8,128)(2,1)S(1)}, u32[]{:S(2)}, u32[]{:S(2)}) collective-permute-start(bf16[4,96,1024]{2,1,0:T(8,128)(2,1)} %get-tuple-element.33), channel_id=1, source_target_pairs={{0,4},{4,8},{8,12},{12,16},{16,20},{20,24},{24,28},{28,32},{32,36}... | collective-permute-start | bytes 2359304 | tf_op jit(solution)/shard_map/ppermute | solution.py:598
  86.8 6.4 %collective-permute-start.5 = (bf16[4,96,1024]{2,1,0:T(8,128)(2,1)}, bf16[4,96,1024]{2,1,0:T(8,128)(2,1)S(1)}, u32[]{:S(2)}, u32[]{:S(2)}) collective-permute-start(bf16[4,96,1024]{2,1,0:T(8,128)(2,1)} %get-tuple-element.34), channel_id=1, source_target_pairs={{4,0},{8,4},{12,8},{16,12},{20,16},{24,20},{28,24},{32,28},{36,32}... | collective-permute-start | bytes 2359304 | tf_op jit(solution)/shard_map/ppermute | solution.py:598
  93.8 0.9 copy-done.8
  94.9 10.4 %own.3 = (f32[4,96,1024]{2,1,0:T(8,128)}, bf16[4,96,1024]{2,1,0:T(8,128)(2,1)}) custom-call(s32[8]{0:T(128)} %get-tuple-element.27.ordered_ref, s32[2]{0:T(128)} %pad_add_fusion.place_ref, f32[8,2304,128]{2,1,0:T(8,128)} %get-tuple-element.36.band_ref, f32[4,128,128]{2,1,0:T(8,128)} %get-tuple-element.37.src_ref, f32[4,128,128]{2,1,0:T(8,128)} %get-tuple-element.38.plus_ref, ...), custom_call_target="tpu_custom_call" | custom-call | tf_op jit(solution)/shard_map/own/pallas_call | solution.py:438
  105.3 2.7 %collective-permute-start.8 = (bf16[4,96,1024]{2,1,0:T(8,128)(2,1)}, bf16[4,96,1024]{2,1,0:T(8,128)(2,1)S(1)}, u32[]{:S(2)}, u32[]{:S(2)}) collective-permute-start(bf16[4,96,1024]{2,1,0:T(8,128)(2,1)} %get-tuple-element.43), channel_id=1, source_target_pairs={{0,2},{1,3},{2,0},{3,1},{4,6},{5,7},{6,4},{7,5},{8,10},{9,11},{10,... | collective-permute-start | bytes 2359304 | tf_op jit(solution)/shard_map/ppermute | solution.py:602
  108.1 0.9 copy-done.11
  109.2 10.5 %own.2 = (f32[4,96,1024]{2,1,0:T(8,128)}, bf16[4,96,1024]{2,1,0:T(8,128)(2,1)}) custom-call(s32[8]{0:T(128)} %get-tuple-element.27.ordered_ref, s32[2]{0:T(128)} %pad_add_fusion.place_ref, f32[8,2304,128]{2,1,0:T(8,128)} %get-tuple-element.29.band_ref, f32[4,128,128]{2,1,0:T(8,128)} %get-tuple-element.30.src_ref, f32[4,128,128]{2,1,0:T(8,128)} %get-tuple-element.31.plus_ref, ...), custom_call_target="tpu_custom_call" | custom-call | tf_op jit(solution)/shard_map/own/pallas_call | solution.py:438
  120.4 6.2 %collective-permute-done.8 = bf16[4,96,1024]{2,1,0:T(8,128)(2,1)S(1)} collective-permute-done((bf16[4,96,1024]{2,1,0:T(8,128)(2,1)}, bf16[4,96,1024]{2,1,0:T(8,128)(2,1)S(1)}, u32[]{:S(2)}, u32[]{:S(2)}) %collective-permute-start.8) | collective-permute-done | bytes 786464 | tf_op jit(solution)/shard_map/ppermute | solution.py:602
  126.9 9.4 %collective-permute-start.11 = (bf16[4,96,1024]{2,1,0:T(8,128)(2,1)S(1)}, bf16[4,96,1024]{2,1,0:T(8,128)(2,1)S(1)}, u32[]{:S(2)}, u32[]{:S(2)}) collective-permute-start(bf16[4,96,1024]{2,1,0:T(8,128)(2,1)S(1)} %add_convert_fusion.1.refs_0_), channel_id=1, source_target_pairs={{0,1},{1,0},{2,3},{3,2},{4,5},{5,4},{6,7},{7,6},{8,9},{9,8},{10,11... | collective-permute-start | bytes 2359304 | tf_op jit(solution)/shard_map/ppermute | solution.py:602
  136.3 7.2 %collective-permute-done.9 = bf16[4,96,1024]{2,1,0:T(8,128)(2,1)S(1)} collective-permute-done((bf16[4,96,1024]{2,1,0:T(8,128)(2,1)}, bf16[4,96,1024]{2,1,0:T(8,128)(2,1)S(1)}, u32[]{:S(2)}, u32[]{:S(2)}) %collective-permute-start.9) | collective-permute-done | bytes 786464 | tf_op jit(solution)/shard_map/ppermute | solution.py:602
  143.8 4.9 %collective-permute-start.10 = (bf16[4,96,1024]{2,1,0:T(8,128)(2,1)S(1)}, bf16[4,96,1024]{2,1,0:T(8,128)(2,1)S(1)}, u32[]{:S(2)}, u32[]{:S(2)}) collective-permute-start(bf16[4,96,1024]{2,1,0:T(8,128)(2,1)S(1)} %add_convert_fusion.mine_ref), channel_id=1, source_target_pairs={{0,1},{1,0},{2,3},{3,2},{4,5},{5,4},{6,7},{7,6},{8,9},{9,8},{10,11... | collective-permute-start | bytes 2359304 | tf_op jit(solution)/shard_map/ppermute | solution.py:602
  148.7 3.7 %tables.7.refs_3_ = bf16[4,1024,256]{2,1,0:T(8,128)(2,1)} custom-call(f32[8,2,32,128]{3,2,1,0:T(8,128)} %constant.16.clone.coarse_ref, f32[8,2,32,128]{3,2,1,0:T(8,128)} %constant.42.clone.fine_ref), custom_call_target="tpu_custom_call" | custom-call | tf_op jit(solution)/shard_map/tables/pallas_call | solution.py:70
  152.4 3.7 %tables.6.lo_ref = bf16[4,1024,256]{2,1,0:T(8,128)(2,1)} custom-call(f32[8,2,32,128]{3,2,1,0:T(8,128)} %constant.16.clone.coarse_ref, f32[8,2,32,128]{3,2,1,0:T(8,128)} %constant.42.clone.fine_ref), custom_call_target="tpu_custom_call" | custom-call | tf_op jit(solution)/shard_map/tables/pallas_call | solution.py:70
  156.2 0.9 copy-done.13
  157.1 7.2 %early.1 = (f32[384,1024]{1,0:T(8,128)}, f32[384,1024]{1,0:T(8,128)}) custom-call(s32[8]{0:T(128)} %get-tuple-element.27.ordered_ref, bf16[4,96,1024]{2,1,0:T(8,128)(2,1)} %copy-done.2, bf16[4,96,1024]{2,1,0:T(8,128)(2,1)} %copy-done.13, bf16[4,1024,256]{2,1,0:T(8,128)(2,1)} %tables.5.table_ref.refs_2_, bf16[4,1024,256]{2,1,0:T(8,128)(2,1)} %tables.7.refs_3_), custom_call_target="tpu_custom_call" | custom-call | tf_op jit(solution)/shard_map/early/pallas_call | solution.py:519
  164.3 0.9 copy-done.12
  165.2 8.1 %last.1 = f32[4,96,2048]{2,1,0:T(8,128)} custom-call(s32[8]{0:T(128)} %get-tuple-element.27.ordered_ref, bf16[4,96,1024]{2,1,0:T(8,128)(2,1)} %copy-done.1, bf16[4,96,1024]{2,1,0:T(8,128)(2,1)} %copy-done.12, bf16[4,1024,256]{2,1,0:T(8,128)(2,1)} %tables.4.table_ref.hi_ref, bf16[4,1024,256]{2,1,0:T(8,128)(2,1)} %tables.6.lo_ref, ...), custom_call_target="tpu_custom_call" | custom-call | tf_op jit(solution)/shard_map/last/pallas_call | solution.py:569
  (44 shorter events, 5.4 us)
Async XLA Ops:
  8.2 25.1 %collective-permute-start.3 = (bf16[12,96,1024]{2,1,0:T(8,128)(2,1)}, bf16[12,96,1024]{2,1,0:T(8,128)(2,1)S(1)}, u32[]{:S(2)}, u32[]{:S(2)}) collective-permute-start(bf16[12,96,1024]{2,1,0:T(8,128)(2,1)} %normalize.3), channel_id=1, source_target_pairs={{0,1},{1,0},{2,3},{3,2},{4,5},{5,4},{6,7},{7,6},{8,9},{9,8},{10,11... | collective-permute-start | bytes 7077896 | tf_op jit(solution)/shard_map/ppermute | solution.py:602
  12.8 1.6 collective-permute-start
  14.5 14.2 %copy-start.3 = (bf16[4,32,1024]{2,1,0:T(8,128)(2,1)}, bf16[4,32,1024]{2,1,0:T(8,128)(2,1)S(1)}, u32[]{:S(2)}) copy-start(bf16[4,32,1024]{2,1,0:T(8,128)(2,1)S(1)} %constant_dynamic-update-slice_fusion.own_src_ref) | copy-start | bytes 786436
  14.5 17.8 %collective-permute-start.2 = (bf16[4,32,1024]{2,1,0:T(8,128)(2,1)S(1)}, bf16[4,32,1024]{2,1,0:T(8,128)(2,1)S(1)}, u32[]{:S(2)}, u32[]{:S(2)}) collective-permute-start(bf16[4,32,1024]{2,1,0:T(8,128)(2,1)S(1)} %constant_dynamic-update-slice_fusion.own_src_ref), channel_id=1, source_target_pairs={{0,4},{4,8},{8,12},{12,16},{16,20},{20,24},{24,28},{28,32},{32,36}... | collective-permute-start | bytes 786440 | tf_op jit(solution)/shard_map/ppermute | solution.py:598
  17.7 14.8 %collective-permute-start.1 = (bf16[4,32,1024]{2,1,0:T(8,128)(2,1)S(1)}, bf16[4,32,1024]{2,1,0:T(8,128)(2,1)S(1)}, u32[]{:S(2)}, u32[]{:S(2)}) collective-permute-start(bf16[4,32,1024]{2,1,0:T(8,128)(2,1)S(1)} %constant_dynamic-update-slice_fusion.own_src_ref), channel_id=1, source_target_pairs={{4,0},{8,4},{12,8},{16,12},{20,16},{24,20},{28,24},{32,28},{36,32}... | collective-permute-start | bytes 786440 | tf_op jit(solution)/shard_map/ppermute | solution.py:598
  32.3 1.0 copy-start.6
  32.5 0.8 copy-start.7
  33.3 1.4 copy-start
  53.9 39.9 %collective-permute-start.6 = (bf16[4,96,1024]{2,1,0:T(8,128)(2,1)}, bf16[4,96,1024]{2,1,0:T(8,128)(2,1)S(1)}, u32[]{:S(2)}, u32[]{:S(2)}) collective-permute-start(bf16[4,96,1024]{2,1,0:T(8,128)(2,1)} %get-tuple-element.40), channel_id=1, source_target_pairs={{0,4},{4,8},{8,12},{12,16},{16,20},{20,24},{24,28},{28,32},{32,36}... | collective-permute-start | bytes 2359304 | tf_op jit(solution)/shard_map/ppermute | solution.py:598
  55.8 38.0 %collective-permute-start.7 = (bf16[4,96,1024]{2,1,0:T(8,128)(2,1)}, bf16[4,96,1024]{2,1,0:T(8,128)(2,1)S(1)}, u32[]{:S(2)}, u32[]{:S(2)}) collective-permute-start(bf16[4,96,1024]{2,1,0:T(8,128)(2,1)} %get-tuple-element.41), channel_id=1, source_target_pairs={{4,0},{8,4},{12,8},{16,12},{20,16},{24,20},{28,24},{32,28},{36,32}... | collective-permute-start | bytes 2359304 | tf_op jit(solution)/shard_map/ppermute | solution.py:598
  84.9 23.2 %collective-permute-start.4 = (bf16[4,96,1024]{2,1,0:T(8,128)(2,1)}, bf16[4,96,1024]{2,1,0:T(8,128)(2,1)S(1)}, u32[]{:S(2)}, u32[]{:S(2)}) collective-permute-start(bf16[4,96,1024]{2,1,0:T(8,128)(2,1)} %get-tuple-element.33), channel_id=1, source_target_pairs={{0,4},{4,8},{8,12},{12,16},{16,20},{20,24},{24,28},{28,32},{32,36}... | collective-permute-start | bytes 2359304 | tf_op jit(solution)/shard_map/ppermute | solution.py:598
  86.8 21.3 %collective-permute-start.5 = (bf16[4,96,1024]{2,1,0:T(8,128)(2,1)}, bf16[4,96,1024]{2,1,0:T(8,128)(2,1)S(1)}, u32[]{:S(2)}, u32[]{:S(2)}) collective-permute-start(bf16[4,96,1024]{2,1,0:T(8,128)(2,1)} %get-tuple-element.34), channel_id=1, source_target_pairs={{4,0},{8,4},{12,8},{16,12},{20,16},{24,20},{28,24},{32,28},{36,32}... | collective-permute-start | bytes 2359304 | tf_op jit(solution)/shard_map/ppermute | solution.py:598
  93.8 0.9 copy-start.8
  93.8 1.1 copy-start.10
  105.3 21.3 %collective-permute-start.8 = (bf16[4,96,1024]{2,1,0:T(8,128)(2,1)}, bf16[4,96,1024]{2,1,0:T(8,128)(2,1)S(1)}, u32[]{:S(2)}, u32[]{:S(2)}) collective-permute-start(bf16[4,96,1024]{2,1,0:T(8,128)(2,1)} %get-tuple-element.43), channel_id=1, source_target_pairs={{0,2},{1,3},{2,0},{3,1},{4,6},{5,7},{6,4},{7,5},{8,10},{9,11},{10,... | collective-permute-start | bytes 2359304 | tf_op jit(solution)/shard_map/ppermute | solution.py:602
  108.1 1.1 copy-start.9
  108.1 0.9 copy-start.11
  109.2 17.4 %copy-start.4 = (f32[4,96,1024]{2,1,0:T(8,128)S(1)}, f32[4,96,1024]{2,1,0:T(8,128)}, u32[]{:S(2)}) copy-start(f32[4,96,1024]{2,1,0:T(8,128)} %get-tuple-element.42) | copy-start | bytes 4718596
  119.8 23.7 %copy-start.5 = (f32[4,96,1024]{2,1,0:T(8,128)S(1)}, f32[4,96,1024]{2,1,0:T(8,128)}, u32[]{:S(2)}) copy-start(f32[4,96,1024]{2,1,0:T(8,128)} %get-tuple-element.44) | copy-start | bytes 4718596
  119.8 23.7 %collective-permute-start.9 = (bf16[4,96,1024]{2,1,0:T(8,128)(2,1)}, bf16[4,96,1024]{2,1,0:T(8,128)(2,1)S(1)}, u32[]{:S(2)}, u32[]{:S(2)}) collective-permute-start(bf16[4,96,1024]{2,1,0:T(8,128)(2,1)} %get-tuple-element.45), channel_id=1, source_target_pairs={{0,2},{1,3},{2,0},{3,1},{4,6},{5,7},{6,4},{7,5},{8,10},{9,11},{10,... | collective-permute-start | bytes 2359304 | tf_op jit(solution)/shard_map/ppermute | solution.py:602
  126.9 25.5 %copy-start.2 = (bf16[4,96,1024]{2,1,0:T(8,128)(2,1)}, bf16[4,96,1024]{2,1,0:T(8,128)(2,1)S(1)}, u32[]{:S(2)}) copy-start(bf16[4,96,1024]{2,1,0:T(8,128)(2,1)S(1)} %add_convert_fusion.1.refs_0_) | copy-start | bytes 2359300
  126.9 29.3 %collective-permute-start.11 = (bf16[4,96,1024]{2,1,0:T(8,128)(2,1)S(1)}, bf16[4,96,1024]{2,1,0:T(8,128)(2,1)S(1)}, u32[]{:S(2)}, u32[]{:S(2)}) collective-permute-start(bf16[4,96,1024]{2,1,0:T(8,128)(2,1)S(1)} %add_convert_fusion.1.refs_0_), channel_id=1, source_target_pairs={{0,1},{1,0},{2,3},{3,2},{4,5},{5,4},{6,7},{7,6},{8,9},{9,8},{10,11... | collective-permute-start | bytes 2359304 | tf_op jit(solution)/shard_map/ppermute | solution.py:602
  143.7 12.4 %copy-start.1 = (bf16[4,96,1024]{2,1,0:T(8,128)(2,1)}, bf16[4,96,1024]{2,1,0:T(8,128)(2,1)S(1)}, u32[]{:S(2)}) copy-start(bf16[4,96,1024]{2,1,0:T(8,128)(2,1)S(1)} %add_convert_fusion.mine_ref) | copy-start | bytes 2359300
  143.8 20.5 %collective-permute-start.10 = (bf16[4,96,1024]{2,1,0:T(8,128)(2,1)S(1)}, bf16[4,96,1024]{2,1,0:T(8,128)(2,1)S(1)}, u32[]{:S(2)}, u32[]{:S(2)}) collective-permute-start(bf16[4,96,1024]{2,1,0:T(8,128)(2,1)S(1)} %add_convert_fusion.mine_ref), channel_id=1, source_target_pairs={{0,1},{1,0},{2,3},{3,2},{4,5},{5,4},{6,7},{7,6},{8,9},{9,8},{10,11... | collective-permute-start | bytes 2359304 | tf_op jit(solution)/shard_map/ppermute | solution.py:602
  156.2 0.9 copy-start.13
  164.3 0.9 copy-start.12

commit v4 on v3

--- a/solution.py
+++ b/solution.py
@@ -348,12 +348,13 @@
         sources = (src_ref, plus_ref, minus_ref)
         for first in (0, 2):
             pair = (first, first + 1)
-
-            @pl.when(channel + SUB > limits_ref[1 + first])
+            at = 1 + first // 2
+
+            @pl.when((channel + SUB > limits_ref[at]) & (channel < limits_ref[at + 2]))
             def _():
                 products(band_ref, sources, 0, pair, to_up, g, row)
 
-            @pl.when(channel < limits_ref[1 + SOURCES + first + 1])
+            @pl.when((channel + SUB > limits_ref[at + 4]) & (channel < limits_ref[at + 6]))
             def _():
                 products(band_ref, sources, per_side, pair, to_down, g, row)
 
@@ -362,7 +363,7 @@
     lax.fori_loop(0, groups * (TILE // SUB), tile, 0)
 
 
-def own_kernel(ordered_ref, place_ref, band_ref, src_ref, plus_ref, minus_ref, below_ref, above_ref,
+def own_kernel(ordered_ref, place_ref, band_ref, src_ref, plus_ref, minus_ref, first_ref, second_ref,
                kept_ref, passed_ref):
     groups = src_ref.shape[0]
     lower = place_ref[1] == 0
@@ -374,10 +375,11 @@
         channel = base + row + lax.broadcasted_iota(jnp.int32, (SUB, LANES), 0)
 
         def emit(j, rows, lanes, value):
-            below_source = channel < ordered_ref[j]
-            above = above_ref[j, rows, lanes].astype(jnp.float32)
-            other = jnp.where(below_source, above, below_ref[j, rows, lanes].astype(jnp.float32))
-            keep = jnp.where(below_source, 1, 0) == jnp.where(lower, 1, 0)
+            below_source = jnp.where(channel < ordered_ref[j], 1, 0)
+            first = first_ref[j, rows, lanes].astype(jnp.float32)
+            second = second_ref[j, rows, lanes].astype(jnp.float32)
+            other = jnp.where(below_source == place_ref[2], first, second)
+            keep = below_source == jnp.where(lower, 1, 0)
             kept_ref[j, rows, lanes] = jnp.where(keep, value, other)
             passed_ref[j, rows, lanes] = jnp.where(keep, other, value).astype(jnp.bfloat16)
 
@@ -429,7 +431,7 @@
     )(limits, near, far, own_src, above_src, below_src, table)
 
 
-def own_chunk(ordered, place, band, src, plus, minus, from_below, from_above):
+def own_chunk(ordered, place, band, src, plus, minus, from_first, from_second):
     groups, per_side, _ = src.shape
     steps = HALF // TILE
     width = groups * PAIR
@@ -455,7 +457,7 @@
             jax.ShapeDtypeStruct((SOURCES, HALF, width), jnp.bfloat16),
         ],
         name="own",
-    )(ordered, place, band, src, plus, minus, from_below, from_above)
+    )(ordered, place, band, src, plus, minus, from_first, from_second)
 
 
 def turned(ordered_ref, mine_ref, mate_ref, top_ref, halve):
@@ -592,10 +594,11 @@
     return scale
 
 
-def passed_along(block, axis, distance):
-    devices = range(lax.axis_size(axis))
-    route = [(i - distance, i) for i in devices if i - distance in devices]
-    return lax.ppermute(block, axis, route)
+def swapped(block, first):
+    route = []
+    for low in range(first, lax.axis_size("chan") - 1, 2):
+        route += [(low, low + 1), (low + 1, low)]
+    return lax.ppermute(block, "chan", route)
 
 
 def partner(block, bit):
@@ -616,8 +619,8 @@
     own_src, ordered = source_rows(offsets, samples_rows, scales, seg_count, windows)
     mate_src = partner(own_src, 1)
     own_src = jnp.concatenate([own_src, mate_src], axis=1)
-    above_src = passed_along(own_src, "chan", -1)
-    below_src = passed_along(own_src, "chan", 1)
+    first_src = swapped(own_src, 0)
+    second_src = swapped(own_src, 1)
 
     sent = normalize_half((1 - core).reshape(1), samples_rows, scales, seg_count, windows)
     far = partner(sent, 1)
@@ -625,12 +628,17 @@
     coarse, fine = (jnp.asarray(t) for t in small_tables())
 
     flag = windows * seg_count
-    above_off = above_src[:, flag, 0].astype(jnp.int32)
-    below_off = below_src[:, flag, 0].astype(jnp.int32)
-    limits = jnp.concatenate(
-        [(core * HALF).reshape(1), jnp.where(above_off == 0, channels, above_off - 1), below_off - 1]
-    ).astype(jnp.int32)
-    where_am_i = jnp.stack([core * HALF, upper_half]).astype(jnp.int32)
+    even = lax.axis_index("chan") % 2 == 0
+    bounds = []
+    for src, is_above in ((first_src, even), (second_src, jnp.logical_not(even))):
+        marks = src[:, flag, 0].astype(jnp.int32)
+        near_pair = marks.reshape(SOURCES // 2, 2)
+        present = near_pair[:, 0] > 0
+        low = jnp.where(is_above, jnp.where(present, near_pair[:, 0] - 1, channels), 0)
+        high = jnp.where(is_above, channels, near_pair[:, 1] - 1)
+        bounds += [low, high]
+    limits = jnp.concatenate([(core * HALF).reshape(1)] + bounds).astype(jnp.int32)
+    where_am_i = jnp.stack([core * HALF, upper_half, even.astype(jnp.int32)]).astype(jnp.int32)
     scale = 2.0 / float(2 * SEG * windows * lax.axis_size("win") * seg_count * SEG)
 
     tables = []
@@ -640,17 +648,17 @@
 
     kept_spectra = []
     for c in range(len(CHUNKS)):
-        to_above, to_below, *spectra = outer_chunk(limits, near, far, own_src, above_src, below_src, tables[c])
+        to_first, to_second, *spectra = outer_chunk(limits, near, far, own_src, first_src, second_src, tables[c])
         kept_spectra.append(spectra)
-        from_below = passed_along(to_above, "chan", 1)
-        from_above = passed_along(to_below, "chan", -1)
-        returned.append((from_below, from_above))
+        from_first = swapped(to_first, 0)
+        from_second = swapped(to_second, 1)
+        returned.append((from_first, from_second))
     for c in range(len(CHUNKS)):
         kept, moved = own_chunk(ordered, where_am_i, *kept_spectra[c], *returned[c])
         selected.append((kept, partner(moved, 2), moved))
     rests = []
-    for first, count in CHUNKS:
-        later = lax.optimization_barrier((fine, selected[0][2]))[0]
+    for c, (first, count) in enumerate(CHUNKS):
+        later = lax.optimization_barrier((fine, selected[c][2]))[0]
         rests.append(make_tables(first, count, coarse, later, True))
     parts = []
     for c in range(len(CHUNKS)):

time: 175 us -> 166 us (0.949)
  the two profiles are of different devices: /device:TPU:97 before, /device:TPU:65 now
where the time goes in v4:
time: 166 us; the launch traced here: 165 us
  Pallas kernels  101 us (61%)
  starting transfers between devices  33.6 us (20%)
  waiting for transfers between devices  18.6 us (11%)
  local copies, waits for them, and re-layouts  7.61 us (5%)
  other arithmetic  3.21 us (2%)
    pallas_call x2, Pallas kernels, outer_chunk(): pl.pallas_call(outer_kernel, grid_spec=pltpu.PrefetchScalarGridSpec(num_s...  34.9 us
    pallas_call x2, Pallas kernels, own_chunk(): pl.pallas_call(own_kernel, grid_spec=pltpu.PrefetchScalarGridSpec(num_sca...  20.9 us
    ppermute x6, starting transfers between devices, swapped(): return lax.ppermute(block, 'chan', route)  19.3 us
    ppermute x6, waiting for transfers between devices, partner(): lax.ppermute(block, 'win', [(i, i ^ bit) for i in range(lax.axis_size('wi...  18.3 us
    pallas_call x4, Pallas kernels, make_tables(): pl.pallas_call(functools.partial(table_kernel, rest=rest), grid=(count,),...  14.7 us
    ppermute x6, starting transfers between devices, partner(): lax.ppermute(block, 'win', [(i, i ^ bit) for i in range(lax.axis_size('wi...  14.3 us
    pallas_call x2, Pallas kernels, normalize_half(): pl.pallas_call(functools.partial(normalize_kernel, seg_count=seg_count, w...  11.8 us
    pallas_call x1, Pallas kernels, last_inverse(): pl.pallas_call(functools.partial(last_kernel, first=first, scale=scale),...  8.06 us
  transfers between devices with their start and end apart: 12, of which 4 were waited for; matrix products, arithmetic and copies ran while one was open for 2% of the time, Pallas kernels for 42%

profile of v4, /device:TPU:65, one launch (start us, length us, event | category | flops | bytes accessed | tf_op | source)
XLA Modules:
  0.0 164.7 jit_solution(3106925830456154015)
XLA Ops:
  0.7 0.8 select_select_fusion
  1.5 0.7 copy.10.scale_ref
  2.3 5.9 %normalize.3 = bf16[12,96,1024]{2,1,0:T(8,128)(2,1)} custom-call(s32[1]{0:T(128)} %bitcast.10.half_ref, s32[192,96,128]{2,1,0:T(8,128)} %bitcast.11, f32[192,48]{1,0:T(8,128)} %copy.10.scale_ref), custom_call_target="tpu_custom_call" | custom-call | tf_op jit(solution)/shard_map/normalize/pallas_call | solution.py:153
  8.2 0.8 collective-permute-start.3
  9.0 3.8 %sources.1 = (bf16[4,16,1024]{2,1,0:T(8,128)(2,1)}, s32[8]{0:T(128)}) custom-call(s32[4]{0:T(128)} %offsets_ref.1, s32[192,96,128]{2,1,0:T(8,128)} %bitcast.12, f32[192,48]{1,0:T(8,128)} %copy.10.scale_ref), custom_call_target="tpu_custom_call" | custom-call | tf_op jit(solution)/shard_map/sources/pallas_call | solution.py:241
  12.9 0.9 constant_dynamic-update-slice_fusion.1
  14.5 1.4 collective-permute-start.1
  15.8 4.3 %collective-permute-start.2 = (bf16[4,32,1024]{2,1,0:T(8,128)(2,1)S(1)}, bf16[4,32,1024]{2,1,0:T(8,128)(2,1)S(1)}, u32[]{:S(2)}, u32[]{:S(2)}) collective-permute-start(bf16[4,32,1024]{2,1,0:T(8,128)(2,1)S(1)} %constant_dynamic-update-slice_fusion.own_src_ref), channel_id=1, source_target_pairs={{4,8},{8,4},{12,16},{16,12},{20,24},{24,20},{28,32},{32,28},{36,40... | collective-permute-start | bytes 786440 | tf_op jit(solution)/shard_map/ppermute | solution.py:601
  20.1 5.9 %normalize.2.near_ref = bf16[12,96,1024]{2,1,0:T(8,128)(2,1)} custom-call(s32[1]{0:T(128)} %bitcast.7.half_ref, s32[192,96,128]{2,1,0:T(8,128)} %bitcast.13, f32[192,48]{1,0:T(8,128)} %copy.10.scale_ref), custom_call_target="tpu_custom_call" | custom-call | tf_op jit(solution)/shard_map/normalize/pallas_call | solution.py:153
  26.0 3.6 %tables.5.table_ref.refs_2_ = bf16[4,1024,256]{2,1,0:T(8,128)(2,1)} custom-call(f32[8,2,32,128]{3,2,1,0:T(8,128)} %constant.59.clone.coarse_ref, f32[8,2,32,128]{3,2,1,0:T(8,128)} %constant.60.clone.fine_ref), custom_call_target="tpu_custom_call" | custom-call | tf_op jit(solution)/shard_map/tables/pallas_call | solution.py:70
  31.0 1.4 copy-done
  32.4 17.4 %outer.3 = (bf16[4,96,1024]{2,1,0:T(8,128)(2,1)}, bf16[4,96,1024]{2,1,0:T(8,128)(2,1)}, f32[8,2304,128]{2,1,0:T(8,128)}, f32[4,128,128]{2,1,0:T(8,128)}, f32[4,128,128]{2,1,0:T(8,128)}, /*index=5*/f32[4,128,128]{2,1,0:T(8,128)}) custom-call(s32[9]{0:T(128)} %concatenate.7.limits_ref, bf16[12,96,1024]{2,1,0:T(8,128)(2,1)} %normalize.2.near_ref, ...), custom_call_target="tpu_custom_call" | custom-call | tf_op jit(solution)/shard_map/outer/pallas_call | solution.py:406
  49.9 7.1 %collective-permute-start.7 = (bf16[4,96,1024]{2,1,0:T(8,128)(2,1)}, bf16[4,96,1024]{2,1,0:T(8,128)(2,1)S(1)}, u32[]{:S(2)}, u32[]{:S(2)}) collective-permute-start(bf16[4,96,1024]{2,1,0:T(8,128)(2,1)} %get-tuple-element.42), channel_id=1, source_target_pairs={{4,8},{8,4},{12,16},{16,12},{20,24},{24,20},{28,32},{32,28},{36,40... | collective-permute-start | bytes 2359304 | tf_op jit(solution)/shard_map/ppermute | solution.py:601
  57.0 3.6 %tables.4.table_ref.hi_ref = bf16[4,1024,256]{2,1,0:T(8,128)(2,1)} custom-call(f32[8,2,32,128]{3,2,1,0:T(8,128)} %constant.59.clone.coarse_ref, f32[8,2,32,128]{3,2,1,0:T(8,128)} %constant.60.clone.fine_ref), custom_call_target="tpu_custom_call" | custom-call | tf_op jit(solution)/shard_map/tables/pallas_call | solution.py:70
  60.7 17.4 %outer.2 = (bf16[4,96,1024]{2,1,0:T(8,128)(2,1)}, bf16[4,96,1024]{2,1,0:T(8,128)(2,1)}, f32[8,2304,128]{2,1,0:T(8,128)}, f32[4,128,128]{2,1,0:T(8,128)}, f32[4,128,128]{2,1,0:T(8,128)}, /*index=5*/f32[4,128,128]{2,1,0:T(8,128)}) custom-call(s32[9]{0:T(128)} %concatenate.7.limits_ref, bf16[12,96,1024]{2,1,0:T(8,128)(2,1)} %normalize.2.near_ref, ...), custom_call_target="tpu_custom_call" | custom-call | tf_op jit(solution)/shard_map/outer/pallas_call | solution.py:406
  78.6 6.0 %collective-permute-start.5 = (bf16[4,96,1024]{2,1,0:T(8,128)(2,1)}, bf16[4,96,1024]{2,1,0:T(8,128)(2,1)S(1)}, u32[]{:S(2)}, u32[]{:S(2)}) collective-permute-start(bf16[4,96,1024]{2,1,0:T(8,128)(2,1)} %get-tuple-element.35), channel_id=1, source_target_pairs={{4,8},{8,4},{12,16},{16,12},{20,24},{24,20},{28,32},{32,28},{36,40... | collective-permute-start | bytes 2359304 | tf_op jit(solution)/shard_map/ppermute | solution.py:601
  85.2 0.9 copy-done.8
  86.4 10.4 %own.3 = (f32[4,96,1024]{2,1,0:T(8,128)}, bf16[4,96,1024]{2,1,0:T(8,128)(2,1)}) custom-call(s32[8]{0:T(128)} %get-tuple-element.28.ordered_ref, s32[3]{0:T(128)} %pad_add_fusion.place_ref, f32[8,2304,128]{2,1,0:T(8,128)} %get-tuple-element.37.band_ref, f32[4,128,128]{2,1,0:T(8,128)} %get-tuple-element.38.src_ref, f32[4,128,128]{2,1,0:T(8,128)} %get-tuple-element.39.plus_ref, ...), custom_call_target="tpu_custom_call" | custom-call | tf_op jit(solution)/shard_map/own/pallas_call | solution.py:440
  96.8 2.7 %collective-permute-start.8 = (bf16[4,96,1024]{2,1,0:T(8,128)(2,1)}, bf16[4,96,1024]{2,1,0:T(8,128)(2,1)S(1)}, u32[]{:S(2)}, u32[]{:S(2)}) collective-permute-start(bf16[4,96,1024]{2,1,0:T(8,128)(2,1)} %get-tuple-element.44), channel_id=1, source_target_pairs={{0,2},{1,3},{2,0},{3,1},{4,6},{5,7},{6,4},{7,5},{8,10},{9,11},{10,... | collective-permute-start | bytes 2359304 | tf_op jit(solution)/shard_map/ppermute | solution.py:605
  99.8 0.9 copy-done.11
  100.7 10.5 %own.2 = (f32[4,96,1024]{2,1,0:T(8,128)}, bf16[4,96,1024]{2,1,0:T(8,128)(2,1)}) custom-call(s32[8]{0:T(128)} %get-tuple-element.28.ordered_ref, s32[3]{0:T(128)} %pad_add_fusion.place_ref, f32[8,2304,128]{2,1,0:T(8,128)} %get-tuple-element.30.band_ref, f32[4,128,128]{2,1,0:T(8,128)} %get-tuple-element.31.src_ref, f32[4,128,128]{2,1,0:T(8,128)} %get-tuple-element.32.plus_ref, ...), custom_call_target="tpu_custom_call" | custom-call | tf_op jit(solution)/shard_map/own/pallas_call | solution.py:440
  111.2 3.0 %collective-permute-start.9 = (bf16[4,96,1024]{2,1,0:T(8,128)(2,1)}, bf16[4,96,1024]{2,1,0:T(8,128)(2,1)S(1)}, u32[]{:S(2)}, u32[]{:S(2)}) collective-permute-start(bf16[4,96,1024]{2,1,0:T(8,128)(2,1)} %get-tuple-element.46), channel_id=1, source_target_pairs={{0,2},{1,3},{2,0},{3,1},{4,6},{5,7},{6,4},{7,5},{8,10},{9,11},{10,... | collective-permute-start | bytes 2359304 | tf_op jit(solution)/shard_map/ppermute | solution.py:605
  114.2 6.1 %collective-permute-done.8 = bf16[4,96,1024]{2,1,0:T(8,128)(2,1)S(1)} collective-permute-done((bf16[4,96,1024]{2,1,0:T(8,128)(2,1)}, bf16[4,96,1024]{2,1,0:T(8,128)(2,1)S(1)}, u32[]{:S(2)}, u32[]{:S(2)}) %collective-permute-start.8) | collective-permute-done | bytes 786464 | tf_op jit(solution)/shard_map/ppermute | solution.py:605
  120.6 5.0 %collective-permute-start.11 = (bf16[4,96,1024]{2,1,0:T(8,128)(2,1)S(1)}, bf16[4,96,1024]{2,1,0:T(8,128)(2,1)S(1)}, u32[]{:S(2)}, u32[]{:S(2)}) collective-permute-start(bf16[4,96,1024]{2,1,0:T(8,128)(2,1)S(1)} %add_convert_fusion.1.refs_0_), channel_id=1, source_target_pairs={{0,1},{1,0},{2,3},{3,2},{4,5},{5,4},{6,7},{7,6},{8,9},{9,8},{10,11... | collective-permute-start | bytes 2359304 | tf_op jit(solution)/shard_map/ppermute | solution.py:605
  125.6 11.6 %collective-permute-done.9 = bf16[4,96,1024]{2,1,0:T(8,128)(2,1)S(1)} collective-permute-done((bf16[4,96,1024]{2,1,0:T(8,128)(2,1)}, bf16[4,96,1024]{2,1,0:T(8,128)(2,1)S(1)}, u32[]{:S(2)}, u32[]{:S(2)}) %collective-permute-start.9) | collective-permute-done | bytes 786464 | tf_op jit(solution)/shard_map/ppermute | solution.py:605
  137.4 2.7 %collective-permute-start.10 = (bf16[4,96,1024]{2,1,0:T(8,128)(2,1)S(1)}, bf16[4,96,1024]{2,1,0:T(8,128)(2,1)S(1)}, u32[]{:S(2)}, u32[]{:S(2)}) collective-permute-start(bf16[4,96,1024]{2,1,0:T(8,128)(2,1)S(1)} %add_convert_fusion.mine_ref), channel_id=1, source_target_pairs={{0,1},{1,0},{2,3},{3,2},{4,5},{5,4},{6,7},{7,6},{8,9},{9,8},{10,11... | collective-permute-start | bytes 2359304 | tf_op jit(solution)/shard_map/ppermute | solution.py:605
  140.1 3.7 %tables.7.refs_3_ = bf16[4,1024,256]{2,1,0:T(8,128)(2,1)} custom-call(f32[8,2,32,128]{3,2,1,0:T(8,128)} %constant.59.clone.coarse_ref, f32[8,2,32,128]{3,2,1,0:T(8,128)} %constant.60.clone.fine_ref), custom_call_target="tpu_custom_call" | custom-call | tf_op jit(solution)/shard_map/tables/pallas_call | solution.py:70
  143.8 3.8 %tables.6.lo_ref = bf16[4,1024,256]{2,1,0:T(8,128)(2,1)} custom-call(f32[8,2,32,128]{3,2,1,0:T(8,128)} %constant.59.clone.coarse_ref, f32[8,2,32,128]{3,2,1,0:T(8,128)} %constant.60.clone.fine_ref), custom_call_target="tpu_custom_call" | custom-call | tf_op jit(solution)/shard_map/tables/pallas_call | solution.py:70
  147.6 0.9 copy-done.13
  148.4 7.2 %early.1 = (f32[384,1024]{1,0:T(8,128)}, f32[384,1024]{1,0:T(8,128)}) custom-call(s32[8]{0:T(128)} %get-tuple-element.28.ordered_ref, bf16[4,96,1024]{2,1,0:T(8,128)(2,1)} %copy-done.2, bf16[4,96,1024]{2,1,0:T(8,128)(2,1)} %copy-done.13, bf16[4,1024,256]{2,1,0:T(8,128)(2,1)} %tables.5.table_ref.refs_2_, bf16[4,1024,256]{2,1,0:T(8,128)(2,1)} %tables.7.refs_3_), custom_call_target="tpu_custom_call" | custom-call | tf_op jit(solution)/shard_map/early/pallas_call | solution.py:521
  155.6 0.9 copy-done.12
  156.5 8.1 %last.1 = f32[4,96,2048]{2,1,0:T(8,128)} custom-call(s32[8]{0:T(128)} %get-tuple-element.28.ordered_ref, bf16[4,96,1024]{2,1,0:T(8,128)(2,1)} %copy-done.1, bf16[4,96,1024]{2,1,0:T(8,128)(2,1)} %copy-done.12, bf16[4,1024,256]{2,1,0:T(8,128)(2,1)} %tables.4.table_ref.hi_ref, bf16[4,1024,256]{2,1,0:T(8,128)(2,1)} %tables.6.lo_ref, ...), custom_call_target="tpu_custom_call" | custom-call | tf_op jit(solution)/shard_map/last/pallas_call | solution.py:571
  (47 shorter events, 5.1 us)
Async XLA Ops:
  8.2 22.8 %collective-permute-start.3 = (bf16[12,96,1024]{2,1,0:T(8,128)(2,1)}, bf16[12,96,1024]{2,1,0:T(8,128)(2,1)S(1)}, u32[]{:S(2)}, u32[]{:S(2)}) collective-permute-start(bf16[12,96,1024]{2,1,0:T(8,128)(2,1)} %normalize.3), channel_id=1, source_target_pairs={{0,1},{1,0},{2,3},{3,2},{4,5},{5,4},{6,7},{7,6},{8,9},{9,8},{10,11... | collective-permute-start | bytes 7077896 | tf_op jit(solution)/shard_map/ppermute | solution.py:605
  12.8 1.6 collective-permute-start
  14.4 11.6 %copy-start.3 = (bf16[4,32,1024]{2,1,0:T(8,128)(2,1)}, bf16[4,32,1024]{2,1,0:T(8,128)(2,1)S(1)}, u32[]{:S(2)}) copy-start(bf16[4,32,1024]{2,1,0:T(8,128)(2,1)S(1)} %constant_dynamic-update-slice_fusion.own_src_ref) | copy-start | bytes 786436
  14.5 15.2 %collective-permute-start.1 = (bf16[4,32,1024]{2,1,0:T(8,128)(2,1)S(1)}, bf16[4,32,1024]{2,1,0:T(8,128)(2,1)S(1)}, u32[]{:S(2)}, u32[]{:S(2)}) collective-permute-start(bf16[4,32,1024]{2,1,0:T(8,128)(2,1)S(1)} %constant_dynamic-update-slice_fusion.own_src_ref), channel_id=1, source_target_pairs={{0,4},{4,0},{8,12},{12,8},{16,20},{20,16},{24,28},{28,24},{32,36},... | collective-permute-start | bytes 786440 | tf_op jit(solution)/shard_map/ppermute | solution.py:601
  15.8 14.1 %collective-permute-start.2 = (bf16[4,32,1024]{2,1,0:T(8,128)(2,1)S(1)}, bf16[4,32,1024]{2,1,0:T(8,128)(2,1)S(1)}, u32[]{:S(2)}, u32[]{:S(2)}) collective-permute-start(bf16[4,32,1024]{2,1,0:T(8,128)(2,1)S(1)} %constant_dynamic-update-slice_fusion.own_src_ref), channel_id=1, source_target_pairs={{4,8},{8,4},{12,16},{16,12},{20,24},{24,20},{28,32},{32,28},{36,40... | collective-permute-start | bytes 786440 | tf_op jit(solution)/shard_map/ppermute | solution.py:601
  29.6 1.4 copy-start.6
  29.9 1.1 copy-start.7
  31.0 1.4 copy-start
  49.9 35.4 %collective-permute-start.6 = (bf16[4,96,1024]{2,1,0:T(8,128)(2,1)}, bf16[4,96,1024]{2,1,0:T(8,128)(2,1)S(1)}, u32[]{:S(2)}, u32[]{:S(2)}) collective-permute-start(bf16[4,96,1024]{2,1,0:T(8,128)(2,1)} %get-tuple-element.41), channel_id=1, source_target_pairs={{0,4},{4,0},{8,12},{12,8},{16,20},{20,16},{24,28},{28,24},{32,36},... | collective-permute-start | bytes 2359304 | tf_op jit(solution)/shard_map/ppermute | solution.py:601
  49.9 35.3 %collective-permute-start.7 = (bf16[4,96,1024]{2,1,0:T(8,128)(2,1)}, bf16[4,96,1024]{2,1,0:T(8,128)(2,1)S(1)}, u32[]{:S(2)}, u32[]{:S(2)}) collective-permute-start(bf16[4,96,1024]{2,1,0:T(8,128)(2,1)} %get-tuple-element.42), channel_id=1, source_target_pairs={{4,8},{8,4},{12,16},{16,12},{20,24},{24,20},{28,32},{32,28},{36,40... | collective-permute-start | bytes 2359304 | tf_op jit(solution)/shard_map/ppermute | solution.py:601
  78.1 21.4 %collective-permute-start.4 = (bf16[4,96,1024]{2,1,0:T(8,128)(2,1)}, bf16[4,96,1024]{2,1,0:T(8,128)(2,1)S(1)}, u32[]{:S(2)}, u32[]{:S(2)}) collective-permute-start(bf16[4,96,1024]{2,1,0:T(8,128)(2,1)} %get-tuple-element.34), channel_id=1, source_target_pairs={{0,4},{4,0},{8,12},{12,8},{16,20},{20,16},{24,28},{28,24},{32,36},... | collective-permute-start | bytes 2359304 | tf_op jit(solution)/shard_map/ppermute | solution.py:601
  78.6 21.2 %collective-permute-start.5 = (bf16[4,96,1024]{2,1,0:T(8,128)(2,1)}, bf16[4,96,1024]{2,1,0:T(8,128)(2,1)S(1)}, u32[]{:S(2)}, u32[]{:S(2)}) collective-permute-start(bf16[4,96,1024]{2,1,0:T(8,128)(2,1)} %get-tuple-element.35), channel_id=1, source_target_pairs={{4,8},{8,4},{12,16},{16,12},{20,24},{24,20},{28,32},{32,28},{36,40... | collective-permute-start | bytes 2359304 | tf_op jit(solution)/shard_map/ppermute | solution.py:601
  85.2 0.9 copy-start.8
  85.2 1.1 copy-start.10
  96.8 23.5 %collective-permute-start.8 = (bf16[4,96,1024]{2,1,0:T(8,128)(2,1)}, bf16[4,96,1024]{2,1,0:T(8,128)(2,1)S(1)}, u32[]{:S(2)}, u32[]{:S(2)}) collective-permute-start(bf16[4,96,1024]{2,1,0:T(8,128)(2,1)} %get-tuple-element.44), channel_id=1, source_target_pairs={{0,2},{1,3},{2,0},{3,1},{4,6},{5,7},{6,4},{7,5},{8,10},{9,11},{10,... | collective-permute-start | bytes 2359304 | tf_op jit(solution)/shard_map/ppermute | solution.py:605
  99.5 1.2 copy-start.9
  99.8 0.9 copy-start.11
  100.7 19.6 %copy-start.4 = (f32[4,96,1024]{2,1,0:T(8,128)S(1)}, f32[4,96,1024]{2,1,0:T(8,128)}, u32[]{:S(2)}) copy-start(f32[4,96,1024]{2,1,0:T(8,128)} %get-tuple-element.43) | copy-start | bytes 4718596
  111.2 26.0 %copy-start.5 = (f32[4,96,1024]{2,1,0:T(8,128)S(1)}, f32[4,96,1024]{2,1,0:T(8,128)}, u32[]{:S(2)}) copy-start(f32[4,96,1024]{2,1,0:T(8,128)} %get-tuple-element.45) | copy-start | bytes 4718596
  111.2 26.0 %collective-permute-start.9 = (bf16[4,96,1024]{2,1,0:T(8,128)(2,1)}, bf16[4,96,1024]{2,1,0:T(8,128)(2,1)S(1)}, u32[]{:S(2)}, u32[]{:S(2)}) collective-permute-start(bf16[4,96,1024]{2,1,0:T(8,128)(2,1)} %get-tuple-element.46), channel_id=1, source_target_pairs={{0,2},{1,3},{2,0},{3,1},{4,6},{5,7},{6,4},{7,5},{8,10},{9,11},{10,... | collective-permute-start | bytes 2359304 | tf_op jit(solution)/shard_map/ppermute | solution.py:605
  120.6 23.3 %copy-start.2 = (bf16[4,96,1024]{2,1,0:T(8,128)(2,1)}, bf16[4,96,1024]{2,1,0:T(8,128)(2,1)S(1)}, u32[]{:S(2)}) copy-start(bf16[4,96,1024]{2,1,0:T(8,128)(2,1)S(1)} %add_convert_fusion.1.refs_0_) | copy-start | bytes 2359300
  120.6 27.0 %collective-permute-start.11 = (bf16[4,96,1024]{2,1,0:T(8,128)(2,1)S(1)}, bf16[4,96,1024]{2,1,0:T(8,128)(2,1)S(1)}, u32[]{:S(2)}, u32[]{:S(2)}) collective-permute-start(bf16[4,96,1024]{2,1,0:T(8,128)(2,1)S(1)} %add_convert_fusion.1.refs_0_), channel_id=1, source_target_pairs={{0,1},{1,0},{2,3},{3,2},{4,5},{5,4},{6,7},{7,6},{8,9},{9,8},{10,11... | collective-permute-start | bytes 2359304 | tf_op jit(solution)/shard_map/ppermute | solution.py:605
  137.4 10.1 %copy-start.1 = (bf16[4,96,1024]{2,1,0:T(8,128)(2,1)}, bf16[4,96,1024]{2,1,0:T(8,128)(2,1)S(1)}, u32[]{:S(2)}) copy-start(bf16[4,96,1024]{2,1,0:T(8,128)(2,1)S(1)} %add_convert_fusion.mine_ref) | copy-start | bytes 2359300
  137.4 18.2 %collective-permute-start.10 = (bf16[4,96,1024]{2,1,0:T(8,128)(2,1)S(1)}, bf16[4,96,1024]{2,1,0:T(8,128)(2,1)S(1)}, u32[]{:S(2)}, u32[]{:S(2)}) collective-permute-start(bf16[4,96,1024]{2,1,0:T(8,128)(2,1)S(1)} %add_convert_fusion.mine_ref), channel_id=1, source_target_pairs={{0,1},{1,0},{2,3},{3,2},{4,5},{5,4},{6,7},{7,6},{8,9},{9,8},{10,11... | collective-permute-start | bytes 2359304 | tf_op jit(solution)/shard_map/ppermute | solution.py:605
  147.6 0.9 copy-start.13
  155.6 0.9 copy-start.12

commit v5 on v4

--- a/solution.py
+++ b/solution.py
@@ -15,7 +15,7 @@
 LANES = 128
 GROUPS = SEG // LANES
 PAIR = 2 * LANES
-CHUNKS = ((0, 4), (4, 4))
+CHUNKS = ((0, 5), (5, 3))
 FOLD = 32
 UNROLL = 4
 TILE = 32
@@ -657,8 +657,8 @@
         kept, moved = own_chunk(ordered, where_am_i, *kept_spectra[c], *returned[c])
         selected.append((kept, partner(moved, 2), moved))
     rests = []
-    for c, (first, count) in enumerate(CHUNKS):
-        later = lax.optimization_barrier((fine, selected[c][2]))[0]
+    for first, count in CHUNKS:
+        later = lax.optimization_barrier((fine, selected[-1][2]))[0]
         rests.append(make_tables(first, count, coarse, later, True))
     parts = []
     for c in range(len(CHUNKS)):

time: 166 us -> 194 us (1.17)
  the two profiles are of different devices: /device:TPU:65 before, /device:TPU:89 now
where the time goes in v5:
time: 194 us; the launch traced here: 192 us
  Pallas kernels  110 us (57%)
  waiting for transfers between devices  54.1 us (28%)
  starting transfers between devices  15.1 us (8%)
  local copies, waits for them, and re-layouts  8.44 us (4%)
  other arithmetic  4.36 us (2%)
    pallas_call x2, Pallas kernels, outer_chunk(): pl.pallas_call(outer_kernel, grid_spec=pltpu.PrefetchScalarGridSpec(num_s...  43.5 us
    ppermute x6, waiting for transfers between devices, swapped(): return lax.ppermute(block, 'chan', route)  41.9 us
    pallas_call x2, Pallas kernels, own_chunk(): pl.pallas_call(own_kernel, grid_spec=pltpu.PrefetchScalarGridSpec(num_sca...  21.2 us
    pallas_call x4, Pallas kernels, make_tables(): pl.pallas_call(functools.partial(table_kernel, rest=rest), grid=(count,),...  14.1 us
    ppermute x6, waiting for transfers between devices, partner(): lax.ppermute(block, 'win', [(i, i ^ bit) for i in range(lax.axis_size('wi...  12.2 us
    pallas_call x2, Pallas kernels, normalize_half(): pl.pallas_call(functools.partial(normalize_kernel, seg_count=seg_count, w...  11.9 us
    ppermute x6, starting transfers between devices, swapped(): return lax.ppermute(block, 'chan', route)  8.15 us
    pallas_call x1, Pallas kernels, early_inverse(): pl.pallas_call(functools.partial(early_kernel, firsts=firsts), grid_spec=...  7.84 us
  transfers between devices with their start and end apart: 12, of which 6 were waited for; matrix products, arithmetic and copies ran while one was open for 2% of the time, Pallas kernels for 30%

profile of v5, /device:TPU:89, one launch (start us, length us, event | category | flops | bytes accessed | tf_op | source)
XLA Modules:
  0.0 192.0 jit_solution(15188193715684701546)
XLA Ops:
  0.7 0.8 select_select_fusion
  2.3 5.9 %normalize.3 = bf16[12,96,1024]{2,1,0:T(8,128)(2,1)} custom-call(s32[1]{0:T(128)} %bitcast.10.half_ref, s32[192,96,128]{2,1,0:T(8,128)} %bitcast.11, f32[192,48]{1,0:T(8,128)} %copy.10.scale_ref), custom_call_target="tpu_custom_call" | custom-call | tf_op jit(solution)/shard_map/normalize/pallas_call | solution.py:153
  9.0 3.8 %sources.1 = (bf16[4,16,1024]{2,1,0:T(8,128)(2,1)}, s32[8]{0:T(128)}) custom-call(s32[4]{0:T(128)} %offsets_ref.1, s32[192,96,128]{2,1,0:T(8,128)} %bitcast.12, f32[192,48]{1,0:T(8,128)} %copy.10.scale_ref), custom_call_target="tpu_custom_call" | custom-call | tf_op jit(solution)/shard_map/sources/pallas_call | solution.py:241
  12.9 0.9 constant_dynamic-update-slice_fusion.1
  15.0 3.6 %collective-permute-start.2 = (bf16[4,32,1024]{2,1,0:T(8,128)(2,1)S(1)}, bf16[4,32,1024]{2,1,0:T(8,128)(2,1)S(1)}, u32[]{:S(2)}, u32[]{:S(2)}) collective-permute-start(bf16[4,32,1024]{2,1,0:T(8,128)(2,1)S(1)} %constant_dynamic-update-slice_fusion.own_src_ref), channel_id=1, source_target_pairs={{4,8},{8,4},{12,16},{16,12},{20,24},{24,20},{28,32},{32,28},{36,40... | collective-permute-start | bytes 786440 | tf_op jit(solution)/shard_map/ppermute | solution.py:601
  18.6 6.0 %normalize.2.near_ref = bf16[12,96,1024]{2,1,0:T(8,128)(2,1)} custom-call(s32[1]{0:T(128)} %bitcast.7.half_ref, s32[192,96,128]{2,1,0:T(8,128)} %bitcast.13, f32[192,48]{1,0:T(8,128)} %copy.10.scale_ref), custom_call_target="tpu_custom_call" | custom-call | tf_op jit(solution)/shard_map/normalize/pallas_call | solution.py:153
  24.6 3.9 %tables.5.table_ref.refs_2_ = bf16[5,1024,256]{2,1,0:T(8,128)(2,1)} custom-call(f32[8,2,32,128]{3,2,1,0:T(8,128)} %constant.59.clone.coarse_ref, f32[8,2,32,128]{3,2,1,0:T(8,128)} %constant.60.clone.fine_ref), custom_call_target="tpu_custom_call" | custom-call | tf_op jit(solution)/shard_map/tables/pallas_call | solution.py:70
  30.0 1.4 copy-done
  31.4 26.2 %outer.3 = (bf16[4,96,1280]{2,1,0:T(8,128)(2,1)}, bf16[4,96,1280]{2,1,0:T(8,128)(2,1)}, f32[10,2304,128]{2,1,0:T(8,128)}, f32[5,128,128]{2,1,0:T(8,128)}, f32[5,...) custom-call(s32[9]{0:T(128)} %concatenate.7.limits_ref, bf16[12,96,1024]{2,1,0:T(8,128)(2,1)} %normalize.2.near_ref, ...), custom_call_target="tpu_custom_call" | custom-call | tf_op jit(solution)/shard_map/outer/pallas_call | solution.py:406
  57.7 1.9 %collective-permute-start.7 = (bf16[4,96,1280]{2,1,0:T(8,128)(2,1)}, bf16[4,96,1280]{2,1,0:T(8,128)(2,1)S(1)}, u32[]{:S(2)}, u32[]{:S(2)}) collective-permute-start(bf16[4,96,1280]{2,1,0:T(8,128)(2,1)} %get-tuple-element.41), channel_id=1, source_target_pairs={{4,8},{8,4},{12,16},{16,12},{20,24},{24,20},{28,32},{32,28},{36,40... | collective-permute-start | bytes 2949128 | tf_op jit(solution)/shard_map/ppermute | solution.py:601
  60.3 21.0 %collective-permute-done.6.first_ref = bf16[4,96,1280]{2,1,0:T(8,128)(2,1)S(1)} collective-permute-done((bf16[4,96,1280]{2,1,0:T(8,128)(2,1)}, bf16[4,96,1280]{2,1,0:T(8,128)(2,1)S(1)}, u32[]{:S(2)}, u32[]{:S(2)}) %collective-permute-start.6) | collective-permute-done | bytes 983072 | tf_op jit(solution)/shard_map/ppermute | solution.py:601
  81.3 3.7 %collective-permute-done.7.second_ref = bf16[4,96,1280]{2,1,0:T(8,128)(2,1)S(1)} collective-permute-done((bf16[4,96,1280]{2,1,0:T(8,128)(2,1)}, bf16[4,96,1280]{2,1,0:T(8,128)(2,1)S(1)}, u32[]{:S(2)}, u32[]{:S(2)}) %collective-permute-start.7) | collective-permute-done | bytes 983072 | tf_op jit(solution)/shard_map/ppermute | solution.py:601
  85.1 1.0 copy-done.10
  86.0 12.5 %own.3 = (f32[4,96,1280]{2,1,0:T(8,128)}, bf16[4,96,1280]{2,1,0:T(8,128)(2,1)}) custom-call(s32[8]{0:T(128)} %get-tuple-element.27.ordered_ref, s32[3]{0:T(128)} %pad_add_fusion.place_ref, f32[10,2304,128]{2,1,0:T(8,128)} %get-tuple-element.36.band_ref, f32[5,128,128]{2,1,0:T(8,128)} %get-tuple-element.37.src_ref, ...), custom_call_target="tpu_custom_call" | custom-call | tf_op jit(solution)/shard_map/own/pallas_call | solution.py:440
  98.5 2.6 %collective-permute-start.8 = (bf16[4,96,1280]{2,1,0:T(8,128)(2,1)}, bf16[4,96,1280]{2,1,0:T(8,128)(2,1)S(1)}, u32[]{:S(2)}, u32[]{:S(2)}) collective-permute-start(bf16[4,96,1280]{2,1,0:T(8,128)(2,1)} %get-tuple-element.43), channel_id=1, source_target_pairs={{0,2},{1,3},{2,0},{3,1},{4,6},{5,7},{6,4},{7,5},{8,10},{9,11},{10,... | collective-permute-start | bytes 2949128 | tf_op jit(solution)/shard_map/ppermute | solution.py:605
  101.0 2.9 %tables.4.table_ref.hi_ref = bf16[3,1024,256]{2,1,0:T(8,128)(2,1)} custom-call(f32[8,2,32,128]{3,2,1,0:T(8,128)} %constant.59.clone.coarse_ref, f32[8,2,32,128]{3,2,1,0:T(8,128)} %constant.60.clone.fine_ref), custom_call_target="tpu_custom_call" | custom-call | tf_op jit(solution)/shard_map/tables/pallas_call | solution.py:70
  104.0 17.3 %outer.2 = (bf16[4,96,768]{2,1,0:T(8,128)(2,1)}, bf16[4,96,768]{2,1,0:T(8,128)(2,1)}, f32[6,2304,128]{2,1,0:T(8,128)}, f32[3,128,128]{2,1,0:T(8,128)}, f32[3,128,128]{2,1,0:T(8,128)}, /*index=5*/f32[3,128,128]{2,1,0:T(8,128)}) custom-call(s32[9]{0:T(128)} %concatenate.7.limits_ref, bf16[12,96,1024]{2,1,0:T(8,128)(2,1)} %normalize.2.near_ref, ...), custom_call_target="tpu_custom_call" | custom-call | tf_op jit(solution)/shard_map/outer/pallas_call | solution.py:406
  121.3 1.9 %collective-permute-start.5 = (bf16[4,96,768]{2,1,0:T(8,128)(2,1)}, bf16[4,96,768]{2,1,0:T(8,128)(2,1)S(1)}, u32[]{:S(2)}, u32[]{:S(2)}) collective-permute-start(bf16[4,96,768]{2,1,0:T(8,128)(2,1)} %get-tuple-element.34), channel_id=1, source_target_pairs={{4,8},{8,4},{12,16},{16,12},{20,24},{24,20},{28,32},{32,28},{36,40... | collective-permute-start | bytes 1769480 | tf_op jit(solution)/shard_map/ppermute | solution.py:601
  123.3 13.4 %collective-permute-done.4.first_ref = bf16[4,96,768]{2,1,0:T(8,128)(2,1)S(1)} collective-permute-done((bf16[4,96,768]{2,1,0:T(8,128)(2,1)}, bf16[4,96,768]{2,1,0:T(8,128)(2,1)S(1)}, u32[]{:S(2)}, u32[]{:S(2)}) %collective-permute-start.4) | collective-permute-done | bytes 589856 | tf_op jit(solution)/shard_map/ppermute | solution.py:601
  136.7 3.7 %collective-permute-done.5.second_ref = bf16[4,96,768]{2,1,0:T(8,128)(2,1)S(1)} collective-permute-done((bf16[4,96,768]{2,1,0:T(8,128)(2,1)}, bf16[4,96,768]{2,1,0:T(8,128)(2,1)S(1)}, u32[]{:S(2)}, u32[]{:S(2)}) %collective-permute-start.5) | collective-permute-done | bytes 589856 | tf_op jit(solution)/shard_map/ppermute | solution.py:601
  140.4 0.8 copy-done.13
  141.2 8.7 %own.2 = (f32[4,96,768]{2,1,0:T(8,128)}, bf16[4,96,768]{2,1,0:T(8,128)(2,1)}) custom-call(s32[8]{0:T(128)} %get-tuple-element.27.ordered_ref, s32[3]{0:T(128)} %pad_add_fusion.place_ref, f32[6,2304,128]{2,1,0:T(8,128)} %get-tuple-element.29.band_ref, f32[3,128,128]{2,1,0:T(8,128)} %get-tuple-element.30.src_ref, f32[3,128,128]{2,1,0:T(8,128)} %get-tuple-element.31.plus_ref, ...), custom_call_target="tpu_custom_call" | custom-call | tf_op jit(solution)/shard_map/own/pallas_call | solution.py:440
  150.3 1.0 copy-done.11
  151.2 1.5 add_convert_fusion.refs_0_
  152.7 1.4 collective-permute-start.11
  154.1 11.6 %collective-permute-done.9 = bf16[4,96,768]{2,1,0:T(8,128)(2,1)S(1)} collective-permute-done((bf16[4,96,768]{2,1,0:T(8,128)(2,1)}, bf16[4,96,768]{2,1,0:T(8,128)(2,1)S(1)}, u32[]{:S(2)}, u32[]{:S(2)}) %collective-permute-start.9) | collective-permute-done | bytes 589856 | tf_op jit(solution)/shard_map/ppermute | solution.py:605
  165.8 1.8 collective-permute-start.10
  167.7 4.2 %tables.7.refs_3_ = bf16[5,1024,256]{2,1,0:T(8,128)(2,1)} custom-call(f32[8,2,32,128]{3,2,1,0:T(8,128)} %constant.59.clone.coarse_ref, f32[8,2,32,128]{3,2,1,0:T(8,128)} %constant.60.clone.fine_ref), custom_call_target="tpu_custom_call" | custom-call | tf_op jit(solution)/shard_map/tables/pallas_call | solution.py:70
  171.9 3.1 %tables.6.lo_ref = bf16[3,1024,256]{2,1,0:T(8,128)(2,1)} custom-call(f32[8,2,32,128]{3,2,1,0:T(8,128)} %constant.59.clone.coarse_ref, f32[8,2,32,128]{3,2,1,0:T(8,128)} %constant.60.clone.fine_ref), custom_call_target="tpu_custom_call" | custom-call | tf_op jit(solution)/shard_map/tables/pallas_call | solution.py:70
  175.0 0.9 copy-done.8
  175.9 7.8 %early.1 = (f32[384,1024]{1,0:T(8,128)}, f32[384,1024]{1,0:T(8,128)}) custom-call(s32[8]{0:T(128)} %get-tuple-element.27.ordered_ref, bf16[4,96,1280]{2,1,0:T(8,128)(2,1)} %copy-done.1, bf16[4,96,1280]{2,1,0:T(8,128)(2,1)} %copy-done.8, bf16[5,1024,256]{2,1,0:T(8,128)(2,1)} %tables.5.table_ref.refs_2_, bf16[5,1024,256]{2,1,0:T(8,128)(2,1)} %tables.7.refs_3_), custom_call_target="tpu_custom_call" | custom-call | tf_op jit(solution)/shard_map/early/pallas_call | solution.py:521
  184.6 7.4 %last.1 = f32[4,96,2048]{2,1,0:T(8,128)} custom-call(s32[8]{0:T(128)} %get-tuple-element.27.ordered_ref, bf16[4,96,768]{2,1,0:T(8,128)(2,1)} %copy-done.2, bf16[4,96,768]{2,1,0:T(8,128)(2,1)} %copy-done.14, bf16[3,1024,256]{2,1,0:T(8,128)(2,1)} %tables.4.table_ref.hi_ref, bf16[3,1024,256]{2,1,0:T(8,128)(2,1)} %tables.6.lo_ref, ...), custom_call_target="tpu_custom_call" | custom-call | tf_op jit(solution)/shard_map/last/pallas_call | solution.py:571
  (49 shorter events, 7.0 us)
Async XLA Ops:
  8.2 21.8 %collective-permute-start.3 = (bf16[12,96,1024]{2,1,0:T(8,128)(2,1)}, bf16[12,96,1024]{2,1,0:T(8,128)(2,1)S(1)}, u32[]{:S(2)}, u32[]{:S(2)}) collective-permute-start(bf16[12,96,1024]{2,1,0:T(8,128)(2,1)} %normalize.3), channel_id=1, source_target_pairs={{0,1},{1,0},{2,3},{3,2},{4,5},{5,4},{6,7},{7,6},{8,9},{9,8},{10,11... | collective-permute-start | bytes 7077896 | tf_op jit(solution)/shard_map/ppermute | solution.py:605
  12.8 1.6 collective-permute-start
  14.5 10.1 %copy-start.4 = (bf16[4,32,1024]{2,1,0:T(8,128)(2,1)}, bf16[4,32,1024]{2,1,0:T(8,128)(2,1)S(1)}, u32[]{:S(2)}) copy-start(bf16[4,32,1024]{2,1,0:T(8,128)(2,1)S(1)} %constant_dynamic-update-slice_fusion.own_src_ref) | copy-start | bytes 786436
  14.5 14.1 %collective-permute-start.1 = (bf16[4,32,1024]{2,1,0:T(8,128)(2,1)S(1)}, bf16[4,32,1024]{2,1,0:T(8,128)(2,1)S(1)}, u32[]{:S(2)}, u32[]{:S(2)}) collective-permute-start(bf16[4,32,1024]{2,1,0:T(8,128)(2,1)S(1)} %constant_dynamic-update-slice_fusion.own_src_ref), channel_id=1, source_target_pairs={{0,4},{4,0},{8,12},{12,8},{16,20},{20,16},{24,28},{28,24},{32,36},... | collective-permute-start | bytes 786440 | tf_op jit(solution)/shard_map/ppermute | solution.py:601
  15.0 13.8 %collective-permute-start.2 = (bf16[4,32,1024]{2,1,0:T(8,128)(2,1)S(1)}, bf16[4,32,1024]{2,1,0:T(8,128)(2,1)S(1)}, u32[]{:S(2)}, u32[]{:S(2)}) collective-permute-start(bf16[4,32,1024]{2,1,0:T(8,128)(2,1)S(1)} %constant_dynamic-update-slice_fusion.own_src_ref), channel_id=1, source_target_pairs={{4,8},{8,4},{12,16},{16,12},{20,24},{24,20},{28,32},{32,28},{36,40... | collective-permute-start | bytes 786440 | tf_op jit(solution)/shard_map/ppermute | solution.py:601
  28.5 1.4 copy-start.6
  28.8 1.2 copy-start.7
  30.0 1.4 copy-start
  57.6 23.7 %collective-permute-start.6 = (bf16[4,96,1280]{2,1,0:T(8,128)(2,1)}, bf16[4,96,1280]{2,1,0:T(8,128)(2,1)S(1)}, u32[]{:S(2)}, u32[]{:S(2)}) collective-permute-start(bf16[4,96,1280]{2,1,0:T(8,128)(2,1)} %get-tuple-element.40), channel_id=1, source_target_pairs={{0,4},{4,0},{8,12},{12,8},{16,20},{20,16},{24,28},{28,24},{32,36},... | collective-permute-start | bytes 2949128 | tf_op jit(solution)/shard_map/ppermute | solution.py:601
  57.7 27.3 %collective-permute-start.7 = (bf16[4,96,1280]{2,1,0:T(8,128)(2,1)}, bf16[4,96,1280]{2,1,0:T(8,128)(2,1)S(1)}, u32[]{:S(2)}, u32[]{:S(2)}) collective-permute-start(bf16[4,96,1280]{2,1,0:T(8,128)(2,1)} %get-tuple-element.41), channel_id=1, source_target_pairs={{4,8},{8,4},{12,16},{16,12},{20,24},{24,20},{28,32},{32,28},{36,40... | collective-permute-start | bytes 2949128 | tf_op jit(solution)/shard_map/ppermute | solution.py:601
  81.3 3.7 %copy-start.9 = (bf16[4,96,1280]{2,1,0:T(8,128)(2,1)}, bf16[4,96,1280]{2,1,0:T(8,128)(2,1)S(1)}, u32[]{:S(2)}) copy-start(bf16[4,96,1280]{2,1,0:T(8,128)(2,1)S(1)} %collective-permute-done.6.first_ref) | copy-start | bytes 2949124
  85.0 1.0 copy-start.10
  98.5 51.8 %collective-permute-start.8 = (bf16[4,96,1280]{2,1,0:T(8,128)(2,1)}, bf16[4,96,1280]{2,1,0:T(8,128)(2,1)S(1)}, u32[]{:S(2)}, u32[]{:S(2)}) collective-permute-start(bf16[4,96,1280]{2,1,0:T(8,128)(2,1)} %get-tuple-element.43), channel_id=1, source_target_pairs={{0,2},{1,3},{2,0},{3,1},{4,6},{5,7},{6,4},{7,5},{8,10},{9,11},{10,... | collective-permute-start | bytes 2949128 | tf_op jit(solution)/shard_map/ppermute | solution.py:605
  121.3 15.4 %collective-permute-start.4 = (bf16[4,96,768]{2,1,0:T(8,128)(2,1)}, bf16[4,96,768]{2,1,0:T(8,128)(2,1)S(1)}, u32[]{:S(2)}, u32[]{:S(2)}) collective-permute-start(bf16[4,96,768]{2,1,0:T(8,128)(2,1)} %get-tuple-element.33), channel_id=1, source_target_pairs={{0,4},{4,0},{8,12},{12,8},{16,20},{20,16},{24,28},{28,24},{32,36},... | collective-permute-start | bytes 1769480 | tf_op jit(solution)/shard_map/ppermute | solution.py:601
  121.3 19.1 %collective-permute-start.5 = (bf16[4,96,768]{2,1,0:T(8,128)(2,1)}, bf16[4,96,768]{2,1,0:T(8,128)(2,1)S(1)}, u32[]{:S(2)}, u32[]{:S(2)}) collective-permute-start(bf16[4,96,768]{2,1,0:T(8,128)(2,1)} %get-tuple-element.34), channel_id=1, source_target_pairs={{4,8},{8,4},{12,16},{16,12},{20,24},{24,20},{28,32},{32,28},{36,40... | collective-permute-start | bytes 1769480 | tf_op jit(solution)/shard_map/ppermute | solution.py:601
  136.7 4.6 %copy-start.12 = (bf16[4,96,768]{2,1,0:T(8,128)(2,1)}, bf16[4,96,768]{2,1,0:T(8,128)(2,1)S(1)}, u32[]{:S(2)}) copy-start(bf16[4,96,768]{2,1,0:T(8,128)(2,1)S(1)} %collective-permute-done.4.first_ref) | copy-start | bytes 1769476
  140.4 0.8 copy-start.13
  141.2 10.0 %copy-start.3 = (f32[4,96,1280]{2,1,0:T(8,128)S(1)}, f32[4,96,1280]{2,1,0:T(8,128)}, u32[]{:S(2)}) copy-start(f32[4,96,1280]{2,1,0:T(8,128)} %get-tuple-element.42) | copy-start | bytes 5898244
  150.0 15.7 %collective-permute-start.9 = (bf16[4,96,768]{2,1,0:T(8,128)(2,1)}, bf16[4,96,768]{2,1,0:T(8,128)(2,1)S(1)}, u32[]{:S(2)}, u32[]{:S(2)}) collective-permute-start(bf16[4,96,768]{2,1,0:T(8,128)(2,1)} %get-tuple-element.45), channel_id=1, source_target_pairs={{0,2},{1,3},{2,0},{3,1},{4,6},{5,7},{6,4},{7,5},{8,10},{9,11},{10,... | collective-permute-start | bytes 1769480 | tf_op jit(solution)/shard_map/ppermute | solution.py:605
  150.3 1.0 copy-start.11
  151.2 14.5 %copy-start.5 = (f32[4,96,768]{2,1,0:T(8,128)S(1)}, f32[4,96,768]{2,1,0:T(8,128)}, u32[]{:S(2)}) copy-start(f32[4,96,768]{2,1,0:T(8,128)} %get-tuple-element.44) | copy-start | bytes 3538948
  152.7 19.1 %copy-start.1 = (bf16[4,96,1280]{2,1,0:T(8,128)(2,1)}, bf16[4,96,1280]{2,1,0:T(8,128)(2,1)S(1)}, u32[]{:S(2)}) copy-start(bf16[4,96,1280]{2,1,0:T(8,128)(2,1)S(1)} %add_convert_fusion.refs_0_) | copy-start | bytes 2949124
  152.7 22.2 %collective-permute-start.11 = (bf16[4,96,1280]{2,1,0:T(8,128)(2,1)S(1)}, bf16[4,96,1280]{2,1,0:T(8,128)(2,1)S(1)}, u32[]{:S(2)}, u32[]{:S(2)}) collective-permute-start(bf16[4,96,1280]{2,1,0:T(8,128)(2,1)S(1)} %add_convert_fusion.refs_0_), channel_id=1, source_target_pairs={{0,1},{1,0},{2,3},{3,2},{4,5},{5,4},{6,7},{7,6},{8,9},{9,8},{10,11... | collective-permute-start | bytes 2949128 | tf_op jit(solution)/shard_map/ppermute | solution.py:605
  165.8 9.1 %copy-start.2 = (bf16[4,96,768]{2,1,0:T(8,128)(2,1)}, bf16[4,96,768]{2,1,0:T(8,128)(2,1)S(1)}, u32[]{:S(2)}) copy-start(bf16[4,96,768]{2,1,0:T(8,128)(2,1)S(1)} %add_convert_fusion.1.mine_ref) | copy-start | bytes 1769476
  165.8 17.9 %collective-permute-start.10 = (bf16[4,96,768]{2,1,0:T(8,128)(2,1)S(1)}, bf16[4,96,768]{2,1,0:T(8,128)(2,1)S(1)}, u32[]{:S(2)}, u32[]{:S(2)}) collective-permute-start(bf16[4,96,768]{2,1,0:T(8,128)(2,1)S(1)} %add_convert_fusion.1.mine_ref), channel_id=1, source_target_pairs={{0,1},{1,0},{2,3},{3,2},{4,5},{5,4},{6,7},{7,6},{8,9},{9,8},{10,11... | collective-permute-start | bytes 1769480 | tf_op jit(solution)/shard_map/ppermute | solution.py:605
  174.9 0.9 copy-start.8
  183.7 0.8 copy-start.14
